TPU v7x, 256 devices: a whole 4x4x8 slice. The times are simulated.
256 devices in a mesh: dp: 32 (over z, y), mp: 8 (over x, core).
Axes of the slice: x: 4, y: 4, z: 8, core: 2. Of those that a mesh axis runs over, the one named last changes fastest.
Arguments:
- tokens: bfloat16 [8192, 4096], P('dp', 'mp'), may hold values from -24 to 24
- cotangent: bfloat16 [8192, 4096], P('dp', 'mp'), may hold values from -6 to 6
- gain_dec: float32 [4096], replicated, may hold values from 0.1 to 1.9
- w_query: bfloat16 [4096, 4096], P(None, 'mp'), may hold values from -1 to 1
- w_out: bfloat16 [4096, 4096], P('mp'), may hold values from -0.5 to 0.5
- encodings: bfloat16 [256, 128, 896], P('dp', 'mp'), may hold values from -24 to 24
- gain_enc: float32 [896], replicated, may hold values from 0.1 to 1.9
- w_key: bfloat16 [896, 4096], P(None, 'mp'), may hold values from -1 to 1
- w_value: bfloat16 [896, 4096], P(None, 'mp'), may hold values from -0.1875 to 0.1875
- gain_post: float32 [4096], replicated, may hold values from 0.1 to 1.9
- neighbour_ids: int32 [128, 2], P('dp'), may hold values from 0 to 255, as said below
Outputs:
- mixed: bfloat16 [8192, 4096], P('dp', 'mp')
- ffn_input: bfloat16 [8192, 4096], P('dp', 'mp')
- d_encodings: bfloat16 [256, 128, 896], P('dp', 'mp')
Inputs may be any that keep to these rules, and one draw needn't show every extreme that they name: `neighbour_ids`: encoder row g is held by index g // 8 of dp. Every encoder row is retrieved by exactly one block. The blocks of one index of dp retrieve at most 1 row held by any one index of dp, and exactly 1 from some.
All inputs are finite; a program needn't handle non-finite values.
Results may differ from a plain program's by a relative error of at most 0.02.
The roundings to bfloat16 on the way count: a program that leaves them out, or rounds other values in their place, can miss the bound.
Values may be sent and summed in bfloat16 or wider, within the bound.
No kernel may reach another device: no remote copies, remote signals or barrier semaphores. Data moves between devices by JAX's collectives and lax.ppermute only.
A program may use at most 64 MiB of HBM per device.

v0:
```python
import jax
import jax.numpy as jnp
from jax import lax
from jax.experimental import pallas as pl
from jax.experimental.pallas import tpu as pltpu
from jax.sharding import PartitionSpec as P

HD = 128
BLOCK = 64
NLEN = 128
NEIGH = 2

EPS = 1e-06
F32 = jnp.float32
BF16 = jnp.bfloat16
IDS_WIDTH = 128
VMEM_LIMIT = 48 * 1024 * 1024


def rms_scale(values):
    return lax.rsqrt(jnp.mean(values * values, axis=-1, keepdims=True) + EPS)


def params():
    return pltpu.CompilerParams(vmem_limit_bytes=VMEM_LIMIT)


def cost(micros):
    return pl.CostEstimate(flops=int(micros * 1.1e9), bytes_accessed=0, transcendentals=0)


def vmem():
    return pl.BlockSpec(memory_space=pltpu.VMEM)


def hbm():
    return pl.BlockSpec(memory_space=pl.ANY)


def smem():
    return pl.BlockSpec(memory_space=pltpu.SMEM)


def chip_shift(count, k):
    return [(i, (i + 2 * k) % count) for i in range(count)]


def core_swap(count):
    return [(i, i ^ 1) for i in range(count)]


def over_chips(x, count):
    return [x] + [lax.ppermute(x, "mp", chip_shift(count, k)) for k in range(1, count // 2)]


def swap(x, count):
    return lax.ppermute(x, "mp", core_swap(count))


def pair_sum(send, keep, count):
    return (keep.astype(F32) + swap(send, count).astype(F32)).astype(BF16)


def pair_shares(pair, count):
    return [pair[0]] + [
        lax.ppermute(pair[k], "mp", chip_shift(count, -k)) for k in range(1, count // 2)
    ]


def shift_matrix(n, lead, transpose):
    r = lax.broadcasted_iota(jnp.int32, (n, n), 0)
    c = lax.broadcasted_iota(jnp.int32, (n, n), 1)
    hit = (r == c + lead) if transpose else (c == r + lead)
    return jnp.where(hit, 1.0, 0.0).astype(BF16)


def dot(a, b):
    return lax.dot_general(a, b, (((1,), (0,)), ((), ())), preferred_element_type=F32)


def dot_nt(a, b):
    return lax.dot_general(a, b, (((1,), (1,)), ((), ())), preferred_element_type=F32)


def dot_tn(a, b):
    return lax.dot_general(a, b, (((0,), (0,)), ((), ())), preferred_element_type=F32)


def views(count, refs):
    half = count // 2
    return list(refs[:half]) + [refs[half].at[k] for k in range(half)], refs[half + 1 :]


def query_kernel(count, src, *refs):
    pieces, rest = views(count, refs)
    gain, w_hbm, out, w_buf, sems = rest
    share = pieces[0].shape[1]
    copies = []
    for k in range(count):
        start = pl.multiple_of(src[k] * share, share)
        cp = pltpu.make_async_copy(w_hbm.at[pl.ds(start, share), :], w_buf.at[k], sems.at[k])
        cp.start()
        copies.append(cp)
    squares = jnp.zeros((pieces[0].shape[0], 1), F32)
    for k in range(count):
        wide = pieces[k][...].astype(F32)
        squares = squares + jnp.sum(wide * wide, axis=1, keepdims=True)
    scale = lax.rsqrt(squares / (share * count) + EPS)
    acc = jnp.zeros(out.shape, F32)
    for k in range(count):
        g = gain[pl.ds(src[k], 1), :]
        normed = (pieces[k][...].astype(F32) * scale * g).astype(BF16)
        copies[k].wait()
        acc = acc + dot(normed, w_buf[k])
    out[...] = dot(shift_matrix(out.shape[0], BLOCK - 1, False), acc.astype(BF16)).astype(BF16)


def run_query(src, pieces, gain, w_query):
    count = 2 * (len(pieces) - 1)
    rows, share = pieces[0].shape
    cols = w_query.shape[1]
    return pl.pallas_call(
        lambda *r: query_kernel(count, *r),
        out_shape=jax.ShapeDtypeStruct((rows, cols), BF16),
        in_specs=[smem()] + [vmem()] * (len(pieces) + 1) + [hbm()],
        out_specs=vmem(),
        scratch_shapes=[pltpu.VMEM((count, share, cols), BF16), pltpu.SemaphoreType.DMA((count,))],
        compiler_params=params(),
        cost_estimate=cost(4.5),
        name="queries",
    )(src, *pieces, gain.reshape(count, share), w_query)


def back_kernel(count, src, *refs):
    pieces, rest = views(count, refs)
    w_hbm, out, w_buf, sems = rest
    share = pieces[0].shape[1]
    copies = []
    for k in range(count):
        start = pl.multiple_of(src[k] * share, share)
        cp = pltpu.make_async_copy(w_hbm.at[:, pl.ds(start, share)], w_buf.at[k], sems.at[k])
        cp.start()
        copies.append(cp)
    acc = jnp.zeros(out.shape, F32)
    for k in range(count):
        copies[k].wait()
        acc = acc + dot_nt(pieces[k][...], w_buf[k])
    out[...] = dot(shift_matrix(out.shape[0], BLOCK - 1, False), acc.astype(BF16)).astype(BF16)


def run_back(src, pieces, w_out):
    count = 2 * (len(pieces) - 1)
    rows, share = pieces[0].shape
    cols = w_out.shape[0]
    return pl.pallas_call(
        lambda *r: back_kernel(count, *r),
        out_shape=jax.ShapeDtypeStruct((rows, cols), BF16),
        in_specs=[smem()] + [vmem()] * len(pieces) + [hbm()],
        out_specs=vmem(),
        scratch_shapes=[pltpu.VMEM((count, cols, share), BF16), pltpu.SemaphoreType.DMA((count,))],
        compiler_params=params(),
        cost_estimate=cost(4.5),
        name="d_attended",
    )(src, *pieces, w_out)


def branch_kernel(count, src, att_a, att_b, w_hbm, send, keep, w_buf, sems):
    share = send.shape[2]
    half = count // 2
    copies = []
    order = list(range(half, count)) + list(range(half))
    for k in order:
        start = pl.multiple_of(src[k] * share, share)
        cp = pltpu.make_async_copy(w_hbm.at[:, pl.ds(start, share)], w_buf.at[k], sems.at[k])
        cp.start()
        copies.append(cp)
    shifted = jnp.concatenate([att_a[...], att_b[...]], axis=0)
    a = dot(shift_matrix(shifted.shape[0], BLOCK - 1, True), shifted).astype(BF16)
    for k, cp in zip(order, copies):
        cp.wait()
        out = keep.at[k] if k < half else send.at[k - half]
        out[...] = dot(a, w_buf[k]).astype(BF16)


def run_branch(src, att_a, att_b, w_out, count):
    rows, cols = 2 * att_a.shape[0], att_a.shape[1]
    share = w_out.shape[1] // count
    shape = jax.ShapeDtypeStruct((count // 2, rows, share), BF16)
    return pl.pallas_call(
        lambda *r: branch_kernel(count, *r),
        out_shape=(shape, shape),
        in_specs=[smem(), vmem(), vmem(), hbm()],
        out_specs=(vmem(), vmem()),
        scratch_shapes=[pltpu.VMEM((count, cols, share), BF16), pltpu.SemaphoreType.DMA((count,))],
        compiler_params=params(),
        cost_estimate=cost(4),
        name="branches",
    )(src, att_a, att_b, w_out)


def attention_kernel(count, first, blocks, *refs):
    half = count // 2
    pieces = list(refs[:half]) + [refs[half].at[0]] + [refs[half + 1].at[k] for k in range(half - 1)]
    q_ref, d_ref, wk, wv, send, keep, att, mem, keys, values, k_grad, v_grad = refs[half + 2 :]
    heads = q_ref.shape[1] // HD
    part = send.shape[1] // blocks
    span = part * count
    scale = HD ** (-0.5)
    for b in range(blocks):
        for k in range(count):
            mem[b * span + k * part : b * span + (k + 1) * part, :] = pieces[k][
                (first + b) * part : (first + b + 1) * part, :
            ]
    keys[...] = dot(mem[...], wk[...]).astype(BF16)
    values[...] = dot(mem[...], wv[...]).astype(BF16)
    for b in range(blocks):
        rows = slice(b * BLOCK, (b + 1) * BLOCK)
        ctx = slice(b * span, (b + 1) * span)
        for h in range(heads):
            cols = slice(h * HD, (h + 1) * HD)
            q = q_ref[first * BLOCK + b * BLOCK : first * BLOCK + (b + 1) * BLOCK, cols]
            d = d_ref[first * BLOCK + b * BLOCK : first * BLOCK + (b + 1) * BLOCK, cols]
            kk = keys[ctx, cols]
            vv = values[ctx, cols]
            scores = dot_nt(q, kk) * scale
            lifted = jnp.exp(scores - jnp.max(scores, axis=-1, keepdims=True))
            prob = lifted / jnp.sum(lifted, axis=-1, keepdims=True)
            weights = prob.astype(BF16)
            att[rows, cols] = dot(weights, vv).astype(BF16)
            d_prob = dot_nt(d, vv)
            d_scores = (
                prob * (d_prob - jnp.sum(prob * d_prob, axis=-1, keepdims=True)) * scale
            ).astype(BF16)
            v_grad[ctx, cols] = dot_tn(weights, d).astype(BF16)
            k_grad[ctx, cols] = dot_tn(d_scores, q).astype(BF16)
    for b in range(blocks):
        ctx = slice(b * span, (b + 1) * span)
        terms = (dot_nt(k_grad[ctx, :], wk[...]) + dot_nt(v_grad[ctx, :], wv[...])).astype(BF16)
        for k in range(count):
            out = keep.at[k] if k < half else send.at[k - half]
            out[b * part : (b + 1) * part, :] = terms[k * part : (k + 1) * part, :]


def run_attention(pieces, q, d, w_key, w_value, first, blocks, all_blocks):
    count = 2 * (len(pieces) - 2)
    rows, width = pieces[0].shape
    rows = rows // all_blocks * blocks
    cols = q.shape[1]
    total = rows * count
    shape = jax.ShapeDtypeStruct((count // 2, rows, width), BF16)
    return pl.pallas_call(
        lambda *r: attention_kernel(count, first, blocks, *r),
        out_shape=(shape, shape, jax.ShapeDtypeStruct((blocks * BLOCK, cols), BF16)),
        in_specs=[vmem()] * (len(pieces) + 4),
        out_specs=(vmem(), vmem(), vmem()),
        scratch_shapes=[pltpu.VMEM((total, width), BF16)]
        + [pltpu.VMEM((total, cols), BF16)] * 4,
        compiler_params=params(),
        cost_estimate=cost(7),
        name="attention",
    )(*pieces, q, d, w_key, w_value)


def outgoing_kernel(req, enc, gain, out, normed):
    wide = enc[...].astype(F32)
    normed[...] = (wide * rms_scale(wide) * gain[...]).astype(BF16)
    for s in range(out.shape[0]):
        out[s] = normed[jnp.maximum(req[s, 0], 0)]


def run_outgoing(requested, encodings, gain):
    slots = requested.shape[0]
    return pl.pallas_call(
        outgoing_kernel,
        out_shape=jax.ShapeDtypeStruct((slots,) + encodings.shape[1:], BF16),
        in_specs=[smem(), vmem(), vmem()],
        out_specs=vmem(),
        scratch_shapes=[pltpu.VMEM(encodings.shape, BF16)],
        compiler_params=params(),
        cost_estimate=cost(1.7),
        name="outgoing_rows",
    )(requested, encodings, gain.reshape(1, 1, -1))


def pick_kernel(owner, rows, out, sems):
    copies = []
    for a in range(out.shape[0]):
        cp = pltpu.make_async_copy(rows.at[owner[a]], out.at[a], sems.at[a])
        cp.start()
        copies.append(cp)
    for cp in copies:
        cp.wait()


def run_pick(owner, rows):
    n = owner.shape[0]
    return pl.pallas_call(
        pick_kernel,
        out_shape=jax.ShapeDtypeStruct((n,) + rows.shape[1:], rows.dtype),
        in_specs=[smem(), hbm()],
        out_specs=vmem(),
        scratch_shapes=[pltpu.SemaphoreType.DMA((n,))],
        compiler_params=params(),
        cost_estimate=cost(1),
        name="picked_rows",
    )(owner, rows)


def place_kernel(reading, *refs):
    parts, out, total = refs[:-2], refs[-2], refs[-1]
    half = len(parts) // 2
    rows = parts[0].shape[0]
    for i in range(2):
        group = [p[...].astype(F32) for p in parts[i * half : (i + 1) * half]]
        total[i * rows : (i + 1) * rows] = sum(group).astype(BF16)
    for s in range(out.shape[0]):
        out[s] = total[reading[s]]


def run_place(reading, parts):
    slots = reading.shape[0]
    rows, *rest = parts[0].shape
    return pl.pallas_call(
        place_kernel,
        out_shape=jax.ShapeDtypeStruct((slots, *rest), BF16),
        in_specs=[smem()] + [vmem()] * len(parts),
        out_specs=vmem(),
        scratch_shapes=[pltpu.VMEM((2 * rows, *rest), BF16)],
        compiler_params=params(),
        cost_estimate=cost(1.7),
        name="placed_grads",
    )(reading, *parts)


def finish_kernel(slot, back, enc, gain, out, buf, sems):
    copies = []
    for j in range(out.shape[0]):
        cp = pltpu.make_async_copy(back.at[slot[j]], buf.at[j], sems.at[j])
        cp.start()
        copies.append(cp)
    wide = enc[...].astype(F32)
    scale = rms_scale(wide)
    hat = wide * scale
    for cp in copies:
        cp.wait()
    up = gain[...] * buf[...].astype(F32)
    out[...] = (scale * (up - hat * jnp.mean(up * hat, axis=-1, keepdims=True))).astype(BF16)


def run_finish(slot, back, encodings, gain):
    rows = encodings.shape[0]
    return pl.pallas_call(
        finish_kernel,
        out_shape=jax.ShapeDtypeStruct(encodings.shape, BF16),
        in_specs=[smem(), hbm(), vmem(), vmem()],
        out_specs=vmem(),
        scratch_shapes=[pltpu.VMEM(encodings.shape, BF16), pltpu.SemaphoreType.DMA((rows,))],
        compiler_params=params(),
        cost_estimate=cost(1.9),
        name="d_encodings",
    )(slot, back, encodings, gain.reshape(1, 1, -1))


def shards(
    tokens,
    cotangent,
    gain_dec,
    w_query,
    w_out,
    encodings,
    gain_enc,
    w_key,
    w_value,
    gain_post,
    neighbour_ids,
):
    dp_count = lax.axis_size("dp")
    count = lax.axis_size("mp")
    half = count // 2
    share_cols = tokens.shape[1]
    own_rows, own_tokens, width = encodings.shape
    blocks = neighbour_ids.shape[0]
    readings = blocks * neighbour_ids.shape[1]
    here = lax.axis_index("mp")
    steps = jnp.arange(half, dtype=jnp.int32)
    same = (here - 2 * steps) % count
    src = jnp.concatenate([same, same ^ 1]).astype(jnp.int32)

    chosen = neighbour_ids.reshape(readings)
    owner = chosen // own_rows
    local_row = chosen % own_rows
    slots = jnp.arange(dp_count, dtype=jnp.int32)
    matches = owner[:, None] == slots[None, :]
    wanted = jnp.sum(jnp.where(matches, local_row[:, None] + 1, 0), axis=0) - 1
    reading = jnp.sum(
        jnp.where(matches, jnp.arange(readings, dtype=jnp.int32)[:, None], 0), axis=0
    )
    requested = lax.all_to_all(
        jnp.broadcast_to(wanted[:, None], (dp_count, IDS_WIDTH)),
        "dp",
        split_axis=0,
        concat_axis=0,
        tiled=True,
    )
    serves = requested[:, :1] == jnp.arange(own_rows, dtype=jnp.int32)[None, :]
    slot = jnp.sum(jnp.where(serves, slots[:, None], 0), axis=0)

    tok_own = over_chips(tokens, count)
    enc_in, tok_own = lax.optimization_barrier((encodings, tok_own))
    outgoing = run_outgoing(requested, enc_in, gain_enc)
    outgoing, cot_in = lax.optimization_barrier((outgoing, cotangent))
    cot_own = over_chips(cot_in, count)
    incoming = lax.all_to_all(outgoing, "dp", split_axis=0, concat_axis=0, tiled=True)
    q = run_query(src, tok_own + [swap(jnp.stack(tok_own), count)], gain_dec, w_query)
    d = run_back(src, cot_own + [swap(jnp.stack(cot_own), count)], w_out)
    incoming, q, d = lax.optimization_barrier((incoming, q, d))
    picked = run_pick(owner, incoming).reshape(readings * own_tokens, width)
    row_own = over_chips(picked, count)
    rows = row_own + [swap(picked, count)[None], swap(jnp.stack(row_own[1:]), count)]
    first = blocks // 2
    send_a, keep_a, att_a = run_attention(rows, q, d, w_key, w_value, 0, first, blocks)
    pair_a = pair_sum(send_a, keep_a, count)
    rows, pair_a = lax.optimization_barrier((rows, pair_a))
    parts_a = pair_shares(pair_a, count)
    send_b, keep_b, att_b = run_attention(
        rows, q, d, w_key, w_value, first, blocks - first, blocks
    )
    send_b, parts_a = lax.optimization_barrier((send_b, parts_a))
    pair_b = pair_sum(send_b, keep_b, count)
    att_b, pair_b = lax.optimization_barrier((att_b, pair_b))
    parts_b = pair_shares(pair_b, count)
    b_send, b_keep = run_branch(src, att_a, att_b, w_out, count)
    b_send, parts_b = lax.optimization_barrier((b_send, parts_b))
    b_pair = pair_sum(b_send, b_keep, count)
    b_parts = pair_shares(b_pair, count)
    back_out = run_place(
        reading,
        [p.reshape(readings // 2, own_tokens, width) for p in parts_a + parts_b],
    )
    back_in = lax.all_to_all(back_out, "dp", split_axis=0, concat_axis=0, tiled=True)

    summed = sum(p.astype(F32) for p in b_parts)
    mixed = (tokens.astype(F32) + summed).astype(BF16)
    mixed_wide = mixed.astype(F32)
    squares = jnp.sum(mixed_wide * mixed_wide, axis=1)
    total = jnp.sum(lax.all_gather(squares, "mp", axis=0), axis=0)
    post = lax.rsqrt(total / (share_cols * count) + EPS)[:, None]
    gain_here = lax.dynamic_slice_in_dim(gain_post, here * share_cols, share_cols, 0)
    ffn = (mixed_wide * post * gain_here).astype(BF16)

    d_encodings = run_finish(slot, back_in, encodings, gain_enc)
    return (mixed, ffn, d_encodings)


def solution(mesh):
    in_specs = (
        P("dp", "mp"),
        P("dp", "mp"),
        P(),
        P(None, "mp"),
        P("mp", None),
        P("dp", "mp", None),
        P(),
        P(None, "mp"),
        P(None, "mp"),
        P(),
        P("dp", None),
    )
    out_specs = (P("dp", "mp"), P("dp", "mp"), P("dp", "mp", None))
    return jax.shard_map(shards, mesh=mesh, in_specs=in_specs, out_specs=out_specs, check_vma=False)
```

profile of v0, /device:TPU:8, one launch (start us, length us, event | category | flops | bytes accessed | tf_op | source)
XLA Modules:
  0.0 152.3 jit_solution(2494960820449361398)
XLA Ops:
  0.6 1.6 %collective-permute-start = (bf16[256,512]{1,0:T(8,128)(2,1)}, bf16[256,512]{1,0:T(8,128)(2,1)S(1)}, u32[]{:S(2)}, u32[]{:S(2)}) collective-permute-start(bf16[256,512]{1,0:T(8,128)(2,1)} %r_1_), channel_id=1, source_target_pairs={{0,2},{1,3},{2,4},{3,5},{4,6},{5,7},{6,0},{7,1},{8,10},{9,11},{10,... | collective-permute-start | bytes 786440 | tf_op jit(solution)/shard_map/ppermute | solution.py:53
  2.2 2.7 %collective-permute-start.1 = (bf16[256,512]{1,0:T(8,128)(2,1)}, bf16[256,512]{1,0:T(8,128)(2,1)S(1)}, u32[]{:S(2)}, u32[]{:S(2)}) collective-permute-start(bf16[256,512]{1,0:T(8,128)(2,1)} %r_1_), channel_id=1, source_target_pairs={{0,4},{1,5},{2,6},{3,7},{4,0},{5,1},{6,2},{7,3},{8,12},{9,13},{10,... | collective-permute-start | bytes 786440 | tf_op jit(solution)/shard_map/ppermute | solution.py:53
  4.9 1.4 collective-permute-start.2
  6.4 0.8 copy.17
  7.2 0.1 select_reduce_fusion
  7.3 0.7 broadcast_in_dim.49
  8.0 11.7 %all-to-all-start = ((s32[32,1,128]{2,1,0:T(1,128)}), s32[32,1,128]{2,1,0:T(1,128)S(1)}, u32[]{:S(2)}, u32[]{:S(2)}) async-start(s32[32,1,128]{2,1,0:T(1,128)} %broadcast_in_dim.49), calls=%async_computation | async-start | bytes 32768 | tf_op jit(solution)/shard_map/all_to_all | solution.py:398
  19.8 0.7 reshape.112.gain
  20.5 2.1 %pad_maximum_fusion = bf16[4,256,512]{2,1,0:T(8,128)(2,1)} fusion(bf16[1,256,512]{2,1,0:T(8,128)(2,1)S(1)} %bitcast.55, bf16[1,256,512]{2,1,0:T(8,128)(2,1)S(1)} %bitcast.54, bf16[1,256,512]{2,1,0:T(8,128)(2,1)S(1)} %bitcast.53, bf16[1,256,512]{2,1,0:T(8,128)(2,1)} %bitcast.51), kind=kLoop, calls=%fused_computation.1 | loop fusion | flops 1572864 | bytes 2097152 | tf_op jit(solution)/shard_map/stack | solution.py:414
  22.5 5.7 %all-to-all-done = s32[32,1,128]{2,1,0:T(1,128)S(1)} async-done(((s32[32,1,128]{2,1,0:T(1,128)}), s32[32,1,128]{2,1,0:T(1,128)S(1)}, u32[]{:S(2)}, u32[]{:S(2)}) %all-to-all-start) | async-done | bytes 16416 | tf_op jit(solution)/shard_map/all_to_all | solution.py:398
  28.2 2.0 %outgoing_rows.1 = bf16[32,16,896]{2,1,0:T(8,128)(2,1)} custom-call(s32[32,128]{1,0:T(8,128)S(1)} %bitcast.64, bf16[8,16,896]{2,1,0:T(8,128)(2,1)S(1)} %copy-done.4, f32[1,1,896]{2,1,0:T(1,128)S(1)} %reshape.112.gain), custom_call_target="tpu_custom_call" | custom-call | flops 1870000000 | tf_op jit(solution)/shard_map/outgoing_rows/pallas_call | solution.py:273
  30.2 0.6 collective-permute-start.4
  30.8 0.9 collective-permute-start.5
  31.7 1.9 %collective-permute-start.6 = (bf16[256,512]{1,0:T(8,128)(2,1)S(1)}, bf16[256,512]{1,0:T(8,128)(2,1)S(1)}, u32[]{:S(2)}, u32[]{:S(2)}) collective-permute-start(bf16[256,512]{1,0:T(8,128)(2,1)S(1)} %copy-done.1), channel_id=1, source_target_pairs={{0,6},{1,7},{2,0},{3,1},{4,2},{5,3},{6,4},{7,5},{8,14},{9,15},{10,... | collective-permute-start | bytes 786440 | tf_op jit(solution)/shard_map/ppermute | solution.py:53
  33.6 5.0 %all-to-all-start.1 = ((bf16[32,16,896]{2,1,0:T(8,128)(2,1)}), bf16[32,16,896]{2,1,0:T(8,128)(2,1)S(1)}, u32[]{:S(2)}, u32[]{:S(2)}) async-start(bf16[32,16,896]{2,1,0:T(8,128)(2,1)} %outgoing_rows.1), calls=%async_computation.1 | async-start | bytes 1835008 | tf_op jit(solution)/shard_map/all_to_all | solution.py:413
  38.6 4.2 %collective-permute-done.4.r_2_ = bf16[256,512]{1,0:T(8,128)(2,1)S(1)} collective-permute-done((bf16[256,512]{1,0:T(8,128)(2,1)S(1)}, bf16[256,512]{1,0:T(8,128)(2,1)S(1)}, u32[]{:S(2)}, u32[]{:S(2)}) %collective-permute-start.4) | collective-permute-done | bytes 262176 | tf_op jit(solution)/shard_map/ppermute | solution.py:53
  42.8 0.6 collective-permute-done.6.r_4_
  43.4 1.1 pad_maximum_fusion.1
  44.7 4.7 %queries.1.r_6_ = bf16[256,512]{1,0:T(8,128)(2,1)S(1)} custom-call(s32[8]{0:T(128)S(1)} %pad_add_fusion.r_0_, bf16[256,512]{1,0:T(8,128)(2,1)S(1)} %copy-done, bf16[256,512]{1,0:T(8,128)(2,1)S(1)} %collective-permute-done.r_2_, bf16[256,512]{1,0:T(8,128)(2,1)S(1)} %collective-permute-done.1.r_3_, bf16[256,512]{1,0:T(8,128)(2,1)S(1)} %collective-permute-done.2.r_4_, ...), custom_call_target="tpu_custom_call" | custom-call | flops 4950000128 | tf_op jit(solution)/shard_map/queries/pallas_call | solution.py:122
  49.3 0.7 copy-done.5
  50.0 4.5 %d_attended.1.r_7_ = bf16[256,512]{1,0:T(8,128)(2,1)S(1)} custom-call(s32[8]{0:T(128)S(1)} %pad_add_fusion.r_0_, bf16[256,512]{1,0:T(8,128)(2,1)S(1)} %copy-done.1, bf16[256,512]{1,0:T(8,128)(2,1)S(1)} %collective-permute-done.4.r_2_, bf16[256,512]{1,0:T(8,128)(2,1)S(1)} %collective-permute-done.5.r_3_, bf16[256,512]{1,0:T(8,128)(2,1)S(1)} %collective-permute-done.6.r_4_, ...), custom_call_target="tpu_custom_call" | custom-call | flops 4950000128 | tf_op jit(solution)/shard_map/d_attended/pallas_call | solution.py:155
  54.5 0.7 copy-done.7
  55.2 7.8 %all-to-all-done.1.rows = bf16[32,16,896]{2,1,0:T(8,128)(2,1)S(1)} async-done(((bf16[32,16,896]{2,1,0:T(8,128)(2,1)}), bf16[32,16,896]{2,1,0:T(8,128)(2,1)S(1)}, u32[]{:S(2)}, u32[]{:S(2)}) %all-to-all-start.1) | async-done | bytes 917536 | tf_op jit(solution)/shard_map/all_to_all | solution.py:413
  63.0 1.0 picked_rows.1
  64.0 0.8 collective-permute-start.8
  64.8 1.9 %collective-permute-start.9 = (bf16[128,896]{1,0:T(8,128)(2,1)S(1)}, bf16[128,896]{1,0:T(8,128)(2,1)S(1)}, u32[]{:S(2)}, u32[]{:S(2)}) collective-permute-start(bf16[128,896]{1,0:T(8,128)(2,1)S(1)} %bitcast.67), channel_id=1, source_target_pairs={{0,4},{1,5},{2,6},{3,7},{4,0},{5,1},{6,2},{7,3},{8,12},{9,13},{10,... | collective-permute-start | bytes 688136 | tf_op jit(solution)/shard_map/ppermute | solution.py:53
  66.7 2.5 %collective-permute-start.10 = (bf16[128,896]{1,0:T(8,128)(2,1)S(1)}, bf16[128,896]{1,0:T(8,128)(2,1)S(1)}, u32[]{:S(2)}, u32[]{:S(2)}) collective-permute-start(bf16[128,896]{1,0:T(8,128)(2,1)S(1)} %bitcast.68), channel_id=1, source_target_pairs={{0,6},{1,7},{2,0},{3,1},{4,2},{5,3},{6,4},{7,5},{8,14},{9,15},{10,... | collective-permute-start | bytes 688136 | tf_op jit(solution)/shard_map/ppermute | solution.py:53
  69.3 6.0 %collective-permute-done.8.r_1_ = bf16[128,896]{1,0:T(8,128)(2,1)S(1)} collective-permute-done((bf16[128,896]{1,0:T(8,128)(2,1)S(1)}, bf16[128,896]{1,0:T(8,128)(2,1)S(1)}, u32[]{:S(2)}, u32[]{:S(2)}) %collective-permute-start.8) | collective-permute-done | bytes 229408 | tf_op jit(solution)/shard_map/ppermute | solution.py:53
  75.3 0.6 collective-permute-done.10.r_3_
  75.9 0.1 pad_maximum_fusion.2
  76.0 0.1 collective-permute-start.12
  76.1 0.5 collective-permute-start.11
  76.6 2.0 %collective-permute-done.11 = bf16[128,896]{1,0:T(8,128)(2,1)S(1)} collective-permute-done((bf16[128,896]{1,0:T(8,128)(2,1)S(1)}, bf16[128,896]{1,0:T(8,128)(2,1)S(1)}, u32[]{:S(2)}, u32[]{:S(2)}) %collective-permute-start.11) | collective-permute-done | bytes 229408 | tf_op jit(solution)/shard_map/ppermute | solution.py:57
  78.6 5.7 %attention.2 = (bf16[4,64,896]{2,1,0:T(8,128)(2,1)S(1)}, bf16[4,64,896]{2,1,0:T(8,128)(2,1)S(1)}, bf16[128,512]{1,0:T(8,128)(2,1)S(1)}) custom-call(bf16[128,896]{1,0:T(8,128)(2,1)S(1)} %bitcast.70, bf16[128,896]{1,0:T(8,128)(2,1)S(1)} %collective-permute-done.8.r_1_, bf16[128,896]{1,0:T(8,128)(2,1)S(1)} %collective-permute-done.9.r_2_, ...), custom_call_target="tpu_custom_call" | custom-call | flops 7699999744 | tf_op jit(solution)/shard_map/attention/pallas_call | solution.py:251
  84.3 0.2 collective-permute-start.13
  84.5 1.7 %collective-permute-done.13 = bf16[4,64,896]{2,1,0:T(8,128)(2,1)S(1)} collective-permute-done((bf16[4,64,896]{2,1,0:T(8,128)(2,1)S(1)}, bf16[4,64,896]{2,1,0:T(8,128)(2,1)S(1)}, u32[]{:S(2)}, u32[]{:S(2)}) %collective-permute-start.13) | collective-permute-done | bytes 458784 | tf_op jit(solution)/shard_map/ppermute | solution.py:57
  86.2 0.1 add_convert_fusion.2
  86.3 2.7 %collective-permute-start.14 = (bf16[64,896]{1,0:T(8,128)(2,1)S(1)}, bf16[64,896]{1,0:T(8,128)(2,1)S(1)}, u32[]{:S(2)}, u32[]{:S(2)}) collective-permute-start(bf16[64,896]{1,0:T(8,128)(2,1)S(1)} %get-tuple-element.90), channel_id=1, source_target_pairs={{0,6},{1,7},{2,0},{3,1},{4,2},{5,3},{6,4},{7,5},{8,14},{9,15},{10,... | collective-permute-start | bytes 344072 | tf_op jit(solution)/shard_map/ppermute | solution.py:66
  89.1 1.1 collective-permute-start.15
  90.2 5.6 %attention.3 = (bf16[4,64,896]{2,1,0:T(8,128)(2,1)S(1)}, bf16[4,64,896]{2,1,0:T(8,128)(2,1)S(1)}, bf16[128,512]{1,0:T(8,128)(2,1)S(1)}) custom-call(bf16[128,896]{1,0:T(8,128)(2,1)S(1)} %bitcast.71, bf16[128,896]{1,0:T(8,128)(2,1)S(1)} %collective-permute-done.8.r_1_, bf16[128,896]{1,0:T(8,128)(2,1)S(1)} %collective-permute-done.9.r_2_, ...), custom_call_target="tpu_custom_call" | custom-call | flops 7699999744 | tf_op jit(solution)/shard_map/attention/pallas_call | solution.py:251
  95.8 0.7 collective-permute-done.15
  96.6 1.3 collective-permute-done.16
  97.9 1.8 %collective-permute-done.17 = bf16[4,64,896]{2,1,0:T(8,128)(2,1)S(1)} collective-permute-done((bf16[4,64,896]{2,1,0:T(8,128)(2,1)S(1)}, bf16[4,64,896]{2,1,0:T(8,128)(2,1)S(1)}, u32[]{:S(2)}, u32[]{:S(2)}) %collective-permute-start.17) | collective-permute-done | bytes 458784 | tf_op jit(solution)/shard_map/ppermute | solution.py:57
  99.7 0.1 add_convert_fusion.1
  99.9 1.3 collective-permute-start.18
  101.2 1.2 collective-permute-start.19
  102.5 4.8 %branches.1 = (bf16[4,256,512]{2,1,0:T(8,128)(2,1)}, bf16[4,256,512]{2,1,0:T(8,128)(2,1)S(1)}) custom-call(s32[8]{0:T(128)S(1)} %pad_add_fusion.r_0_, bf16[128,512]{1,0:T(8,128)(2,1)S(1)} %get-tuple-element.50.r_1_, bf16[128,512]{1,0:T(8,128)(2,1)S(1)} %get-tuple-element.64.r_2_, bf16[512,4096]{1,0:T(8,128)(2,1)} %r_3_.1), custom_call_target="tpu_custom_call" | custom-call | flops 4400000000 | tf_op jit(solution)/shard_map/branches/pallas_call | solution.py:189
  107.3 1.5 collective-permute-done.19
  108.8 1.3 collective-permute-done.20
  110.1 1.7 %placed_grads.1 = bf16[32,16,896]{2,1,0:T(8,128)(2,1)} custom-call(s32[32]{0:T(128)S(1)} %get-tuple-element.77.reading, bf16[4,16,896]{2,1,0:T(8,128)(2,1)S(1)} %bitcast.62, bf16[4,16,896]{2,1,0:T(8,128)(2,1)S(1)} %bitcast.74, bf16[4,16,896]{2,1,0:T(8,128)(2,1)S(1)} %bitcast.75, bf16[4,16,896]{2,1,0:T(8,128)(2,1)S(1)} %bitcast.76, ...), custom_call_target="tpu_custom_call" | custom-call | flops 1870000000 | tf_op jit(solution)/shard_map/placed_grads/pallas_call | solution.py:323
  111.8 6.5 %all-to-all-start.2 = ((bf16[32,16,896]{2,1,0:T(8,128)(2,1)}), bf16[32,16,896]{2,1,0:T(8,128)(2,1)S(1)}, u32[]{:S(2)}, u32[]{:S(2)}) async-start(bf16[32,16,896]{2,1,0:T(8,128)(2,1)} %placed_grads.1), calls=%async_computation.2 | async-start | bytes 1835008 | tf_op jit(solution)/shard_map/all_to_all | solution.py:440
  118.3 2.5 %add_convert_fusion = bf16[4,256,512]{2,1,0:T(8,128)(2,1)} fusion(bf16[4,256,512]{2,1,0:T(8,128)(2,1)} %collective-permute-done.21, bf16[4,256,512]{2,1,0:T(8,128)(2,1)S(1)} %get-tuple-element.65), kind=kLoop, calls=%fused_computation | loop fusion | flops 2097152 | bytes 3145728 | tf_op jit(solution)/shard_map/convert_element_type | solution.py:61
  120.8 1.2 slice_bitcast_fusion.2
  122.1 2.0 %collective-permute-start.23 = (bf16[256,512]{1,0:T(8,128)(2,1)S(1)}, bf16[256,512]{1,0:T(8,128)(2,1)S(1)}, u32[]{:S(2)}, u32[]{:S(2)}) collective-permute-start(bf16[256,512]{1,0:T(8,128)(2,1)S(1)} %get-tuple-element.83), channel_id=1, source_target_pairs={{0,4},{1,5},{2,6},{3,7},{4,0},{5,1},{6,2},{7,3},{8,12},{9,13},{10,... | collective-permute-start | bytes 786440 | tf_op jit(solution)/shard_map/ppermute | solution.py:66
  124.1 1.9 %collective-permute-start.22 = (bf16[256,512]{1,0:T(8,128)(2,1)S(1)}, bf16[256,512]{1,0:T(8,128)(2,1)S(1)}, u32[]{:S(2)}, u32[]{:S(2)}) collective-permute-start(bf16[256,512]{1,0:T(8,128)(2,1)S(1)} %get-tuple-element.81), channel_id=1, source_target_pairs={{0,6},{1,7},{2,0},{3,1},{4,2},{5,3},{6,4},{7,5},{8,14},{9,15},{10,... | collective-permute-start | bytes 786440 | tf_op jit(solution)/shard_map/ppermute | solution.py:66
  126.0 0.8 dynamic_slice.3
  126.8 0.1 slice_reduce_fusion
  126.9 0.1 select_reduce_fusion.1.slot
  127.0 10.1 %collective-permute-done.24 = bf16[256,512]{1,0:T(8,128)(2,1)S(1)} collective-permute-done((bf16[256,512]{1,0:T(8,128)(2,1)S(1)}, bf16[256,512]{1,0:T(8,128)(2,1)S(1)}, u32[]{:S(2)}, u32[]{:S(2)}) %collective-permute-start.24) | collective-permute-done | bytes 262176 | tf_op jit(solution)/shard_map/ppermute | solution.py:66
  137.0 0.6 collective-permute-done.22
  137.7 1.2 fusion
  138.9 10.4 %all-gather.1 = f32[8,1,256]{2,1,0:T(1,128)S(1)} all-gather(f32[1,1,256]{2,1,0:T(1,128)S(1)} %bitcast.80), channel_id=2, replica_groups=mesh['dp'=32,'mp'=8] {'mp'}, dimensions={0}, use_global_device_ids=true | all-gather | bytes 9216 | tf_op jit(solution)/shard_map/all_gather | solution.py:446
  149.4 0.8 fusion.2
  150.2 1.9 %d_encodings.1 = bf16[8,16,896]{2,1,0:T(8,128)(2,1)} custom-call(s32[8]{0:T(128)S(1)} %select_reduce_fusion.1.slot, bf16[32,16,896]{2,1,0:T(8,128)(2,1)S(1)} %all-to-all-done.2.back, bf16[8,16,896]{2,1,0:T(8,128)(2,1)S(1)} %copy-done.4, f32[1,1,896]{2,1,0:T(1,128)S(1)} %reshape.112.gain), custom_call_target="tpu_custom_call" | custom-call | flops 2090000000 | tf_op jit(solution)/shard_map/d_encodings/pallas_call | solution.py:352
  (50 shorter events, 0.6 us)
Async XLA Ops:
  0.6 27.6 %copy-start.4 = (bf16[8,16,896]{2,1,0:T(8,128)(2,1)S(1)}, bf16[8,16,896]{2,1,0:T(8,128)(2,1)}, u32[]{:S(2)}) copy-start(bf16[8,16,896]{2,1,0:T(8,128)(2,1)} %enc.2) | copy-start | bytes 688132
  0.6 19.8 %collective-permute-start = (bf16[256,512]{1,0:T(8,128)(2,1)}, bf16[256,512]{1,0:T(8,128)(2,1)S(1)}, u32[]{:S(2)}, u32[]{:S(2)}) collective-permute-start(bf16[256,512]{1,0:T(8,128)(2,1)} %r_1_), channel_id=1, source_target_pairs={{0,2},{1,3},{2,4},{3,5},{4,6},{5,7},{6,0},{7,1},{8,10},{9,11},{10,... | collective-permute-start | bytes 786440 | tf_op jit(solution)/shard_map/ppermute | solution.py:53
  2.2 18.2 %collective-permute-start.1 = (bf16[256,512]{1,0:T(8,128)(2,1)}, bf16[256,512]{1,0:T(8,128)(2,1)S(1)}, u32[]{:S(2)}, u32[]{:S(2)}) collective-permute-start(bf16[256,512]{1,0:T(8,128)(2,1)} %r_1_), channel_id=1, source_target_pairs={{0,4},{1,5},{2,6},{3,7},{4,0},{5,1},{6,2},{7,3},{8,12},{9,13},{10,... | collective-permute-start | bytes 786440 | tf_op jit(solution)/shard_map/ppermute | solution.py:53
  4.9 15.5 %collective-permute-start.2 = (bf16[256,512]{1,0:T(8,128)(2,1)}, bf16[256,512]{1,0:T(8,128)(2,1)S(1)}, u32[]{:S(2)}, u32[]{:S(2)}) collective-permute-start(bf16[256,512]{1,0:T(8,128)(2,1)} %r_1_), channel_id=1, source_target_pairs={{0,6},{1,7},{2,0},{3,1},{4,2},{5,3},{6,4},{7,5},{8,14},{9,15},{10,... | collective-permute-start | bytes 786440 | tf_op jit(solution)/shard_map/ppermute | solution.py:53
  8.0 20.2 %all-to-all-start = ((s32[32,1,128]{2,1,0:T(1,128)}), s32[32,1,128]{2,1,0:T(1,128)S(1)}, u32[]{:S(2)}, u32[]{:S(2)}) async-start(s32[32,1,128]{2,1,0:T(1,128)} %broadcast_in_dim.49), calls=%async_computation | async-start | bytes 32768 | tf_op jit(solution)/shard_map/all_to_all | solution.py:398
  22.5 22.1 %collective-permute-start.3 = (bf16[4,256,512]{2,1,0:T(8,128)(2,1)}, bf16[4,256,512]{2,1,0:T(8,128)(2,1)}, u32[]{:S(2)}, u32[]{:S(2)}) collective-permute-start(bf16[4,256,512]{2,1,0:T(8,128)(2,1)} %pad_maximum_fusion), channel_id=1, source_target_pairs={{0,1},{1,0},{2,3},{3,2},{4,5},{5,4},{6,7},{7,6},{8,9},{9,8},{10,11... | collective-permute-start | bytes 3145736 | tf_op jit(solution)/shard_map/ppermute | solution.py:57
  28.2 2.0 %copy-start.1 = (bf16[256,512]{1,0:T(8,128)(2,1)S(1)}, bf16[256,512]{1,0:T(8,128)(2,1)}, u32[]{:S(2)}) copy-start(bf16[256,512]{1,0:T(8,128)(2,1)} %r_1_.1) | copy-start | bytes 786436
  30.2 14.4 %copy-start.10 = (f32[4096]{0:T(1024)S(1)}, f32[4096]{0:T(1024)}, u32[]{:S(2)}) copy-start(f32[4096]{0:T(1024)} %param.13) | copy-start | bytes 49156
  30.2 14.5 %copy-start = (bf16[256,512]{1,0:T(8,128)(2,1)S(1)}, bf16[256,512]{1,0:T(8,128)(2,1)}, u32[]{:S(2)}) copy-start(bf16[256,512]{1,0:T(8,128)(2,1)} %r_1_) | copy-start | bytes 786436
  30.2 12.6 %collective-permute-start.4 = (bf16[256,512]{1,0:T(8,128)(2,1)S(1)}, bf16[256,512]{1,0:T(8,128)(2,1)S(1)}, u32[]{:S(2)}, u32[]{:S(2)}) collective-permute-start(bf16[256,512]{1,0:T(8,128)(2,1)S(1)} %copy-done.1), channel_id=1, source_target_pairs={{0,2},{1,3},{2,4},{3,5},{4,6},{5,7},{6,0},{7,1},{8,10},{9,11},{10,... | collective-permute-start | bytes 786440 | tf_op jit(solution)/shard_map/ppermute | solution.py:53
  30.8 12.0 %collective-permute-start.5 = (bf16[256,512]{1,0:T(8,128)(2,1)S(1)}, bf16[256,512]{1,0:T(8,128)(2,1)S(1)}, u32[]{:S(2)}, u32[]{:S(2)}) collective-permute-start(bf16[256,512]{1,0:T(8,128)(2,1)S(1)} %copy-done.1), channel_id=1, source_target_pairs={{0,4},{1,5},{2,6},{3,7},{4,0},{5,1},{6,2},{7,3},{8,12},{9,13},{10,... | collective-permute-start | bytes 786440 | tf_op jit(solution)/shard_map/ppermute | solution.py:53
  31.7 11.8 %collective-permute-start.6 = (bf16[256,512]{1,0:T(8,128)(2,1)S(1)}, bf16[256,512]{1,0:T(8,128)(2,1)S(1)}, u32[]{:S(2)}, u32[]{:S(2)}) collective-permute-start(bf16[256,512]{1,0:T(8,128)(2,1)S(1)} %copy-done.1), channel_id=1, source_target_pairs={{0,6},{1,7},{2,0},{3,1},{4,2},{5,3},{6,4},{7,5},{8,14},{9,15},{10,... | collective-permute-start | bytes 786440 | tf_op jit(solution)/shard_map/ppermute | solution.py:53
  33.6 29.5 %all-to-all-start.1 = ((bf16[32,16,896]{2,1,0:T(8,128)(2,1)}), bf16[32,16,896]{2,1,0:T(8,128)(2,1)S(1)}, u32[]{:S(2)}, u32[]{:S(2)}) async-start(bf16[32,16,896]{2,1,0:T(8,128)(2,1)} %outgoing_rows.1), calls=%async_computation.1 | async-start | bytes 1835008 | tf_op jit(solution)/shard_map/all_to_all | solution.py:413
  44.5 5.5 %collective-permute-start.7 = (bf16[4,256,512]{2,1,0:T(8,128)(2,1)}, bf16[4,256,512]{2,1,0:T(8,128)(2,1)}, u32[]{:S(2)}, u32[]{:S(2)}) collective-permute-start(bf16[4,256,512]{2,1,0:T(8,128)(2,1)} %pad_maximum_fusion.1), channel_id=1, source_target_pairs={{0,1},{1,0},{2,3},{3,2},{4,5},{5,4},{6,7},{7,6},{8,9},{9,8},{10,11... | collective-permute-start | bytes 3145736 | tf_op jit(solution)/shard_map/ppermute | solution.py:57
  49.3 0.7 copy-start.5
  54.5 0.7 copy-start.7
  55.2 23.3 %copy-start.2 = (bf16[896,512]{1,0:T(8,128)(2,1)S(1)}, bf16[896,512]{1,0:T(8,128)(2,1)}, u32[]{:S(2)}) copy-start(bf16[896,512]{1,0:T(8,128)(2,1)} %r_8_.3) | copy-start | bytes 2752516
  55.2 23.3 %copy-start.3 = (bf16[896,512]{1,0:T(8,128)(2,1)S(1)}, bf16[896,512]{1,0:T(8,128)(2,1)}, u32[]{:S(2)}) copy-start(bf16[896,512]{1,0:T(8,128)(2,1)} %r_9_.3) | copy-start | bytes 2752516
  63.0 15.5 %copy-start.6 = (bf16[256,512]{1,0:T(8,128)(2,1)S(1)}, bf16[256,512]{1,0:T(8,128)(2,1)}, u32[]{:S(2)}) copy-start(bf16[256,512]{1,0:T(8,128)(2,1)} %copy-done.5) | copy-start | bytes 786436
  63.0 15.5 %copy-start.8 = (bf16[256,512]{1,0:T(8,128)(2,1)S(1)}, bf16[256,512]{1,0:T(8,128)(2,1)}, u32[]{:S(2)}) copy-start(bf16[256,512]{1,0:T(8,128)(2,1)} %copy-done.7) | copy-start | bytes 786436
  64.0 11.3 %collective-permute-start.8 = (bf16[128,896]{1,0:T(8,128)(2,1)S(1)}, bf16[128,896]{1,0:T(8,128)(2,1)S(1)}, u32[]{:S(2)}, u32[]{:S(2)}) collective-permute-start(bf16[128,896]{1,0:T(8,128)(2,1)S(1)} %bitcast.66), channel_id=1, source_target_pairs={{0,2},{1,3},{2,4},{3,5},{4,6},{5,7},{6,0},{7,1},{8,10},{9,11},{10,... | collective-permute-start | bytes 688136 | tf_op jit(solution)/shard_map/ppermute | solution.py:53
  64.8 10.5 %collective-permute-start.9 = (bf16[128,896]{1,0:T(8,128)(2,1)S(1)}, bf16[128,896]{1,0:T(8,128)(2,1)S(1)}, u32[]{:S(2)}, u32[]{:S(2)}) collective-permute-start(bf16[128,896]{1,0:T(8,128)(2,1)S(1)} %bitcast.67), channel_id=1, source_target_pairs={{0,4},{1,5},{2,6},{3,7},{4,0},{5,1},{6,2},{7,3},{8,12},{9,13},{10,... | collective-permute-start | bytes 688136 | tf_op jit(solution)/shard_map/ppermute | solution.py:53
  66.7 9.2 %collective-permute-start.10 = (bf16[128,896]{1,0:T(8,128)(2,1)S(1)}, bf16[128,896]{1,0:T(8,128)(2,1)S(1)}, u32[]{:S(2)}, u32[]{:S(2)}) collective-permute-start(bf16[128,896]{1,0:T(8,128)(2,1)S(1)} %bitcast.68), channel_id=1, source_target_pairs={{0,6},{1,7},{2,0},{3,1},{4,2},{5,3},{6,4},{7,5},{8,14},{9,15},{10,... | collective-permute-start | bytes 688136 | tf_op jit(solution)/shard_map/ppermute | solution.py:53
  76.0 2.6 %collective-permute-start.12 = (bf16[3,128,896]{2,1,0:T(8,128)(2,1)S(1)}, bf16[3,128,896]{2,1,0:T(8,128)(2,1)S(1)}, u32[]{:S(2)}, u32[]{:S(2)}) collective-permute-start(bf16[3,128,896]{2,1,0:T(8,128)(2,1)S(1)} %pad_maximum_fusion.2), channel_id=1, source_target_pairs={{0,1},{1,0},{2,3},{3,2},{4,5},{5,4},{6,7},{7,6},{8,9},{9,8},{10,11... | collective-permute-start | bytes 2064392 | tf_op jit(solution)/shard_map/ppermute | solution.py:57
  76.1 2.5 %collective-permute-start.11 = (bf16[128,896]{1,0:T(8,128)(2,1)S(1)}, bf16[128,896]{1,0:T(8,128)(2,1)S(1)}, u32[]{:S(2)}, u32[]{:S(2)}) collective-permute-start(bf16[128,896]{1,0:T(8,128)(2,1)S(1)} %bitcast.69), channel_id=1, source_target_pairs={{0,1},{1,0},{2,3},{3,2},{4,5},{5,4},{6,7},{7,6},{8,9},{9,8},{10,11... | collective-permute-start | bytes 688136 | tf_op jit(solution)/shard_map/ppermute | solution.py:57
  84.3 1.9 %collective-permute-start.13 = (bf16[4,64,896]{2,1,0:T(8,128)(2,1)S(1)}, bf16[4,64,896]{2,1,0:T(8,128)(2,1)S(1)}, u32[]{:S(2)}, u32[]{:S(2)}) collective-permute-start(bf16[4,64,896]{2,1,0:T(8,128)(2,1)S(1)} %get-tuple-element.52), channel_id=1, source_target_pairs={{0,1},{1,0},{2,3},{3,2},{4,5},{5,4},{6,7},{7,6},{8,9},{9,8},{10,11... | collective-permute-start | bytes 1376264 | tf_op jit(solution)/shard_map/ppermute | solution.py:57
  86.3 9.5 %collective-permute-start.14 = (bf16[64,896]{1,0:T(8,128)(2,1)S(1)}, bf16[64,896]{1,0:T(8,128)(2,1)S(1)}, u32[]{:S(2)}, u32[]{:S(2)}) collective-permute-start(bf16[64,896]{1,0:T(8,128)(2,1)S(1)} %get-tuple-element.90), channel_id=1, source_target_pairs={{0,6},{1,7},{2,0},{3,1},{4,2},{5,3},{6,4},{7,5},{8,14},{9,15},{10,... | collective-permute-start | bytes 344072 | tf_op jit(solution)/shard_map/ppermute | solution.py:66
  89.1 7.5 %collective-permute-start.15 = (bf16[64,896]{1,0:T(8,128)(2,1)S(1)}, bf16[64,896]{1,0:T(8,128)(2,1)S(1)}, u32[]{:S(2)}, u32[]{:S(2)}) collective-permute-start(bf16[64,896]{1,0:T(8,128)(2,1)S(1)} %get-tuple-element.89), channel_id=1, source_target_pairs={{0,4},{1,5},{2,6},{3,7},{4,0},{5,1},{6,2},{7,3},{8,12},{9,13},{10,... | collective-permute-start | bytes 344072 | tf_op jit(solution)/shard_map/ppermute | solution.py:66
  90.1 7.8 %collective-permute-start.16 = (bf16[64,896]{1,0:T(8,128)(2,1)S(1)}, bf16[64,896]{1,0:T(8,128)(2,1)S(1)}, u32[]{:S(2)}, u32[]{:S(2)}) collective-permute-start(bf16[64,896]{1,0:T(8,128)(2,1)S(1)} %get-tuple-element.88), channel_id=1, source_target_pairs={{0,2},{1,3},{2,4},{3,5},{4,6},{5,7},{6,0},{7,1},{8,10},{9,11},{10,... | collective-permute-start | bytes 344072 | tf_op jit(solution)/shard_map/ppermute | solution.py:66
  97.9 1.8 %collective-permute-start.17 = (bf16[4,64,896]{2,1,0:T(8,128)(2,1)S(1)}, bf16[4,64,896]{2,1,0:T(8,128)(2,1)S(1)}, u32[]{:S(2)}, u32[]{:S(2)}) collective-permute-start(bf16[4,64,896]{2,1,0:T(8,128)(2,1)S(1)} %get-tuple-element.63), channel_id=1, source_target_pairs={{0,1},{1,0},{2,3},{3,2},{4,5},{5,4},{6,7},{7,6},{8,9},{9,8},{10,11... | collective-permute-start | bytes 1376264 | tf_op jit(solution)/shard_map/ppermute | solution.py:57
  99.9 7.4 %collective-permute-start.18 = (bf16[64,896]{1,0:T(8,128)(2,1)S(1)}, bf16[64,896]{1,0:T(8,128)(2,1)S(1)}, u32[]{:S(2)}, u32[]{:S(2)}) collective-permute-start(bf16[64,896]{1,0:T(8,128)(2,1)S(1)} %get-tuple-element.86), channel_id=1, source_target_pairs={{0,6},{1,7},{2,0},{3,1},{4,2},{5,3},{6,4},{7,5},{8,14},{9,15},{10,... | collective-permute-start | bytes 344072 | tf_op jit(solution)/shard_map/ppermute | solution.py:66
  101.2 7.5 %collective-permute-start.19 = (bf16[64,896]{1,0:T(8,128)(2,1)S(1)}, bf16[64,896]{1,0:T(8,128)(2,1)S(1)}, u32[]{:S(2)}, u32[]{:S(2)}) collective-permute-start(bf16[64,896]{1,0:T(8,128)(2,1)S(1)} %get-tuple-element.85), channel_id=1, source_target_pairs={{0,4},{1,5},{2,6},{3,7},{4,0},{5,1},{6,2},{7,3},{8,12},{9,13},{10,... | collective-permute-start | bytes 344072 | tf_op jit(solution)/shard_map/ppermute | solution.py:66
  102.5 7.6 %collective-permute-start.20 = (bf16[64,896]{1,0:T(8,128)(2,1)S(1)}, bf16[64,896]{1,0:T(8,128)(2,1)S(1)}, u32[]{:S(2)}, u32[]{:S(2)}) collective-permute-start(bf16[64,896]{1,0:T(8,128)(2,1)S(1)} %get-tuple-element.84), channel_id=1, source_target_pairs={{0,2},{1,3},{2,4},{3,5},{4,6},{5,7},{6,0},{7,1},{8,10},{9,11},{10,... | collective-permute-start | bytes 344072 | tf_op jit(solution)/shard_map/ppermute | solution.py:66
  110.1 8.2 %collective-permute-start.21 = (bf16[4,256,512]{2,1,0:T(8,128)(2,1)}, bf16[4,256,512]{2,1,0:T(8,128)(2,1)}, u32[]{:S(2)}, u32[]{:S(2)}) collective-permute-start(bf16[4,256,512]{2,1,0:T(8,128)(2,1)} %get-tuple-element.68), channel_id=1, source_target_pairs={{0,1},{1,0},{2,3},{3,2},{4,5},{5,4},{6,7},{7,6},{8,9},{9,8},{10,11... | collective-permute-start | bytes 3145736 | tf_op jit(solution)/shard_map/ppermute | solution.py:57
  111.8 38.4 %all-to-all-start.2 = ((bf16[32,16,896]{2,1,0:T(8,128)(2,1)}), bf16[32,16,896]{2,1,0:T(8,128)(2,1)S(1)}, u32[]{:S(2)}, u32[]{:S(2)}) async-start(bf16[32,16,896]{2,1,0:T(8,128)(2,1)} %placed_grads.1), calls=%async_computation.2 | async-start | bytes 1835008 | tf_op jit(solution)/shard_map/all_to_all | solution.py:440
  122.0 15.1 %collective-permute-start.24 = (bf16[256,512]{1,0:T(8,128)(2,1)S(1)}, bf16[256,512]{1,0:T(8,128)(2,1)S(1)}, u32[]{:S(2)}, u32[]{:S(2)}) collective-permute-start(bf16[256,512]{1,0:T(8,128)(2,1)S(1)} %get-tuple-element.82), channel_id=1, source_target_pairs={{0,2},{1,3},{2,4},{3,5},{4,6},{5,7},{6,0},{7,1},{8,10},{9,11},{10,... | collective-permute-start | bytes 786440 | tf_op jit(solution)/shard_map/ppermute | solution.py:66
  122.1 15.0 %collective-permute-start.23 = (bf16[256,512]{1,0:T(8,128)(2,1)S(1)}, bf16[256,512]{1,0:T(8,128)(2,1)S(1)}, u32[]{:S(2)}, u32[]{:S(2)}) collective-permute-start(bf16[256,512]{1,0:T(8,128)(2,1)S(1)} %get-tuple-element.83), channel_id=1, source_target_pairs={{0,4},{1,5},{2,6},{3,7},{4,0},{5,1},{6,2},{7,3},{8,12},{9,13},{10,... | collective-permute-start | bytes 786440 | tf_op jit(solution)/shard_map/ppermute | solution.py:66
  124.1 13.6 %collective-permute-start.22 = (bf16[256,512]{1,0:T(8,128)(2,1)S(1)}, bf16[256,512]{1,0:T(8,128)(2,1)S(1)}, u32[]{:S(2)}, u32[]{:S(2)}) collective-permute-start(bf16[256,512]{1,0:T(8,128)(2,1)S(1)} %get-tuple-element.81), channel_id=1, source_target_pairs={{0,6},{1,7},{2,0},{3,1},{4,2},{5,3},{6,4},{7,5},{8,14},{9,15},{10,... | collective-permute-start | bytes 786440 | tf_op jit(solution)/shard_map/ppermute | solution.py:66
  138.9 13.2 %copy-start.9 = (bf16[256,512]{1,0:T(8,128)(2,1)}, bf16[256,512]{1,0:T(8,128)(2,1)S(1)}, u32[]{:S(2)}) copy-start(bf16[256,512]{1,0:T(8,128)(2,1)S(1)} %get-tuple-element.80) | copy-start | bytes 786436
where the time goes:
time: 154 us; the launch traced here: 152 us
  starting transfers between devices  48.8 us (32%)
  waiting for transfers between devices  46 us (30%)
  Pallas kernels  31.8 us (21%)
  blocking collectives  10.4 us (7%)
  other arithmetic  8.43 us (5%)
  local copies, waits for them, and re-layouts  5.78 us (4%)
    ppermute x9, waiting for transfers between devices, pair_shares(): lax.ppermute(pair[k], 'mp', chip_shift(count, -k))  15.6 us
    ppermute x9, starting transfers between devices, over_chips(): lax.ppermute(x, 'mp', chip_shift(count, k))  14.3 us
    all_to_all x1, starting transfers between devices, shards(): lax.all_to_all(jnp.broadcast_to(wanted[:, None], (dp_count, IDS_WIDTH)),...  11.7 us
    ppermute x9, waiting for transfers between devices, over_chips(): lax.ppermute(x, 'mp', chip_shift(count, k))  11.5 us
    pallas_call x2, Pallas kernels, run_attention(): pl.pallas_call(lambda *r: attention_kernel(count, first, blocks, *r), out...  11.3 us
    ppermute x9, starting transfers between devices, pair_shares(): lax.ppermute(pair[k], 'mp', chip_shift(count, -k))  10.4 us
    all_gather x1, blocking collectives, shards(): total = jnp.sum(lax.all_gather(squares, 'mp', axis=0), axis=0)  10.4 us
    all_to_all x1, waiting for transfers between devices, shards(): lax.all_to_all(outgoing, 'dp', split_axis=0, concat_axis=0, tiled=True)  7.79 us
  transfers between devices with their start and end apart: 28, of which 15 were waited for; matrix products, arithmetic and copies ran while one was open for 8% of the time, Pallas kernels for 15%

commit v1 on v0

--- a/solution.py
+++ b/solution.py
@@ -14,6 +14,8 @@
 F32 = jnp.float32
 BF16 = jnp.bfloat16
 IDS_WIDTH = 128
+GROUP = 8
+MIX_COST = 100
 VMEM_LIMIT = 48 * 1024 * 1024
 
 
@@ -126,7 +128,7 @@
         out_specs=vmem(),
         scratch_shapes=[pltpu.VMEM((count, share, cols), BF16), pltpu.SemaphoreType.DMA((count,))],
         compiler_params=params(),
-        cost_estimate=cost(4.5),
+        cost_estimate=cost(2.25),
         name="queries",
     )(src, *pieces, gain.reshape(count, share), w_query)
 
@@ -159,12 +161,12 @@
         out_specs=vmem(),
         scratch_shapes=[pltpu.VMEM((count, cols, share), BF16), pltpu.SemaphoreType.DMA((count,))],
         compiler_params=params(),
-        cost_estimate=cost(4.5),
+        cost_estimate=cost(2.25),
         name="d_attended",
     )(src, *pieces, w_out)
 
 
-def branch_kernel(count, src, att_a, att_b, w_hbm, send, keep, w_buf, sems):
+def branch_kernel(count, src, att, w_hbm, send, keep, w_buf, sems):
     share = send.shape[2]
     half = count // 2
     copies = []
@@ -174,31 +176,30 @@
         cp = pltpu.make_async_copy(w_hbm.at[:, pl.ds(start, share)], w_buf.at[k], sems.at[k])
         cp.start()
         copies.append(cp)
-    shifted = jnp.concatenate([att_a[...], att_b[...]], axis=0)
-    a = dot(shift_matrix(shifted.shape[0], BLOCK - 1, True), shifted).astype(BF16)
+    a = dot(shift_matrix(att.shape[0], BLOCK - 1, True), att[...]).astype(BF16)
     for k, cp in zip(order, copies):
         cp.wait()
         out = keep.at[k] if k < half else send.at[k - half]
         out[...] = dot(a, w_buf[k]).astype(BF16)
 
 
-def run_branch(src, att_a, att_b, w_out, count):
-    rows, cols = 2 * att_a.shape[0], att_a.shape[1]
+def run_branch(src, att, w_out, count):
+    rows, cols = att.shape
     share = w_out.shape[1] // count
     shape = jax.ShapeDtypeStruct((count // 2, rows, share), BF16)
     return pl.pallas_call(
         lambda *r: branch_kernel(count, *r),
         out_shape=(shape, shape),
-        in_specs=[smem(), vmem(), vmem(), hbm()],
+        in_specs=[smem(), vmem(), hbm()],
         out_specs=(vmem(), vmem()),
         scratch_shapes=[pltpu.VMEM((count, cols, share), BF16), pltpu.SemaphoreType.DMA((count,))],
         compiler_params=params(),
         cost_estimate=cost(4),
         name="branches",
-    )(src, att_a, att_b, w_out)
-
-
-def attention_kernel(count, first, blocks, *refs):
+    )(src, att, w_out)
+
+
+def attention_kernel(count, blocks, *refs):
     half = count // 2
     pieces = list(refs[:half]) + [refs[half].at[0]] + [refs[half + 1].at[k] for k in range(half - 1)]
     q_ref, d_ref, wk, wv, send, keep, att, mem, keys, values, k_grad, v_grad = refs[half + 2 :]
@@ -206,57 +207,67 @@
     part = send.shape[1] // blocks
     span = part * count
     scale = HD ** (-0.5)
+
+    def rows(b):
+        return slice(b * BLOCK, (b + 1) * BLOCK)
+
+    def ctx(b):
+        return slice(b * span, (b + 1) * span)
+
+    def cols(h):
+        return slice(h * HD, (h + 1) * HD)
+
+    def softmax(scores):
+        scores = scores * scale
+        lifted = jnp.exp(scores - jnp.max(scores, axis=-1, keepdims=True))
+        return lifted / jnp.sum(lifted, axis=-1, keepdims=True)
+
+    def score_grad(p, dp):
+        return (p * (dp - jnp.sum(p * dp, axis=-1, keepdims=True)) * scale).astype(BF16)
+
     for b in range(blocks):
         for k in range(count):
             mem[b * span + k * part : b * span + (k + 1) * part, :] = pieces[k][
-                (first + b) * part : (first + b + 1) * part, :
+                b * part : (b + 1) * part, :
             ]
     keys[...] = dot(mem[...], wk[...]).astype(BF16)
     values[...] = dot(mem[...], wv[...]).astype(BF16)
+    every = [(b, h) for b in range(blocks) for h in range(heads)]
+    for start in range(0, len(every), GROUP):
+        group = every[start : start + GROUP]
+        scores = [dot_nt(q_ref[rows(b), cols(h)], keys[ctx(b), cols(h)]) for b, h in group]
+        d_probs = [dot_nt(d_ref[rows(b), cols(h)], values[ctx(b), cols(h)]) for b, h in group]
+        probs = [softmax(s) for s in scores]
+        weights = [p.astype(BF16) for p in probs]
+        d_scores = [score_grad(p, dp) for p, dp in zip(probs, d_probs)]
+        for w, ds, (b, h) in zip(weights, d_scores, group):
+            att[rows(b), cols(h)] = dot(w, values[ctx(b), cols(h)]).astype(BF16)
+            v_grad[ctx(b), cols(h)] = dot_tn(w, d_ref[rows(b), cols(h)]).astype(BF16)
+            k_grad[ctx(b), cols(h)] = dot_tn(ds, q_ref[rows(b), cols(h)]).astype(BF16)
     for b in range(blocks):
-        rows = slice(b * BLOCK, (b + 1) * BLOCK)
-        ctx = slice(b * span, (b + 1) * span)
-        for h in range(heads):
-            cols = slice(h * HD, (h + 1) * HD)
-            q = q_ref[first * BLOCK + b * BLOCK : first * BLOCK + (b + 1) * BLOCK, cols]
-            d = d_ref[first * BLOCK + b * BLOCK : first * BLOCK + (b + 1) * BLOCK, cols]
-            kk = keys[ctx, cols]
-            vv = values[ctx, cols]
-            scores = dot_nt(q, kk) * scale
-            lifted = jnp.exp(scores - jnp.max(scores, axis=-1, keepdims=True))
-            prob = lifted / jnp.sum(lifted, axis=-1, keepdims=True)
-            weights = prob.astype(BF16)
-            att[rows, cols] = dot(weights, vv).astype(BF16)
-            d_prob = dot_nt(d, vv)
-            d_scores = (
-                prob * (d_prob - jnp.sum(prob * d_prob, axis=-1, keepdims=True)) * scale
-            ).astype(BF16)
-            v_grad[ctx, cols] = dot_tn(weights, d).astype(BF16)
-            k_grad[ctx, cols] = dot_tn(d_scores, q).astype(BF16)
-    for b in range(blocks):
-        ctx = slice(b * span, (b + 1) * span)
-        terms = (dot_nt(k_grad[ctx, :], wk[...]) + dot_nt(v_grad[ctx, :], wv[...])).astype(BF16)
+        terms = (dot_nt(k_grad[ctx(b), :], wk[...]) + dot_nt(v_grad[ctx(b), :], wv[...])).astype(
+            BF16
+        )
         for k in range(count):
             out = keep.at[k] if k < half else send.at[k - half]
             out[b * part : (b + 1) * part, :] = terms[k * part : (k + 1) * part, :]
 
 
-def run_attention(pieces, q, d, w_key, w_value, first, blocks, all_blocks):
+def run_attention(pieces, q, d, w_key, w_value, blocks):
     count = 2 * (len(pieces) - 2)
     rows, width = pieces[0].shape
-    rows = rows // all_blocks * blocks
     cols = q.shape[1]
     total = rows * count
     shape = jax.ShapeDtypeStruct((count // 2, rows, width), BF16)
     return pl.pallas_call(
-        lambda *r: attention_kernel(count, first, blocks, *r),
+        lambda *r: attention_kernel(count, blocks, *r),
         out_shape=(shape, shape, jax.ShapeDtypeStruct((blocks * BLOCK, cols), BF16)),
         in_specs=[vmem()] * (len(pieces) + 4),
         out_specs=(vmem(), vmem(), vmem()),
         scratch_shapes=[pltpu.VMEM((total, width), BF16)]
         + [pltpu.VMEM((total, cols), BF16)] * 4,
         compiler_params=params(),
-        cost_estimate=cost(7),
+        cost_estimate=cost(9),
         name="attention",
     )(*pieces, q, d, w_key, w_value)
 
@@ -301,35 +312,55 @@
         out_specs=vmem(),
         scratch_shapes=[pltpu.SemaphoreType.DMA((n,))],
         compiler_params=params(),
-        cost_estimate=cost(1),
+        cost_estimate=cost(2.25),
         name="picked_rows",
     )(owner, rows)
 
 
 def place_kernel(reading, *refs):
     parts, out, total = refs[:-2], refs[-2], refs[-1]
-    half = len(parts) // 2
-    rows = parts[0].shape[0]
-    for i in range(2):
-        group = [p[...].astype(F32) for p in parts[i * half : (i + 1) * half]]
-        total[i * rows : (i + 1) * rows] = sum(group).astype(BF16)
+    total[...] = sum(p[...].astype(F32) for p in parts).astype(BF16)
     for s in range(out.shape[0]):
         out[s] = total[reading[s]]
 
 
 def run_place(reading, parts):
     slots = reading.shape[0]
-    rows, *rest = parts[0].shape
+    shape = parts[0].shape
     return pl.pallas_call(
         place_kernel,
-        out_shape=jax.ShapeDtypeStruct((slots, *rest), BF16),
+        out_shape=jax.ShapeDtypeStruct((slots,) + shape[1:], BF16),
         in_specs=[smem()] + [vmem()] * len(parts),
         out_specs=vmem(),
-        scratch_shapes=[pltpu.VMEM((2 * rows, *rest), BF16)],
+        scratch_shapes=[pltpu.VMEM(shape, BF16)],
         compiler_params=params(),
         cost_estimate=cost(1.7),
         name="placed_grads",
     )(reading, *parts)
+
+
+def mix_kernel(tok, *refs):
+    parts, mixed, squares = refs[:-2], refs[-2], refs[-1]
+    summed = sum(p[...].astype(F32) for p in parts)
+    out = (tok[...].astype(F32) + summed).astype(BF16)
+    mixed[...] = out
+    wide = out.astype(F32)
+    squares[...] = jnp.sum(wide * wide, axis=1, keepdims=True)
+
+
+def run_mix(tokens, parts):
+    return pl.pallas_call(
+        mix_kernel,
+        out_shape=(
+            jax.ShapeDtypeStruct(tokens.shape, BF16),
+            jax.ShapeDtypeStruct((tokens.shape[0], 1), F32),
+        ),
+        in_specs=[vmem()] * (len(parts) + 1),
+        out_specs=(vmem(), vmem()),
+        compiler_params=params(),
+        cost_estimate=cost(MIX_COST),
+        name="mixed",
+    )(tokens, *parts)
 
 
 def finish_kernel(slot, back, enc, gain, out, buf, sems):
@@ -406,43 +437,29 @@
     slot = jnp.sum(jnp.where(serves, slots[:, None], 0), axis=0)
 
     tok_own = over_chips(tokens, count)
-    enc_in, tok_own = lax.optimization_barrier((encodings, tok_own))
-    outgoing = run_outgoing(requested, enc_in, gain_enc)
+    outgoing = run_outgoing(requested, encodings, gain_enc)
     outgoing, cot_in = lax.optimization_barrier((outgoing, cotangent))
+    incoming = lax.all_to_all(outgoing, "dp", split_axis=0, concat_axis=0, tiled=True)
     cot_own = over_chips(cot_in, count)
-    incoming = lax.all_to_all(outgoing, "dp", split_axis=0, concat_axis=0, tiled=True)
     q = run_query(src, tok_own + [swap(jnp.stack(tok_own), count)], gain_dec, w_query)
     d = run_back(src, cot_own + [swap(jnp.stack(cot_own), count)], w_out)
     incoming, q, d = lax.optimization_barrier((incoming, q, d))
     picked = run_pick(owner, incoming).reshape(readings * own_tokens, width)
     row_own = over_chips(picked, count)
     rows = row_own + [swap(picked, count)[None], swap(jnp.stack(row_own[1:]), count)]
-    first = blocks // 2
-    send_a, keep_a, att_a = run_attention(rows, q, d, w_key, w_value, 0, first, blocks)
-    pair_a = pair_sum(send_a, keep_a, count)
-    rows, pair_a = lax.optimization_barrier((rows, pair_a))
-    parts_a = pair_shares(pair_a, count)
-    send_b, keep_b, att_b = run_attention(
-        rows, q, d, w_key, w_value, first, blocks - first, blocks
-    )
-    send_b, parts_a = lax.optimization_barrier((send_b, parts_a))
-    pair_b = pair_sum(send_b, keep_b, count)
-    att_b, pair_b = lax.optimization_barrier((att_b, pair_b))
-    parts_b = pair_shares(pair_b, count)
-    b_send, b_keep = run_branch(src, att_a, att_b, w_out, count)
-    b_send, parts_b = lax.optimization_barrier((b_send, parts_b))
+    send, keep, att = run_attention(rows, q, d, w_key, w_value, blocks)
+    pair = pair_sum(send, keep, count)
+    parts = pair_shares(pair, count)
+    b_send, b_keep = run_branch(src, att, w_out, count)
     b_pair = pair_sum(b_send, b_keep, count)
+    parts, b_pair = lax.optimization_barrier((parts, b_pair))
     b_parts = pair_shares(b_pair, count)
-    back_out = run_place(
-        reading,
-        [p.reshape(readings // 2, own_tokens, width) for p in parts_a + parts_b],
-    )
+    back_out = run_place(reading, [p.reshape(readings, own_tokens, width) for p in parts])
     back_in = lax.all_to_all(back_out, "dp", split_axis=0, concat_axis=0, tiled=True)
 
-    summed = sum(p.astype(F32) for p in b_parts)
-    mixed = (tokens.astype(F32) + summed).astype(BF16)
+    mixed, squares = run_mix(tokens, b_parts)
     mixed_wide = mixed.astype(F32)
-    squares = jnp.sum(mixed_wide * mixed_wide, axis=1)
+    squares = squares[:, 0]
     total = jnp.sum(lax.all_gather(squares, "mp", axis=0), axis=0)
     post = lax.rsqrt(total / (share_cols * count) + EPS)[:, None]
     gain_here = lax.dynamic_slice_in_dim(gain_post, here * share_cols, share_cols, 0)

time: 154 us -> 152 us (0.987)
  blocking collectives: 10.4 us -> 14 us
  waiting for transfers between devices: 46 us -> 43.3 us
  other arithmetic: 8.43 us -> 6.78 us
    ppermute x9, waiting for transfers between devices: 11.5 us -> 19.9 us  [over_chips(): lax.ppermute(x, 'mp', chip_shift(count, k))]
    all_to_all x1, waiting for transfers between devices: 7.79 us -> 0.01 us  [shards(): lax.all_to_all(outgoing, 'dp', split_axis=0, concat_axis=0, tiled=True)]
    all_to_all x1, waiting for transfers between devices: 0.01 us -> 6.72 us  [shards(): lax.all_to_all(back_out, 'dp', split_axis=0, concat_axis=0, tiled=True)]
    ppermute x9 -> x6, starting transfers between devices: 10.4 us -> 5.74 us  [pair_shares(): lax.ppermute(pair[k], 'mp', chip_shift(count, -k))]
    all_to_all x1, waiting for transfers between devices: 5.68 us -> 2.02 us  [shards(): lax.all_to_all(jnp.broadcast_to(wanted[:, None], (dp_count, IDS_WIDTH)),...]
    all_gather x1, blocking collectives: 10.4 us -> 14 us  [shards(): total = jnp.sum(lax.all_gather(squares, 'mp', axis=0), axis=0)]
    ppermute x7 -> x6, waiting for transfers between devices: 5.47 us -> 1.98 us  [swap(): return lax.ppermute(x, 'mp', core_swap(count))]
    all_to_all x1, starting transfers between devices: 6.48 us -> 9.76 us  [shards(): lax.all_to_all(back_out, 'dp', split_axis=0, concat_axis=0, tiled=True)]
  transfers between devices with their start and end apart: 28 -> 24, of which waited for: 15 -> 10; matrix products, arithmetic and copies ran while one was open for 8% -> 5% of each run, Pallas kernels for 15% -> 12%
where the time goes in v1:
time: 152 us; the launch traced here: 150 us
  starting transfers between devices  49.3 us (32%)
  waiting for transfers between devices  43.3 us (28%)
  Pallas kernels  30.4 us (20%)
  blocking collectives  14 us (9%)
  other arithmetic  6.78 us (4%)
  local copies, waits for them, and re-layouts  5.19 us (3%)
    ppermute x9, waiting for transfers between devices, over_chips(): lax.ppermute(x, 'mp', chip_shift(count, k))  19.9 us
    all_gather x1, blocking collectives, shards(): total = jnp.sum(lax.all_gather(squares, 'mp', axis=0), axis=0)  14 us
    ppermute x9, starting transfers between devices, over_chips(): lax.ppermute(x, 'mp', chip_shift(count, k))  13.2 us
    ppermute x6, waiting for transfers between devices, pair_shares(): lax.ppermute(pair[k], 'mp', chip_shift(count, -k))  12.7 us
    all_to_all x1, starting transfers between devices, shards(): lax.all_to_all(jnp.broadcast_to(wanted[:, None], (dp_count, IDS_WIDTH)),...  11.7 us
    all_to_all x1, starting transfers between devices, shards(): lax.all_to_all(back_out, 'dp', split_axis=0, concat_axis=0, tiled=True)  9.76 us
    pallas_call x1, Pallas kernels, run_attention(): pl.pallas_call(lambda *r: attention_kernel(count, blocks, *r), out_shape=...  9.01 us
    all_to_all x1, starting transfers between devices, shards(): lax.all_to_all(outgoing, 'dp', split_axis=0, concat_axis=0, tiled=True)  7.75 us
  transfers between devices with their start and end apart: 24, of which 10 were waited for; matrix products, arithmetic and copies ran while one was open for 5% of the time, Pallas kernels for 12%

profile of v1, /device:TPU:8, one launch (start us, length us, event | category | flops | bytes accessed | tf_op | source)
XLA Modules:
  0.0 150.1 jit_solution(18201271859376125188)
XLA Ops:
  0.6 0.8 copy.17
  1.4 0.1 reshape.97
  1.5 0.1 select_reduce_fusion
  1.6 0.7 broadcast_in_dim.49
  2.3 11.7 %all-to-all-start = ((s32[32,1,128]{2,1,0:T(1,128)}), s32[32,1,128]{2,1,0:T(1,128)S(1)}, u32[]{:S(2)}, u32[]{:S(2)}) async-start(s32[32,1,128]{2,1,0:T(1,128)} %broadcast_in_dim.49), calls=%async_computation | async-start | bytes 32768 | tf_op jit(solution)/shard_map/all_to_all | solution.py:429
  14.0 1.6 %collective-permute-start = (bf16[256,512]{1,0:T(8,128)(2,1)}, bf16[256,512]{1,0:T(8,128)(2,1)S(1)}, u32[]{:S(2)}, u32[]{:S(2)}) collective-permute-start(bf16[256,512]{1,0:T(8,128)(2,1)} %tok.1), channel_id=1, source_target_pairs={{0,2},{1,3},{2,4},{3,5},{4,6},{5,7},{6,0},{7,1},{8,10},{9,11},{10,... | collective-permute-start | bytes 786440 | tf_op jit(solution)/shard_map/ppermute | solution.py:55
  15.6 2.7 %collective-permute-start.1 = (bf16[256,512]{1,0:T(8,128)(2,1)}, bf16[256,512]{1,0:T(8,128)(2,1)S(1)}, u32[]{:S(2)}, u32[]{:S(2)}) collective-permute-start(bf16[256,512]{1,0:T(8,128)(2,1)} %tok.1), channel_id=1, source_target_pairs={{0,4},{1,5},{2,6},{3,7},{4,0},{5,1},{6,2},{7,3},{8,12},{9,13},{10,... | collective-permute-start | bytes 786440 | tf_op jit(solution)/shard_map/ppermute | solution.py:55
  18.3 1.4 collective-permute-start.2
  19.7 0.7 reshape.98.gain
  20.4 2.0 %all-to-all-done = s32[32,1,128]{2,1,0:T(1,128)S(1)} async-done(((s32[32,1,128]{2,1,0:T(1,128)}), s32[32,1,128]{2,1,0:T(1,128)S(1)}, u32[]{:S(2)}, u32[]{:S(2)}) %all-to-all-start) | async-done | bytes 16416 | tf_op jit(solution)/shard_map/all_to_all | solution.py:429
  22.5 0.9 copy-done.3
  23.4 2.0 %outgoing_rows.1 = bf16[32,16,896]{2,1,0:T(8,128)(2,1)} custom-call(s32[32,128]{1,0:T(8,128)S(1)} %bitcast.46, bf16[8,16,896]{2,1,0:T(8,128)(2,1)S(1)} %copy-done.3, f32[1,1,896]{2,1,0:T(1,128)S(1)} %reshape.98.gain), custom_call_target="tpu_custom_call" | custom-call | flops 1870000000 | tf_op jit(solution)/shard_map/outgoing_rows/pallas_call | solution.py:284
  25.4 7.7 %all-to-all-start.1 = ((bf16[32,16,896]{2,1,0:T(8,128)(2,1)}), bf16[32,16,896]{2,1,0:T(8,128)(2,1)S(1)}, u32[]{:S(2)}, u32[]{:S(2)}) async-start(bf16[32,16,896]{2,1,0:T(8,128)(2,1)} %outgoing_rows.1), calls=%async_computation.1 | async-start | bytes 1835008 | tf_op jit(solution)/shard_map/all_to_all | solution.py:442
  33.1 0.7 collective-permute-start.4
  33.8 0.9 collective-permute-start.5
  34.7 1.9 %collective-permute-start.6 = (bf16[256,512]{1,0:T(8,128)(2,1)S(1)}, bf16[256,512]{1,0:T(8,128)(2,1)S(1)}, u32[]{:S(2)}, u32[]{:S(2)}) collective-permute-start(bf16[256,512]{1,0:T(8,128)(2,1)S(1)} %copy-done), channel_id=1, source_target_pairs={{0,6},{1,7},{2,0},{3,1},{4,2},{5,3},{6,4},{7,5},{8,14},{9,15},{10,... | collective-permute-start | bytes 786440 | tf_op jit(solution)/shard_map/ppermute | solution.py:55
  36.6 0.0 copy-start.8
  36.6 1.2 pad_maximum_fusion
  37.8 8.4 %collective-permute-done.4.r_2_ = bf16[256,512]{1,0:T(8,128)(2,1)S(1)} collective-permute-done((bf16[256,512]{1,0:T(8,128)(2,1)S(1)}, bf16[256,512]{1,0:T(8,128)(2,1)S(1)}, u32[]{:S(2)}, u32[]{:S(2)}) %collective-permute-start.4) | collective-permute-done | bytes 262176 | tf_op jit(solution)/shard_map/ppermute | solution.py:55
  46.1 0.6 collective-permute-done.6.r_4_
  46.7 1.1 pad_maximum_fusion.1
  47.9 0.1 pad_add_fusion.r_0_
  48.0 4.7 %queries.1.r_6_ = bf16[256,512]{1,0:T(8,128)(2,1)S(1)} custom-call(s32[8]{0:T(128)S(1)} %pad_add_fusion.r_0_, bf16[256,512]{1,0:T(8,128)(2,1)S(1)} %copy-done.1, bf16[256,512]{1,0:T(8,128)(2,1)S(1)} %collective-permute-done.r_2_, bf16[256,512]{1,0:T(8,128)(2,1)S(1)} %collective-permute-done.1.r_3_, bf16[256,512]{1,0:T(8,128)(2,1)S(1)} %collective-permute-done.2.r_4_, ...), custom_call_target="tpu_custom_call" | custom-call | flops 2475000064 | tf_op jit(solution)/shard_map/queries/pallas_call | solution.py:124
  52.6 4.5 %d_attended.1.r_7_ = bf16[256,512]{1,0:T(8,128)(2,1)S(1)} custom-call(s32[8]{0:T(128)S(1)} %pad_add_fusion.r_0_, bf16[256,512]{1,0:T(8,128)(2,1)S(1)} %copy-done, bf16[256,512]{1,0:T(8,128)(2,1)S(1)} %collective-permute-done.4.r_2_, bf16[256,512]{1,0:T(8,128)(2,1)S(1)} %collective-permute-done.5.r_3_, bf16[256,512]{1,0:T(8,128)(2,1)S(1)} %collective-permute-done.6.r_4_, ...), custom_call_target="tpu_custom_call" | custom-call | flops 2475000064 | tf_op jit(solution)/shard_map/d_attended/pallas_call | solution.py:157
  57.1 0.0 copy-start.5
  57.2 0.0 copy-start.2
  57.2 1.0 picked_rows.1
  58.2 0.5 collective-permute-start.8
  58.6 3.5 %collective-permute-start.9 = (bf16[128,896]{1,0:T(8,128)(2,1)S(1)}, bf16[128,896]{1,0:T(8,128)(2,1)S(1)}, u32[]{:S(2)}, u32[]{:S(2)}) collective-permute-start(bf16[128,896]{1,0:T(8,128)(2,1)S(1)} %bitcast.52), channel_id=1, source_target_pairs={{0,4},{1,5},{2,6},{3,7},{4,0},{5,1},{6,2},{7,3},{8,12},{9,13},{10,... | collective-permute-start | bytes 688136 | tf_op jit(solution)/shard_map/ppermute | solution.py:55
  62.2 0.0 collective-permute-start.10
  62.2 5.3 %collective-permute-done.8.r_1_ = bf16[128,896]{1,0:T(8,128)(2,1)S(1)} collective-permute-done((bf16[128,896]{1,0:T(8,128)(2,1)S(1)}, bf16[128,896]{1,0:T(8,128)(2,1)S(1)}, u32[]{:S(2)}, u32[]{:S(2)}) %collective-permute-start.8) | collective-permute-done | bytes 229408 | tf_op jit(solution)/shard_map/ppermute | solution.py:55
  67.5 5.6 %collective-permute-done.9.r_2_ = bf16[128,896]{1,0:T(8,128)(2,1)S(1)} collective-permute-done((bf16[128,896]{1,0:T(8,128)(2,1)S(1)}, bf16[128,896]{1,0:T(8,128)(2,1)S(1)}, u32[]{:S(2)}, u32[]{:S(2)}) %collective-permute-start.9) | collective-permute-done | bytes 229408 | tf_op jit(solution)/shard_map/ppermute | solution.py:55
  73.1 0.1 pad_maximum_fusion.2
  73.2 0.1 collective-permute-start.12
  73.3 0.5 collective-permute-start.11
  73.8 2.0 %collective-permute-done.11 = bf16[128,896]{1,0:T(8,128)(2,1)S(1)} collective-permute-done((bf16[128,896]{1,0:T(8,128)(2,1)S(1)}, bf16[128,896]{1,0:T(8,128)(2,1)S(1)}, u32[]{:S(2)}, u32[]{:S(2)}) %collective-permute-start.11) | collective-permute-done | bytes 229408 | tf_op jit(solution)/shard_map/ppermute | solution.py:59
  75.7 0.9 copy-done.6
  76.7 9.0 %attention.1 = (bf16[4,128,896]{2,1,0:T(8,128)(2,1)}, bf16[4,128,896]{2,1,0:T(8,128)(2,1)S(1)}, bf16[256,512]{1,0:T(8,128)(2,1)S(1)}) custom-call(bf16[128,896]{1,0:T(8,128)(2,1)S(1)} %bitcast.55, bf16[128,896]{1,0:T(8,128)(2,1)S(1)} %collective-permute-done.8.r_1_, bf16[128,896]{1,0:T(8,128)(2,1)S(1)} %collective-permute-done.9.r_2_, ...), custom_call_target="tpu_custom_call" | custom-call | flops 9900000256 | tf_op jit(solution)/shard_map/attention/pallas_call | solution.py:262
  85.7 0.1 collective-permute-start.13
  85.8 4.8 %branches.1 = (bf16[4,256,512]{2,1,0:T(8,128)(2,1)}, bf16[4,256,512]{2,1,0:T(8,128)(2,1)S(1)}) custom-call(s32[8]{0:T(128)S(1)} %pad_add_fusion.r_0_, bf16[256,512]{1,0:T(8,128)(2,1)S(1)} %get-tuple-element.27.r_1_, bf16[512,4096]{1,0:T(8,128)(2,1)} %r_2_.1), custom_call_target="tpu_custom_call" | custom-call | flops 4400000000 | tf_op jit(solution)/shard_map/branches/pallas_call | solution.py:190
  90.7 0.5 collective-permute-start.17
  91.1 0.8 dynamic_slice.3
  91.9 0.1 slice_reduce_fusion
  92.0 1.4 add_convert_fusion.1
  93.4 0.1 slice_bitcast_fusion.4
  93.5 2.6 %collective-permute-start.14 = (bf16[128,896]{1,0:T(8,128)(2,1)S(1)}, bf16[128,896]{1,0:T(8,128)(2,1)S(1)}, u32[]{:S(2)}, u32[]{:S(2)}) collective-permute-start(bf16[128,896]{1,0:T(8,128)(2,1)S(1)} %get-tuple-element.45), channel_id=1, source_target_pairs={{0,6},{1,7},{2,0},{3,1},{4,2},{5,3},{6,4},{7,5},{8,14},{9,15},{10,... | collective-permute-start | bytes 688136 | tf_op jit(solution)/shard_map/ppermute | solution.py:68
  96.1 1.0 collective-permute-start.16
  97.1 1.5 %add_convert_fusion = bf16[4,256,512]{2,1,0:T(8,128)(2,1)S(1)} fusion(bf16[4,256,512]{2,1,0:T(8,128)(2,1)} %collective-permute-done.17, bf16[4,256,512]{2,1,0:T(8,128)(2,1)S(1)} %get-tuple-element.28), kind=kLoop, calls=%fused_computation | loop fusion | flops 2097152 | bytes 3145728 | tf_op jit(solution)/shard_map/convert_element_type | solution.py:63
  98.6 7.6 %collective-permute-done.14 = bf16[128,896]{1,0:T(8,128)(2,1)S(1)} collective-permute-done((bf16[128,896]{1,0:T(8,128)(2,1)S(1)}, bf16[128,896]{1,0:T(8,128)(2,1)S(1)}, u32[]{:S(2)}, u32[]{:S(2)}) %collective-permute-start.14) | collective-permute-done | bytes 229408 | tf_op jit(solution)/shard_map/ppermute | solution.py:68
  106.2 3.4 %collective-permute-done.16 = bf16[128,896]{1,0:T(8,128)(2,1)S(1)} collective-permute-done((bf16[128,896]{1,0:T(8,128)(2,1)S(1)}, bf16[128,896]{1,0:T(8,128)(2,1)S(1)}, u32[]{:S(2)}, u32[]{:S(2)}) %collective-permute-start.16) | collective-permute-done | bytes 229408 | tf_op jit(solution)/shard_map/ppermute | solution.py:68
  109.6 0.1 slice_bitcast_fusion
  109.7 1.0 collective-permute-start.18
  110.7 0.3 collective-permute-start.19
  110.9 0.9 collective-permute-start.20
  111.8 0.1 select_reduce_fusion.1.slot
  112.0 1.7 %placed_grads.1 = bf16[32,16,896]{2,1,0:T(8,128)(2,1)} custom-call(s32[32]{0:T(128)S(1)} %get-tuple-element.37.reading, bf16[8,16,896]{2,1,0:T(8,128)(2,1)S(1)} %bitcast.42, bf16[8,16,896]{2,1,0:T(8,128)(2,1)S(1)} %bitcast.48, bf16[8,16,896]{2,1,0:T(8,128)(2,1)S(1)} %bitcast.49, bf16[8,16,896]{2,1,0:T(8,128)(2,1)S(1)} %bitcast.50), custom_call_target="tpu_custom_call" | custom-call | flops 1870000000 | tf_op jit(solution)/shard_map/placed_grads/pallas_call | solution.py:330
  113.7 9.8 %all-to-all-start.2 = ((bf16[32,16,896]{2,1,0:T(8,128)(2,1)}), bf16[32,16,896]{2,1,0:T(8,128)(2,1)S(1)}, u32[]{:S(2)}, u32[]{:S(2)}) async-start(bf16[32,16,896]{2,1,0:T(8,128)(2,1)} %placed_grads.1), calls=%async_computation.2 | async-start | bytes 1835008 | tf_op jit(solution)/shard_map/all_to_all | solution.py:458
  123.5 1.6 %collective-permute-done.20.refs_3_ = bf16[256,512]{1,0:T(8,128)(2,1)S(1)} collective-permute-done((bf16[256,512]{1,0:T(8,128)(2,1)S(1)}, bf16[256,512]{1,0:T(8,128)(2,1)S(1)}, u32[]{:S(2)}, u32[]{:S(2)}) %collective-permute-start.20) | collective-permute-done | bytes 262176 | tf_op jit(solution)/shard_map/ppermute | solution.py:68
  125.1 0.9 mixed.1
  126.0 14.0 %all-gather = f32[2048,1]{1,0:T(8,128)S(1)} all-gather(f32[256,1]{1,0:T(8,128)S(1)} %get-tuple-element.32), channel_id=2, replica_groups=mesh['dp'=32,'mp'=8] {'mp'}, dimensions={0}, use_global_device_ids=true | all-gather | bytes 9216 | tf_op jit(solution)/shard_map/all_gather | solution.py:463
  140.1 0.3 reduce
  140.5 0.8 multiply_convert_fusion
  141.3 6.7 %all-to-all-done.2.back = bf16[32,16,896]{2,1,0:T(8,128)(2,1)S(1)} async-done(((bf16[32,16,896]{2,1,0:T(8,128)(2,1)}), bf16[32,16,896]{2,1,0:T(8,128)(2,1)S(1)}, u32[]{:S(2)}, u32[]{:S(2)}) %all-to-all-start.2) | async-done | bytes 917536 | tf_op jit(solution)/shard_map/all_to_all | solution.py:458
  148.0 1.9 %d_encodings.1 = bf16[8,16,896]{2,1,0:T(8,128)(2,1)} custom-call(s32[8]{0:T(128)S(1)} %select_reduce_fusion.1.slot, bf16[32,16,896]{2,1,0:T(8,128)(2,1)S(1)} %all-to-all-done.2.back, bf16[8,16,896]{2,1,0:T(8,128)(2,1)S(1)} %copy-done.4, f32[1,1,896]{2,1,0:T(1,128)S(1)} %reshape.98.gain), custom_call_target="tpu_custom_call" | custom-call | flops 2090000000 | tf_op jit(solution)/shard_map/d_encodings/pallas_call | solution.py:383
  (37 shorter events, 0.1 us)
Async XLA Ops:
  2.3 20.2 %all-to-all-start = ((s32[32,1,128]{2,1,0:T(1,128)}), s32[32,1,128]{2,1,0:T(1,128)S(1)}, u32[]{:S(2)}, u32[]{:S(2)}) async-start(s32[32,1,128]{2,1,0:T(1,128)} %broadcast_in_dim.49), calls=%async_computation | async-start | bytes 32768 | tf_op jit(solution)/shard_map/all_to_all | solution.py:429
  14.0 20.7 %collective-permute-start = (bf16[256,512]{1,0:T(8,128)(2,1)}, bf16[256,512]{1,0:T(8,128)(2,1)S(1)}, u32[]{:S(2)}, u32[]{:S(2)}) collective-permute-start(bf16[256,512]{1,0:T(8,128)(2,1)} %tok.1), channel_id=1, source_target_pairs={{0,2},{1,3},{2,4},{3,5},{4,6},{5,7},{6,0},{7,1},{8,10},{9,11},{10,... | collective-permute-start | bytes 786440 | tf_op jit(solution)/shard_map/ppermute | solution.py:55
  15.6 21.0 %collective-permute-start.1 = (bf16[256,512]{1,0:T(8,128)(2,1)}, bf16[256,512]{1,0:T(8,128)(2,1)S(1)}, u32[]{:S(2)}, u32[]{:S(2)}) collective-permute-start(bf16[256,512]{1,0:T(8,128)(2,1)} %tok.1), channel_id=1, source_target_pairs={{0,4},{1,5},{2,6},{3,7},{4,0},{5,1},{6,2},{7,3},{8,12},{9,13},{10,... | collective-permute-start | bytes 786440 | tf_op jit(solution)/shard_map/ppermute | solution.py:55
  18.3 18.3 %collective-permute-start.2 = (bf16[256,512]{1,0:T(8,128)(2,1)}, bf16[256,512]{1,0:T(8,128)(2,1)S(1)}, u32[]{:S(2)}, u32[]{:S(2)}) collective-permute-start(bf16[256,512]{1,0:T(8,128)(2,1)} %tok.1), channel_id=1, source_target_pairs={{0,6},{1,7},{2,0},{3,1},{4,2},{5,3},{6,4},{7,5},{8,14},{9,15},{10,... | collective-permute-start | bytes 786440 | tf_op jit(solution)/shard_map/ppermute | solution.py:55
  22.5 0.9 copy-start.3
  23.4 9.7 %copy-start = (bf16[256,512]{1,0:T(8,128)(2,1)S(1)}, bf16[256,512]{1,0:T(8,128)(2,1)}, u32[]{:S(2)}) copy-start(bf16[256,512]{1,0:T(8,128)(2,1)} %r_1_.2) | copy-start | bytes 786436
  23.4 13.2 %copy-start.1 = (bf16[256,512]{1,0:T(8,128)(2,1)S(1)}, bf16[256,512]{1,0:T(8,128)(2,1)}, u32[]{:S(2)}) copy-start(bf16[256,512]{1,0:T(8,128)(2,1)} %tok.1) | copy-start | bytes 786436
  25.4 31.8 %all-to-all-start.1 = ((bf16[32,16,896]{2,1,0:T(8,128)(2,1)}), bf16[32,16,896]{2,1,0:T(8,128)(2,1)S(1)}, u32[]{:S(2)}, u32[]{:S(2)}) async-start(bf16[32,16,896]{2,1,0:T(8,128)(2,1)} %outgoing_rows.1), calls=%async_computation.1 | async-start | bytes 1835008 | tf_op jit(solution)/shard_map/all_to_all | solution.py:442
  33.1 13.0 %collective-permute-start.4 = (bf16[256,512]{1,0:T(8,128)(2,1)S(1)}, bf16[256,512]{1,0:T(8,128)(2,1)S(1)}, u32[]{:S(2)}, u32[]{:S(2)}) collective-permute-start(bf16[256,512]{1,0:T(8,128)(2,1)S(1)} %copy-done), channel_id=1, source_target_pairs={{0,2},{1,3},{2,4},{3,5},{4,6},{5,7},{6,0},{7,1},{8,10},{9,11},{10,... | collective-permute-start | bytes 786440 | tf_op jit(solution)/shard_map/ppermute | solution.py:55
  33.8 12.3 %collective-permute-start.5 = (bf16[256,512]{1,0:T(8,128)(2,1)S(1)}, bf16[256,512]{1,0:T(8,128)(2,1)S(1)}, u32[]{:S(2)}, u32[]{:S(2)}) collective-permute-start(bf16[256,512]{1,0:T(8,128)(2,1)S(1)} %copy-done), channel_id=1, source_target_pairs={{0,4},{1,5},{2,6},{3,7},{4,0},{5,1},{6,2},{7,3},{8,12},{9,13},{10,... | collective-permute-start | bytes 786440 | tf_op jit(solution)/shard_map/ppermute | solution.py:55
  34.7 12.0 %collective-permute-start.6 = (bf16[256,512]{1,0:T(8,128)(2,1)S(1)}, bf16[256,512]{1,0:T(8,128)(2,1)S(1)}, u32[]{:S(2)}, u32[]{:S(2)}) collective-permute-start(bf16[256,512]{1,0:T(8,128)(2,1)S(1)} %copy-done), channel_id=1, source_target_pairs={{0,6},{1,7},{2,0},{3,1},{4,2},{5,3},{6,4},{7,5},{8,14},{9,15},{10,... | collective-permute-start | bytes 786440 | tf_op jit(solution)/shard_map/ppermute | solution.py:55
  36.6 11.3 %copy-start.8 = (f32[4096]{0:T(1024)S(1)}, f32[4096]{0:T(1024)}, u32[]{:S(2)}) copy-start(f32[4096]{0:T(1024)} %param.13) | copy-start | bytes 49156
  37.7 10.2 %collective-permute-start.3 = (bf16[4,256,512]{2,1,0:T(8,128)(2,1)}, bf16[4,256,512]{2,1,0:T(8,128)(2,1)}, u32[]{:S(2)}, u32[]{:S(2)}) collective-permute-start(bf16[4,256,512]{2,1,0:T(8,128)(2,1)} %pad_maximum_fusion), channel_id=1, source_target_pairs={{0,1},{1,0},{2,3},{3,2},{4,5},{5,4},{6,7},{7,6},{8,9},{9,8},{10,11... | collective-permute-start | bytes 3145736 | tf_op jit(solution)/shard_map/ppermute | solution.py:59
  47.9 4.8 %collective-permute-start.7 = (bf16[4,256,512]{2,1,0:T(8,128)(2,1)}, bf16[4,256,512]{2,1,0:T(8,128)(2,1)}, u32[]{:S(2)}, u32[]{:S(2)}) collective-permute-start(bf16[4,256,512]{2,1,0:T(8,128)(2,1)} %pad_maximum_fusion.1), channel_id=1, source_target_pairs={{0,1},{1,0},{2,3},{3,2},{4,5},{5,4},{6,7},{7,6},{8,9},{9,8},{10,11... | collective-permute-start | bytes 3145736 | tf_op jit(solution)/shard_map/ppermute | solution.py:59
  57.1 1.0 copy-start.5
  57.2 18.6 %copy-start.2 = (bf16[896,512]{1,0:T(8,128)(2,1)S(1)}, bf16[896,512]{1,0:T(8,128)(2,1)}, u32[]{:S(2)}) copy-start(bf16[896,512]{1,0:T(8,128)(2,1)} %r_8_.1) | copy-start | bytes 2752516
  58.2 9.3 %collective-permute-start.8 = (bf16[128,896]{1,0:T(8,128)(2,1)S(1)}, bf16[128,896]{1,0:T(8,128)(2,1)S(1)}, u32[]{:S(2)}, u32[]{:S(2)}) collective-permute-start(bf16[128,896]{1,0:T(8,128)(2,1)S(1)} %bitcast.51), channel_id=1, source_target_pairs={{0,2},{1,3},{2,4},{3,5},{4,6},{5,7},{6,0},{7,1},{8,10},{9,11},{10,... | collective-permute-start | bytes 688136 | tf_op jit(solution)/shard_map/ppermute | solution.py:55
  58.6 14.5 %collective-permute-start.9 = (bf16[128,896]{1,0:T(8,128)(2,1)S(1)}, bf16[128,896]{1,0:T(8,128)(2,1)S(1)}, u32[]{:S(2)}, u32[]{:S(2)}) collective-permute-start(bf16[128,896]{1,0:T(8,128)(2,1)S(1)} %bitcast.52), channel_id=1, source_target_pairs={{0,4},{1,5},{2,6},{3,7},{4,0},{5,1},{6,2},{7,3},{8,12},{9,13},{10,... | collective-permute-start | bytes 688136 | tf_op jit(solution)/shard_map/ppermute | solution.py:55
  62.2 10.9 %collective-permute-start.10 = (bf16[128,896]{1,0:T(8,128)(2,1)S(1)}, bf16[128,896]{1,0:T(8,128)(2,1)S(1)}, u32[]{:S(2)}, u32[]{:S(2)}) collective-permute-start(bf16[128,896]{1,0:T(8,128)(2,1)S(1)} %bitcast.53), channel_id=1, source_target_pairs={{0,6},{1,7},{2,0},{3,1},{4,2},{5,3},{6,4},{7,5},{8,14},{9,15},{10,... | collective-permute-start | bytes 688136 | tf_op jit(solution)/shard_map/ppermute | solution.py:55
  73.2 2.6 %collective-permute-start.12 = (bf16[3,128,896]{2,1,0:T(8,128)(2,1)S(1)}, bf16[3,128,896]{2,1,0:T(8,128)(2,1)S(1)}, u32[]{:S(2)}, u32[]{:S(2)}) collective-permute-start(bf16[3,128,896]{2,1,0:T(8,128)(2,1)S(1)} %pad_maximum_fusion.2), channel_id=1, source_target_pairs={{0,1},{1,0},{2,3},{3,2},{4,5},{5,4},{6,7},{7,6},{8,9},{9,8},{10,11... | collective-permute-start | bytes 2064392 | tf_op jit(solution)/shard_map/ppermute | solution.py:59
  73.3 2.5 %collective-permute-start.11 = (bf16[128,896]{1,0:T(8,128)(2,1)S(1)}, bf16[128,896]{1,0:T(8,128)(2,1)S(1)}, u32[]{:S(2)}, u32[]{:S(2)}) collective-permute-start(bf16[128,896]{1,0:T(8,128)(2,1)S(1)} %bitcast.54), channel_id=1, source_target_pairs={{0,1},{1,0},{2,3},{3,2},{4,5},{5,4},{6,7},{7,6},{8,9},{9,8},{10,11... | collective-permute-start | bytes 688136 | tf_op jit(solution)/shard_map/ppermute | solution.py:59
  75.7 1.0 copy-start.6
  85.7 6.3 %collective-permute-start.13 = (bf16[4,128,896]{2,1,0:T(8,128)(2,1)}, bf16[4,128,896]{2,1,0:T(8,128)(2,1)}, u32[]{:S(2)}, u32[]{:S(2)}) collective-permute-start(bf16[4,128,896]{2,1,0:T(8,128)(2,1)} %get-tuple-element.26), channel_id=1, source_target_pairs={{0,1},{1,0},{2,3},{3,2},{4,5},{5,4},{6,7},{7,6},{8,9},{9,8},{10,11... | collective-permute-start | bytes 2752520 | tf_op jit(solution)/shard_map/ppermute | solution.py:59
  90.7 6.4 %collective-permute-start.17 = (bf16[4,256,512]{2,1,0:T(8,128)(2,1)}, bf16[4,256,512]{2,1,0:T(8,128)(2,1)}, u32[]{:S(2)}, u32[]{:S(2)}) collective-permute-start(bf16[4,256,512]{2,1,0:T(8,128)(2,1)} %get-tuple-element.29), channel_id=1, source_target_pairs={{0,1},{1,0},{2,3},{3,2},{4,5},{5,4},{6,7},{7,6},{8,9},{9,8},{10,11... | collective-permute-start | bytes 3145736 | tf_op jit(solution)/shard_map/ppermute | solution.py:59
  93.5 12.8 %collective-permute-start.14 = (bf16[128,896]{1,0:T(8,128)(2,1)S(1)}, bf16[128,896]{1,0:T(8,128)(2,1)S(1)}, u32[]{:S(2)}, u32[]{:S(2)}) collective-permute-start(bf16[128,896]{1,0:T(8,128)(2,1)S(1)} %get-tuple-element.45), channel_id=1, source_target_pairs={{0,6},{1,7},{2,0},{3,1},{4,2},{5,3},{6,4},{7,5},{8,14},{9,15},{10,... | collective-permute-start | bytes 688136 | tf_op jit(solution)/shard_map/ppermute | solution.py:68
  96.1 10.1 %collective-permute-start.15 = (bf16[128,896]{1,0:T(8,128)(2,1)S(1)}, bf16[128,896]{1,0:T(8,128)(2,1)S(1)}, u32[]{:S(2)}, u32[]{:S(2)}) collective-permute-start(bf16[128,896]{1,0:T(8,128)(2,1)S(1)} %get-tuple-element.44), channel_id=1, source_target_pairs={{0,4},{1,5},{2,6},{3,7},{4,0},{5,1},{6,2},{7,3},{8,12},{9,13},{10,... | collective-permute-start | bytes 688136 | tf_op jit(solution)/shard_map/ppermute | solution.py:68
  96.1 13.5 %collective-permute-start.16 = (bf16[128,896]{1,0:T(8,128)(2,1)S(1)}, bf16[128,896]{1,0:T(8,128)(2,1)S(1)}, u32[]{:S(2)}, u32[]{:S(2)}) collective-permute-start(bf16[128,896]{1,0:T(8,128)(2,1)S(1)} %get-tuple-element.43), channel_id=1, source_target_pairs={{0,2},{1,3},{2,4},{3,5},{4,6},{5,7},{6,0},{7,1},{8,10},{9,11},{10,... | collective-permute-start | bytes 688136 | tf_op jit(solution)/shard_map/ppermute | solution.py:68
  109.7 13.8 %collective-permute-start.18 = (bf16[256,512]{1,0:T(8,128)(2,1)S(1)}, bf16[256,512]{1,0:T(8,128)(2,1)S(1)}, u32[]{:S(2)}, u32[]{:S(2)}) collective-permute-start(bf16[256,512]{1,0:T(8,128)(2,1)S(1)} %get-tuple-element.41), channel_id=1, source_target_pairs={{0,6},{1,7},{2,0},{3,1},{4,2},{5,3},{6,4},{7,5},{8,14},{9,15},{10,... | collective-permute-start | bytes 786440 | tf_op jit(solution)/shard_map/ppermute | solution.py:68
  110.7 12.8 %collective-permute-start.19 = (bf16[256,512]{1,0:T(8,128)(2,1)S(1)}, bf16[256,512]{1,0:T(8,128)(2,1)S(1)}, u32[]{:S(2)}, u32[]{:S(2)}) collective-permute-start(bf16[256,512]{1,0:T(8,128)(2,1)S(1)} %get-tuple-element.40), channel_id=1, source_target_pairs={{0,4},{1,5},{2,6},{3,7},{4,0},{5,1},{6,2},{7,3},{8,12},{9,13},{10,... | collective-permute-start | bytes 786440 | tf_op jit(solution)/shard_map/ppermute | solution.py:68
  110.9 14.2 %collective-permute-start.20 = (bf16[256,512]{1,0:T(8,128)(2,1)S(1)}, bf16[256,512]{1,0:T(8,128)(2,1)S(1)}, u32[]{:S(2)}, u32[]{:S(2)}) collective-permute-start(bf16[256,512]{1,0:T(8,128)(2,1)S(1)} %get-tuple-element.39), channel_id=1, source_target_pairs={{0,2},{1,3},{2,4},{3,5},{4,6},{5,7},{6,0},{7,1},{8,10},{9,11},{10,... | collective-permute-start | bytes 786440 | tf_op jit(solution)/shard_map/ppermute | solution.py:68
  113.7 34.3 %all-to-all-start.2 = ((bf16[32,16,896]{2,1,0:T(8,128)(2,1)}), bf16[32,16,896]{2,1,0:T(8,128)(2,1)S(1)}, u32[]{:S(2)}, u32[]{:S(2)}) async-start(bf16[32,16,896]{2,1,0:T(8,128)(2,1)} %placed_grads.1), calls=%async_computation.2 | async-start | bytes 1835008 | tf_op jit(solution)/shard_map/all_to_all | solution.py:458
  126.0 14.4 %copy-start.7 = (bf16[256,512]{1,0:T(8,128)(2,1)S(1)}, bf16[256,512]{1,0:T(8,128)(2,1)}, u32[]{:S(2)}) copy-start(bf16[256,512]{1,0:T(8,128)(2,1)} %get-tuple-element.17) | copy-start | bytes 786436
  126.0 22.0 %copy-start.4 = (bf16[8,16,896]{2,1,0:T(8,128)(2,1)S(1)}, bf16[8,16,896]{2,1,0:T(8,128)(2,1)}, u32[]{:S(2)}) copy-start(bf16[8,16,896]{2,1,0:T(8,128)(2,1)} %enc.3) | copy-start | bytes 688132

commit v2 on v1

--- a/solution.py
+++ b/solution.py
@@ -16,7 +16,7 @@
 IDS_WIDTH = 128
 GROUP = 8
 MIX_COST = 100
-VMEM_LIMIT = 48 * 1024 * 1024
+VMEM_LIMIT = 24 * 1024 * 1024
 
 
 def rms_scale(values):
@@ -133,70 +133,66 @@
     )(src, *pieces, gain.reshape(count, share), w_query)
 
 
-def back_kernel(count, src, *refs):
-    pieces, rest = views(count, refs)
-    w_hbm, out, w_buf, sems = rest
-    share = pieces[0].shape[1]
+def back_kernel(count, whole, w_hbm, out, w_buf, sems):
+    share = whole.shape[1] // count
     copies = []
     for k in range(count):
-        start = pl.multiple_of(src[k] * share, share)
-        cp = pltpu.make_async_copy(w_hbm.at[:, pl.ds(start, share)], w_buf.at[k], sems.at[k])
+        cols = slice(k * share, (k + 1) * share)
+        cp = pltpu.make_async_copy(w_hbm.at[:, cols], w_buf.at[k], sems.at[k])
         cp.start()
         copies.append(cp)
     acc = jnp.zeros(out.shape, F32)
     for k in range(count):
         copies[k].wait()
-        acc = acc + dot_nt(pieces[k][...], w_buf[k])
+        acc = acc + dot_nt(whole[:, k * share : (k + 1) * share], w_buf[k])
     out[...] = dot(shift_matrix(out.shape[0], BLOCK - 1, False), acc.astype(BF16)).astype(BF16)
 
 
-def run_back(src, pieces, w_out):
-    count = 2 * (len(pieces) - 1)
-    rows, share = pieces[0].shape
+def run_back(whole, w_out, count):
     cols = w_out.shape[0]
+    share = whole.shape[1] // count
     return pl.pallas_call(
         lambda *r: back_kernel(count, *r),
-        out_shape=jax.ShapeDtypeStruct((rows, cols), BF16),
-        in_specs=[smem()] + [vmem()] * len(pieces) + [hbm()],
+        out_shape=jax.ShapeDtypeStruct((whole.shape[0], cols), BF16),
+        in_specs=[vmem(), hbm()],
         out_specs=vmem(),
         scratch_shapes=[pltpu.VMEM((count, cols, share), BF16), pltpu.SemaphoreType.DMA((count,))],
         compiler_params=params(),
         cost_estimate=cost(2.25),
         name="d_attended",
-    )(src, *pieces, w_out)
-
-
-def branch_kernel(count, src, att, w_hbm, send, keep, w_buf, sems):
-    share = send.shape[2]
-    half = count // 2
+    )(whole, w_out)
+
+
+def branch_kernel(count, att, w_hbm, out, w_buf, sems):
+    share = out.shape[1] // count
     copies = []
-    order = list(range(half, count)) + list(range(half))
-    for k in order:
-        start = pl.multiple_of(src[k] * share, share)
-        cp = pltpu.make_async_copy(w_hbm.at[:, pl.ds(start, share)], w_buf.at[k], sems.at[k])
+    for k in range(count):
+        cols = slice(k * share, (k + 1) * share)
+        cp = pltpu.make_async_copy(w_hbm.at[:, cols], w_buf.at[k], sems.at[k])
         cp.start()
         copies.append(cp)
     a = dot(shift_matrix(att.shape[0], BLOCK - 1, True), att[...]).astype(BF16)
-    for k, cp in zip(order, copies):
-        cp.wait()
-        out = keep.at[k] if k < half else send.at[k - half]
-        out[...] = dot(a, w_buf[k]).astype(BF16)
-
-
-def run_branch(src, att, w_out, count):
+    for k in range(count):
+        copies[k].wait()
+        out[:, k * share : (k + 1) * share] = dot(a, w_buf[k]).astype(BF16)
+
+
+def run_branch(att, w_out, count):
     rows, cols = att.shape
-    share = w_out.shape[1] // count
-    shape = jax.ShapeDtypeStruct((count // 2, rows, share), BF16)
+    width = w_out.shape[1]
     return pl.pallas_call(
         lambda *r: branch_kernel(count, *r),
-        out_shape=(shape, shape),
-        in_specs=[smem(), vmem(), hbm()],
-        out_specs=(vmem(), vmem()),
-        scratch_shapes=[pltpu.VMEM((count, cols, share), BF16), pltpu.SemaphoreType.DMA((count,))],
+        out_shape=jax.ShapeDtypeStruct((rows, width), BF16),
+        in_specs=[vmem(), hbm()],
+        out_specs=vmem(),
+        scratch_shapes=[
+            pltpu.VMEM((count, cols, width // count), BF16),
+            pltpu.SemaphoreType.DMA((count,)),
+        ],
         compiler_params=params(),
         cost_estimate=cost(4),
         name="branches",
-    )(src, att, w_out)
+    )(att, w_out)
 
 
 def attention_kernel(count, blocks, *refs):
@@ -334,7 +330,7 @@
         out_specs=vmem(),
         scratch_shapes=[pltpu.VMEM(shape, BF16)],
         compiler_params=params(),
-        cost_estimate=cost(1.7),
+        cost_estimate=cost(60),
         name="placed_grads",
     )(reading, *parts)
 
@@ -438,29 +434,29 @@
 
     tok_own = over_chips(tokens, count)
     outgoing = run_outgoing(requested, encodings, gain_enc)
-    outgoing, cot_in = lax.optimization_barrier((outgoing, cotangent))
     incoming = lax.all_to_all(outgoing, "dp", split_axis=0, concat_axis=0, tiled=True)
-    cot_own = over_chips(cot_in, count)
     q = run_query(src, tok_own + [swap(jnp.stack(tok_own), count)], gain_dec, w_query)
-    d = run_back(src, cot_own + [swap(jnp.stack(cot_own), count)], w_out)
+    d = run_back(lax.all_gather(cotangent, "mp", axis=1, tiled=True), w_out, count)
     incoming, q, d = lax.optimization_barrier((incoming, q, d))
     picked = run_pick(owner, incoming).reshape(readings * own_tokens, width)
     row_own = over_chips(picked, count)
     rows = row_own + [swap(picked, count)[None], swap(jnp.stack(row_own[1:]), count)]
     send, keep, att = run_attention(rows, q, d, w_key, w_value, blocks)
     pair = pair_sum(send, keep, count)
+    branch = run_branch(att, w_out, count)
+    pair, branch = lax.optimization_barrier((pair, branch))
     parts = pair_shares(pair, count)
-    b_send, b_keep = run_branch(src, att, w_out, count)
-    b_pair = pair_sum(b_send, b_keep, count)
-    parts, b_pair = lax.optimization_barrier((parts, b_pair))
-    b_parts = pair_shares(b_pair, count)
+    summed = lax.psum_scatter(branch, "mp", scatter_dimension=1, tiled=True)
     back_out = run_place(reading, [p.reshape(readings, own_tokens, width) for p in parts])
     back_in = lax.all_to_all(back_out, "dp", split_axis=0, concat_axis=0, tiled=True)
 
-    mixed, squares = run_mix(tokens, b_parts)
+    mixed, squares = run_mix(tokens, [summed])
     mixed_wide = mixed.astype(F32)
     squares = squares[:, 0]
-    total = jnp.sum(lax.all_gather(squares, "mp", axis=0), axis=0)
+    squares = squares + swap(squares, count)
+    total = squares
+    for k in range(1, half):
+        total = total + lax.ppermute(squares, "mp", chip_shift(count, k))
     post = lax.rsqrt(total / (share_cols * count) + EPS)[:, None]
     gain_here = lax.dynamic_slice_in_dim(gain_post, here * share_cols, share_cols, 0)
     ffn = (mixed_wide * post * gain_here).astype(BF16)

time: 152 us -> 155 us (1.020)
  blocking collectives: 14 us -> 0 us
  between operations: 1.05 us -> 14.3 us
  waiting for transfers between devices: 43.3 us -> 55.9 us
  local copies, waits for them, and re-layouts: 5.19 us -> 12.2 us
  starting transfers between devices: 49.3 us -> 42.9 us
  Pallas kernels: 30.4 us -> 26.3 us
  other arithmetic: 6.78 us -> 2.7 us
    reduce_scatter x0 -> x1, waiting for transfers between devices: none -> 16.5 us  [shards(): summed = lax.psum_scatter(branch, 'mp', scatter_dimension=1, tiled=True)]
    all_gather x1 -> x0, blocking collectives: 14 us -> none  [shards(): total = jnp.sum(lax.all_gather(squares, 'mp', axis=0), axis=0)]
    unnamed x19 -> x33, local copies, waits for them, and re-layouts: 2.69 us -> 8.66 us
    ppermute x9 -> x6, waiting for transfers between devices: 19.9 us -> 15 us  [over_chips(): lax.ppermute(x, 'mp', chip_shift(count, k))]
    ppermute x9 -> x6, starting transfers between devices: 13.2 us -> 8.46 us  [over_chips(): lax.ppermute(x, 'mp', chip_shift(count, k))]
    ppermute x6 -> x5, waiting for transfers between devices: 1.98 us -> 5.73 us  [swap(): return lax.ppermute(x, 'mp', core_swap(count))]
    all_to_all x1, waiting for transfers between devices: 6.72 us -> 2.97 us  [shards(): lax.all_to_all(back_out, 'dp', split_axis=0, concat_axis=0, tiled=True)]
    ppermute x6 -> x3, waiting for transfers between devices: 12.7 us -> 9.38 us  [pair_shares(): lax.ppermute(pair[k], 'mp', chip_shift(count, -k))]
  transfers between devices with their start and end apart: 24 -> 22, of which waited for: 10 -> 13; matrix products, arithmetic and copies ran while one was open for 5% -> 4% of each run, Pallas kernels for 12% -> 11%
where the time goes in v2:
time: 155 us; the launch traced here: 154 us
  waiting for transfers between devices  55.9 us (36%)
  starting transfers between devices  42.9 us (28%)
  Pallas kernels  26.3 us (17%)
  between operations  14.3 us (9%)
  local copies, waits for them, and re-layouts  12.2 us (8%)
  other arithmetic  2.7 us (2%)
    reduce_scatter x1, waiting for transfers between devices, shards(): summed = lax.psum_scatter(branch, 'mp', scatter_dimension=1, tiled=True)  16.5 us
    ppermute x6, waiting for transfers between devices, over_chips(): lax.ppermute(x, 'mp', chip_shift(count, k))  15 us
    all_to_all x1, starting transfers between devices, shards(): lax.all_to_all(jnp.broadcast_to(wanted[:, None], (dp_count, IDS_WIDTH)),...  11.7 us
    all_to_all x1, starting transfers between devices, shards(): lax.all_to_all(back_out, 'dp', split_axis=0, concat_axis=0, tiled=True)  9.69 us
    ppermute x3, waiting for transfers between devices, pair_shares(): lax.ppermute(pair[k], 'mp', chip_shift(count, -k))  9.38 us
    unnamed x33, local copies, waits for them, and re-layouts  8.66 us
    ppermute x6, starting transfers between devices, over_chips(): lax.ppermute(x, 'mp', chip_shift(count, k))  8.46 us
    pallas_call x1, Pallas kernels, run_attention(): pl.pallas_call(lambda *r: attention_kernel(count, blocks, *r), out_shape=...  7.86 us
  transfers between devices with their start and end apart: 22, of which 13 were waited for; matrix products, arithmetic and copies ran while one was open for 4% of the time, Pallas kernels for 11%

profile of v2, /device:TPU:8, one launch (start us, length us, event | category | flops | bytes accessed | tf_op | source)
XLA Modules:
  0.0 154.3 jit_solution(9059426970689512957)
XLA Ops:
  7.2 0.0 all-gather.2.cloned.1.call-start
  7.2 0.7 all-gather.2.cloned.1.call-update
  7.9 0.8 copy.17
  8.7 0.1 reshape.90
  8.8 0.1 select_reduce_fusion
  8.9 0.7 broadcast_in_dim.49
  9.6 11.7 %all-to-all-start = ((s32[32,1,128]{2,1,0:T(1,128)}), s32[32,1,128]{2,1,0:T(1,128)S(1)}, u32[]{:S(2)}, u32[]{:S(2)}) async-start(s32[32,1,128]{2,1,0:T(1,128)} %broadcast_in_dim.49), calls=%async_computation | async-start | bytes 32768 | tf_op jit(solution)/shard_map/all_to_all | solution.py:425
  21.3 2.8 %collective-permute-start.2 = (bf16[256,512]{1,0:T(8,128)(2,1)}, bf16[256,512]{1,0:T(8,128)(2,1)S(1)}, u32[]{:S(2)}, u32[]{:S(2)}) collective-permute-start(bf16[256,512]{1,0:T(8,128)(2,1)} %tok.1), channel_id=1, source_target_pairs={{0,6},{1,7},{2,0},{3,1},{4,2},{5,3},{6,4},{7,5},{8,14},{9,15},{10,... | collective-permute-start | bytes 786440 | tf_op jit(solution)/shard_map/ppermute | solution.py:55
  24.1 0.8 collective-permute-start.1
  24.9 0.9 collective-permute-start
  25.8 0.7 reshape.91.gain
  26.5 3.2 %all-to-all-done = s32[32,1,128]{2,1,0:T(1,128)S(1)} async-done(((s32[32,1,128]{2,1,0:T(1,128)}), s32[32,1,128]{2,1,0:T(1,128)S(1)}, u32[]{:S(2)}, u32[]{:S(2)}) %all-to-all-start) | async-done | bytes 16416 | tf_op jit(solution)/shard_map/all_to_all | solution.py:425
  29.7 0.9 copy-done.10
  30.7 1.9 %outgoing_rows.1 = bf16[32,16,896]{2,1,0:T(8,128)(2,1)} custom-call(s32[32,128]{1,0:T(8,128)S(1)} %bitcast.28, bf16[8,16,896]{2,1,0:T(8,128)(2,1)S(1)} %copy-done.10, f32[1,1,896]{2,1,0:T(1,128)S(1)} %reshape.91.gain), custom_call_target="tpu_custom_call" | custom-call | flops 1870000000 | tf_op jit(solution)/shard_map/outgoing_rows/pallas_call | solution.py:280
  32.6 6.7 %all-to-all-start.1 = ((bf16[32,16,896]{2,1,0:T(8,128)(2,1)}), bf16[32,16,896]{2,1,0:T(8,128)(2,1)S(1)}, u32[]{:S(2)}, u32[]{:S(2)}) async-start(bf16[32,16,896]{2,1,0:T(8,128)(2,1)} %outgoing_rows.1), calls=%async_computation.1 | async-start | bytes 1835008 | tf_op jit(solution)/shard_map/all_to_all | solution.py:437
  39.3 0.0 reduce-scatter.2.cloned.1.call-start
  39.4 4.9 %collective-permute-done.r_2_ = bf16[256,512]{1,0:T(8,128)(2,1)S(1)} collective-permute-done((bf16[256,512]{1,0:T(8,128)(2,1)}, bf16[256,512]{1,0:T(8,128)(2,1)S(1)}, u32[]{:S(2)}, u32[]{:S(2)}) %collective-permute-start) | collective-permute-done | bytes 262176 | tf_op jit(solution)/shard_map/ppermute | solution.py:55
  44.3 1.1 pad_maximum_fusion
  45.4 0.1 pad_add_fusion.r_0_
  45.5 2.8 %collective-permute-done.3.r_5_ = bf16[4,256,512]{2,1,0:T(8,128)(2,1)S(1)} collective-permute-done((bf16[4,256,512]{2,1,0:T(8,128)(2,1)}, bf16[4,256,512]{2,1,0:T(8,128)(2,1)S(1)}, u32[]{:S(2)}, u32[]{:S(2)}) %collective-permute-start.3) | collective-permute-done | bytes 1048608 | tf_op jit(solution)/shard_map/ppermute | solution.py:59
  48.3 2.2 %copy-done.3 = bf16[4096,512]{1,0:T(8,128)(2,1)S(1)} copy-done((bf16[4096,512]{1,0:T(8,128)(2,1)S(1)}, bf16[4096,512]{1,0:T(8,128)(2,1)}, u32[]{:S(2)}) %copy-start.3) | copy-done | bytes 4194328
  50.4 3.7 %queries.1.r_6_ = bf16[256,512]{1,0:T(8,128)(2,1)S(1)} custom-call(s32[8]{0:T(128)S(1)} %pad_add_fusion.r_0_, bf16[256,512]{1,0:T(8,128)(2,1)S(1)} %copy-done, bf16[256,512]{1,0:T(8,128)(2,1)S(1)} %collective-permute-done.r_2_, bf16[256,512]{1,0:T(8,128)(2,1)S(1)} %collective-permute-done.1.r_3_, bf16[256,512]{1,0:T(8,128)(2,1)S(1)} %collective-permute-done.2.r_4_, ...), custom_call_target="tpu_custom_call" | custom-call | flops 2475000064 | tf_op jit(solution)/shard_map/queries/pallas_call | solution.py:124
  54.1 0.0 all-gather.2.cloned.1.call-done.r_0_
  54.2 2.2 %copy-done.4 = bf16[512,4096]{1,0:T(8,128)(2,1)S(1)} copy-done((bf16[512,4096]{1,0:T(8,128)(2,1)S(1)}, bf16[512,4096]{1,0:T(8,128)(2,1)}, u32[]{:S(2)}) %copy-start.4) | copy-done | bytes 4194328
  56.4 1.6 %copy-done.6 = bf16[256,4096]{1,0:T(8,128)(2,1)S(1)} copy-done((bf16[256,4096]{1,0:T(8,128)(2,1)S(1)}, bf16[256,4096]{1,0:T(8,128)(2,1)}, u32[]{:S(2)}) %copy-start.6) | copy-done | bytes 2097176
  57.9 2.7 %d_attended.1.r_7_ = bf16[256,512]{1,0:T(8,128)(2,1)S(1)} custom-call(bf16[256,4096]{1,0:T(8,128)(2,1)S(1)} %copy-done.6, bf16[512,4096]{1,0:T(8,128)(2,1)S(1)} %copy-done.4), custom_call_target="tpu_custom_call" | custom-call | flops 2475000064 | tf_op jit(solution)/shard_map/d_attended/pallas_call | solution.py:154
  60.7 2.4 %all-to-all-done.1.rows = bf16[32,16,896]{2,1,0:T(8,128)(2,1)S(1)} async-done(((bf16[32,16,896]{2,1,0:T(8,128)(2,1)}), bf16[32,16,896]{2,1,0:T(8,128)(2,1)S(1)}, u32[]{:S(2)}, u32[]{:S(2)}) %all-to-all-start.1) | async-done | bytes 917536 | tf_op jit(solution)/shard_map/all_to_all | solution.py:437
  63.2 1.0 picked_rows.1
  64.1 2.4 %collective-permute-start.6 = (bf16[128,896]{1,0:T(8,128)(2,1)S(1)}, bf16[128,896]{1,0:T(8,128)(2,1)S(1)}, u32[]{:S(2)}, u32[]{:S(2)}) collective-permute-start(bf16[128,896]{1,0:T(8,128)(2,1)S(1)} %bitcast.31), channel_id=1, source_target_pairs={{0,6},{1,7},{2,0},{3,1},{4,2},{5,3},{6,4},{7,5},{8,14},{9,15},{10,... | collective-permute-start | bytes 688136 | tf_op jit(solution)/shard_map/ppermute | solution.py:55
  66.6 1.5 collective-permute-start.5
  68.1 6.6 %collective-permute-done.6.r_3_ = bf16[128,896]{1,0:T(8,128)(2,1)S(1)} collective-permute-done((bf16[128,896]{1,0:T(8,128)(2,1)S(1)}, bf16[128,896]{1,0:T(8,128)(2,1)S(1)}, u32[]{:S(2)}, u32[]{:S(2)}) %collective-permute-start.6) | collective-permute-done | bytes 229408 | tf_op jit(solution)/shard_map/ppermute | solution.py:55
  74.7 1.3 collective-permute-done.5.r_2_
  76.0 2.1 %collective-permute-done.4.r_1_ = bf16[128,896]{1,0:T(8,128)(2,1)S(1)} collective-permute-done((bf16[128,896]{1,0:T(8,128)(2,1)S(1)}, bf16[128,896]{1,0:T(8,128)(2,1)S(1)}, u32[]{:S(2)}, u32[]{:S(2)}) %collective-permute-start.4) | collective-permute-done | bytes 229408 | tf_op jit(solution)/shard_map/ppermute | solution.py:55
  78.1 0.1 pad_maximum_fusion.1
  78.2 0.1 collective-permute-start.8
  78.3 0.5 collective-permute-start.7
  78.8 2.0 %collective-permute-done.7 = bf16[128,896]{1,0:T(8,128)(2,1)S(1)} collective-permute-done((bf16[128,896]{1,0:T(8,128)(2,1)S(1)}, bf16[128,896]{1,0:T(8,128)(2,1)S(1)}, u32[]{:S(2)}, u32[]{:S(2)}) %collective-permute-start.7) | collective-permute-done | bytes 229408 | tf_op jit(solution)/shard_map/ppermute | solution.py:59
  80.8 7.9 %attention.1 = (bf16[4,128,896]{2,1,0:T(8,128)(2,1)}, bf16[4,128,896]{2,1,0:T(8,128)(2,1)S(1)}, bf16[256,512]{1,0:T(8,128)(2,1)S(1)}) custom-call(bf16[128,896]{1,0:T(8,128)(2,1)S(1)} %bitcast.35, bf16[128,896]{1,0:T(8,128)(2,1)S(1)} %collective-permute-done.4.r_1_, bf16[128,896]{1,0:T(8,128)(2,1)S(1)} %collective-permute-done.5.r_2_, ...), custom_call_target="tpu_custom_call" | custom-call | flops 9900000256 | tf_op jit(solution)/shard_map/attention/pallas_call | solution.py:258
  88.7 0.1 collective-permute-start.9
  88.8 4.7 %branches.1 = bf16[256,4096]{1,0:T(8,128)(2,1)} custom-call(bf16[256,512]{1,0:T(8,128)(2,1)S(1)} %get-tuple-element.18.r_0_, bf16[512,4096]{1,0:T(8,128)(2,1)S(1)} %copy-done.5), custom_call_target="tpu_custom_call" | custom-call | flops 4400000000 | tf_op jit(solution)/shard_map/branches/pallas_call | solution.py:183
  93.5 0.2 add_convert_fusion
  93.8 0.1 slice_bitcast_fusion
  93.8 0.1 collective-permute-start.16
  93.9 2.4 %collective-permute-start.15 = (bf16[128,896]{1,0:T(8,128)(2,1)S(1)}, bf16[128,896]{1,0:T(8,128)(2,1)S(1)}, u32[]{:S(2)}, u32[]{:S(2)}) collective-permute-start(bf16[128,896]{1,0:T(8,128)(2,1)S(1)} %get-tuple-element.26), channel_id=1, source_target_pairs={{0,4},{1,5},{2,6},{3,7},{4,0},{5,1},{6,2},{7,3},{8,12},{9,13},{10,... | collective-permute-start | bytes 688136 | tf_op jit(solution)/shard_map/ppermute | solution.py:68
  96.3 0.9 collective-permute-start.14
  97.2 1.4 dynamic_slice.3
  98.5 0.6 slice_reduce_fusion
  99.2 0.0 reduce-scatter.2.cloned.1.call-update
  99.2 8.8 %collective-permute-done.16 = bf16[128,896]{1,0:T(8,128)(2,1)S(1)} collective-permute-done((bf16[128,896]{1,0:T(8,128)(2,1)S(1)}, bf16[128,896]{1,0:T(8,128)(2,1)S(1)}, u32[]{:S(2)}, u32[]{:S(2)}) %collective-permute-start.16) | collective-permute-done | bytes 229408 | tf_op jit(solution)/shard_map/ppermute | solution.py:68
  107.9 0.6 collective-permute-done.14
  108.6 1.7 %placed_grads.1 = bf16[32,16,896]{2,1,0:T(8,128)(2,1)} custom-call(s32[32]{0:T(128)S(1)} %get-tuple-element.23.reading, bf16[8,16,896]{2,1,0:T(8,128)(2,1)S(1)} %bitcast.24, bf16[8,16,896]{2,1,0:T(8,128)(2,1)S(1)} %bitcast.37, bf16[8,16,896]{2,1,0:T(8,128)(2,1)S(1)} %bitcast.36, bf16[8,16,896]{2,1,0:T(8,128)(2,1)S(1)} %bitcast.30), custom_call_target="tpu_custom_call" | custom-call | flops 65999998976 | tf_op jit(solution)/shard_map/placed_grads/pallas_call | solution.py:326
  110.3 9.7 %all-to-all-start.2 = ((bf16[32,16,896]{2,1,0:T(8,128)(2,1)}), bf16[32,16,896]{2,1,0:T(8,128)(2,1)S(1)}, u32[]{:S(2)}, u32[]{:S(2)}) async-start(bf16[32,16,896]{2,1,0:T(8,128)(2,1)} %placed_grads.1), calls=%async_computation.3 | async-start | bytes 1835008 | tf_op jit(solution)/shard_map/all_to_all | solution.py:451
  120.0 16.5 %reduce-scatter.2.cloned.1.call-done.refs_0_ = bf16[256,512]{1,0:T(8,128)(2,1)} async-done(((bf16[256,4096]{1,0:T(8,128)(2,1)}), bf16[256,512]{1,0:T(8,128)(2,1)}) %reduce-scatter.2.cloned.1.call-update) | async-done | bytes 262160 | tf_op jit(solution)/shard_map/reduce_scatter | solution.py:449
  136.5 0.9 copy-done.9
  137.5 0.8 mixed.1
  138.3 0.1 reduce
  138.4 0.1 collective-permute-start.10
  138.5 0.1 select_reduce_fusion.1.slot
  138.6 1.0 collective-permute-done.10
  139.6 0.6 collective-permute-start.13
  140.2 1.5 collective-permute-start.11
  141.7 3.0 %all-to-all-done.2.back = bf16[32,16,896]{2,1,0:T(8,128)(2,1)S(1)} async-done(((bf16[32,16,896]{2,1,0:T(8,128)(2,1)}), bf16[32,16,896]{2,1,0:T(8,128)(2,1)S(1)}, u32[]{:S(2)}, u32[]{:S(2)}) %all-to-all-start.2) | async-done | bytes 917536 | tf_op jit(solution)/shard_map/all_to_all | solution.py:451
  144.7 1.9 %d_encodings.1 = bf16[8,16,896]{2,1,0:T(8,128)(2,1)} custom-call(s32[8]{0:T(128)S(1)} %select_reduce_fusion.1.slot, bf16[32,16,896]{2,1,0:T(8,128)(2,1)S(1)} %all-to-all-done.2.back, bf16[8,16,896]{2,1,0:T(8,128)(2,1)S(1)} %copy-done.11, f32[1,1,896]{2,1,0:T(1,128)S(1)} %copy-done.2), custom_call_target="tpu_custom_call" | custom-call | flops 2090000000 | tf_op jit(solution)/shard_map/d_encodings/pallas_call | solution.py:379
  146.7 0.8 multiply_convert_fusion
  (44 shorter events, 0.1 us)
Async XLA Ops:
  7.2 47.0 %all-gather.2.cloned.1.call-start = ((), (), s32[]{:S(2)}) async-start(), calls=%async_computation.4 | async-start | bytes 2359296 | tf_op jit(solution)/shard_map/all_gather | solution.py:439
  9.6 20.2 %all-to-all-start = ((s32[32,1,128]{2,1,0:T(1,128)}), s32[32,1,128]{2,1,0:T(1,128)S(1)}, u32[]{:S(2)}, u32[]{:S(2)}) async-start(s32[32,1,128]{2,1,0:T(1,128)} %broadcast_in_dim.49), calls=%async_computation | async-start | bytes 32768 | tf_op jit(solution)/shard_map/all_to_all | solution.py:425
  21.3 18.1 %collective-permute-start.2 = (bf16[256,512]{1,0:T(8,128)(2,1)}, bf16[256,512]{1,0:T(8,128)(2,1)S(1)}, u32[]{:S(2)}, u32[]{:S(2)}) collective-permute-start(bf16[256,512]{1,0:T(8,128)(2,1)} %tok.1), channel_id=1, source_target_pairs={{0,6},{1,7},{2,0},{3,1},{4,2},{5,3},{6,4},{7,5},{8,14},{9,15},{10,... | collective-permute-start | bytes 786440 | tf_op jit(solution)/shard_map/ppermute | solution.py:55
  24.1 15.2 %collective-permute-start.1 = (bf16[256,512]{1,0:T(8,128)(2,1)}, bf16[256,512]{1,0:T(8,128)(2,1)S(1)}, u32[]{:S(2)}, u32[]{:S(2)}) collective-permute-start(bf16[256,512]{1,0:T(8,128)(2,1)} %tok.1), channel_id=1, source_target_pairs={{0,4},{1,5},{2,6},{3,7},{4,0},{5,1},{6,2},{7,3},{8,12},{9,13},{10,... | collective-permute-start | bytes 786440 | tf_op jit(solution)/shard_map/ppermute | solution.py:55
  24.9 19.4 %collective-permute-start = (bf16[256,512]{1,0:T(8,128)(2,1)}, bf16[256,512]{1,0:T(8,128)(2,1)S(1)}, u32[]{:S(2)}, u32[]{:S(2)}) collective-permute-start(bf16[256,512]{1,0:T(8,128)(2,1)} %tok.1), channel_id=1, source_target_pairs={{0,2},{1,3},{2,4},{3,5},{4,6},{5,7},{6,0},{7,1},{8,10},{9,11},{10,... | collective-permute-start | bytes 786440 | tf_op jit(solution)/shard_map/ppermute | solution.py:55
  26.5 6.1 %copy-start.1 = (f32[1,1,896]{2,1,0:T(1,128)}, f32[1,1,896]{2,1,0:T(1,128)S(1)}, u32[]{:S(2)}) copy-start(f32[1,1,896]{2,1,0:T(1,128)S(1)} %reshape.91.gain) | copy-start | bytes 10756
  29.7 0.9 copy-start.10
  30.7 13.6 %copy-start = (bf16[256,512]{1,0:T(8,128)(2,1)S(1)}, bf16[256,512]{1,0:T(8,128)(2,1)}, u32[]{:S(2)}) copy-start(bf16[256,512]{1,0:T(8,128)(2,1)} %tok.1) | copy-start | bytes 786436
  32.6 12.8 %copy-start.13 = (f32[4096]{0:T(1024)S(1)}, f32[4096]{0:T(1024)}, u32[]{:S(2)}) copy-start(f32[4096]{0:T(1024)} %param.13) | copy-start | bytes 49156
  32.6 30.6 %all-to-all-start.1 = ((bf16[32,16,896]{2,1,0:T(8,128)(2,1)}), bf16[32,16,896]{2,1,0:T(8,128)(2,1)S(1)}, u32[]{:S(2)}, u32[]{:S(2)}) async-start(bf16[32,16,896]{2,1,0:T(8,128)(2,1)} %outgoing_rows.1), calls=%async_computation.1 | async-start | bytes 1835008 | tf_op jit(solution)/shard_map/all_to_all | solution.py:437
  39.3 97.2 %reduce-scatter.2.cloned.1.call-start = ((), (), s32[]{:S(2)}) async-start(), calls=%async_computation.5 | async-start | bytes 2359296 | tf_op jit(solution)/shard_map/reduce_scatter | solution.py:449
  45.4 2.9 %collective-permute-start.3 = (bf16[4,256,512]{2,1,0:T(8,128)(2,1)}, bf16[4,256,512]{2,1,0:T(8,128)(2,1)S(1)}, u32[]{:S(2)}, u32[]{:S(2)}) collective-permute-start(bf16[4,256,512]{2,1,0:T(8,128)(2,1)} %pad_maximum_fusion), channel_id=1, source_target_pairs={{0,1},{1,0},{2,3},{3,2},{4,5},{5,4},{6,7},{7,6},{8,9},{9,8},{10,11... | collective-permute-start | bytes 3145736 | tf_op jit(solution)/shard_map/ppermute | solution.py:59
  48.3 2.2 %copy-start.3 = (bf16[4096,512]{1,0:T(8,128)(2,1)S(1)}, bf16[4096,512]{1,0:T(8,128)(2,1)}, u32[]{:S(2)}) copy-start(bf16[4096,512]{1,0:T(8,128)(2,1)} %r_7_.1) | copy-start | bytes 12582916
  54.2 2.2 %copy-start.4 = (bf16[512,4096]{1,0:T(8,128)(2,1)S(1)}, bf16[512,4096]{1,0:T(8,128)(2,1)}, u32[]{:S(2)}) copy-start(bf16[512,4096]{1,0:T(8,128)(2,1)} %r_1_.5) | copy-start | bytes 12582916
  56.4 1.6 %copy-start.6 = (bf16[256,4096]{1,0:T(8,128)(2,1)S(1)}, bf16[256,4096]{1,0:T(8,128)(2,1)}, u32[]{:S(2)}) copy-start(bf16[256,4096]{1,0:T(8,128)(2,1)} %all-gather.2.cloned.1.call-done.r_0_) | copy-start | bytes 6291460
  60.7 20.1 %copy-start.7 = (bf16[896,512]{1,0:T(8,128)(2,1)S(1)}, bf16[896,512]{1,0:T(8,128)(2,1)}, u32[]{:S(2)}) copy-start(bf16[896,512]{1,0:T(8,128)(2,1)} %r_8_.1) | copy-start | bytes 2752516
  63.2 17.6 %copy-start.8 = (bf16[896,512]{1,0:T(8,128)(2,1)S(1)}, bf16[896,512]{1,0:T(8,128)(2,1)}, u32[]{:S(2)}) copy-start(bf16[896,512]{1,0:T(8,128)(2,1)} %r_9_.1) | copy-start | bytes 2752516
  64.1 10.6 %collective-permute-start.6 = (bf16[128,896]{1,0:T(8,128)(2,1)S(1)}, bf16[128,896]{1,0:T(8,128)(2,1)S(1)}, u32[]{:S(2)}, u32[]{:S(2)}) collective-permute-start(bf16[128,896]{1,0:T(8,128)(2,1)S(1)} %bitcast.31), channel_id=1, source_target_pairs={{0,6},{1,7},{2,0},{3,1},{4,2},{5,3},{6,4},{7,5},{8,14},{9,15},{10,... | collective-permute-start | bytes 688136 | tf_op jit(solution)/shard_map/ppermute | solution.py:55
  66.6 9.5 %collective-permute-start.5 = (bf16[128,896]{1,0:T(8,128)(2,1)S(1)}, bf16[128,896]{1,0:T(8,128)(2,1)S(1)}, u32[]{:S(2)}, u32[]{:S(2)}) collective-permute-start(bf16[128,896]{1,0:T(8,128)(2,1)S(1)} %bitcast.32), channel_id=1, source_target_pairs={{0,4},{1,5},{2,6},{3,7},{4,0},{5,1},{6,2},{7,3},{8,12},{9,13},{10,... | collective-permute-start | bytes 688136 | tf_op jit(solution)/shard_map/ppermute | solution.py:55
  68.1 10.1 %collective-permute-start.4 = (bf16[128,896]{1,0:T(8,128)(2,1)S(1)}, bf16[128,896]{1,0:T(8,128)(2,1)S(1)}, u32[]{:S(2)}, u32[]{:S(2)}) collective-permute-start(bf16[128,896]{1,0:T(8,128)(2,1)S(1)} %bitcast.33), channel_id=1, source_target_pairs={{0,2},{1,3},{2,4},{3,5},{4,6},{5,7},{6,0},{7,1},{8,10},{9,11},{10,... | collective-permute-start | bytes 688136 | tf_op jit(solution)/shard_map/ppermute | solution.py:55
  78.2 2.6 %collective-permute-start.8 = (bf16[3,128,896]{2,1,0:T(8,128)(2,1)S(1)}, bf16[3,128,896]{2,1,0:T(8,128)(2,1)S(1)}, u32[]{:S(2)}, u32[]{:S(2)}) collective-permute-start(bf16[3,128,896]{2,1,0:T(8,128)(2,1)S(1)} %pad_maximum_fusion.1), channel_id=1, source_target_pairs={{0,1},{1,0},{2,3},{3,2},{4,5},{5,4},{6,7},{7,6},{8,9},{9,8},{10,11... | collective-permute-start | bytes 2064392 | tf_op jit(solution)/shard_map/ppermute | solution.py:59
  78.3 2.5 %collective-permute-start.7 = (bf16[128,896]{1,0:T(8,128)(2,1)S(1)}, bf16[128,896]{1,0:T(8,128)(2,1)S(1)}, u32[]{:S(2)}, u32[]{:S(2)}) collective-permute-start(bf16[128,896]{1,0:T(8,128)(2,1)S(1)} %bitcast.34), channel_id=1, source_target_pairs={{0,1},{1,0},{2,3},{3,2},{4,5},{5,4},{6,7},{7,6},{8,9},{9,8},{10,11... | collective-permute-start | bytes 688136 | tf_op jit(solution)/shard_map/ppermute | solution.py:59
  80.8 8.0 %copy-start.5 = (bf16[512,4096]{1,0:T(8,128)(2,1)S(1)}, bf16[512,4096]{1,0:T(8,128)(2,1)}, u32[]{:S(2)}) copy-start(bf16[512,4096]{1,0:T(8,128)(2,1)} %r_1_.5) | copy-start | bytes 12582916
  88.7 4.9 %collective-permute-start.9 = (bf16[4,128,896]{2,1,0:T(8,128)(2,1)}, bf16[4,128,896]{2,1,0:T(8,128)(2,1)S(1)}, u32[]{:S(2)}, u32[]{:S(2)}) collective-permute-start(bf16[4,128,896]{2,1,0:T(8,128)(2,1)} %get-tuple-element.17), channel_id=1, source_target_pairs={{0,1},{1,0},{2,3},{3,2},{4,5},{5,4},{6,7},{7,6},{8,9},{9,8},{10,11... | collective-permute-start | bytes 2752520 | tf_op jit(solution)/shard_map/ppermute | solution.py:59
  93.8 14.1 %collective-permute-start.16 = (bf16[128,896]{1,0:T(8,128)(2,1)S(1)}, bf16[128,896]{1,0:T(8,128)(2,1)S(1)}, u32[]{:S(2)}, u32[]{:S(2)}) collective-permute-start(bf16[128,896]{1,0:T(8,128)(2,1)S(1)} %get-tuple-element.25), channel_id=1, source_target_pairs={{0,2},{1,3},{2,4},{3,5},{4,6},{5,7},{6,0},{7,1},{8,10},{9,11},{10,... | collective-permute-start | bytes 688136 | tf_op jit(solution)/shard_map/ppermute | solution.py:68
  93.9 14.0 %collective-permute-start.15 = (bf16[128,896]{1,0:T(8,128)(2,1)S(1)}, bf16[128,896]{1,0:T(8,128)(2,1)S(1)}, u32[]{:S(2)}, u32[]{:S(2)}) collective-permute-start(bf16[128,896]{1,0:T(8,128)(2,1)S(1)} %get-tuple-element.26), channel_id=1, source_target_pairs={{0,4},{1,5},{2,6},{3,7},{4,0},{5,1},{6,2},{7,3},{8,12},{9,13},{10,... | collective-permute-start | bytes 688136 | tf_op jit(solution)/shard_map/ppermute | solution.py:68
  96.3 12.3 %collective-permute-start.14 = (bf16[128,896]{1,0:T(8,128)(2,1)S(1)}, bf16[128,896]{1,0:T(8,128)(2,1)S(1)}, u32[]{:S(2)}, u32[]{:S(2)}) collective-permute-start(bf16[128,896]{1,0:T(8,128)(2,1)S(1)} %get-tuple-element.27), channel_id=1, source_target_pairs={{0,6},{1,7},{2,0},{3,1},{4,2},{5,3},{6,4},{7,5},{8,14},{9,15},{10,... | collective-permute-start | bytes 688136 | tf_op jit(solution)/shard_map/ppermute | solution.py:68
  110.3 34.4 %all-to-all-start.2 = ((bf16[32,16,896]{2,1,0:T(8,128)(2,1)}), bf16[32,16,896]{2,1,0:T(8,128)(2,1)S(1)}, u32[]{:S(2)}, u32[]{:S(2)}) async-start(bf16[32,16,896]{2,1,0:T(8,128)(2,1)} %placed_grads.1), calls=%async_computation.3 | async-start | bytes 1835008 | tf_op jit(solution)/shard_map/all_to_all | solution.py:451
  120.0 24.7 %copy-start.2 = (f32[1,1,896]{2,1,0:T(1,128)S(1)}, f32[1,1,896]{2,1,0:T(1,128)}, u32[]{:S(2)}) copy-start(f32[1,1,896]{2,1,0:T(1,128)} %copy-done.1) | copy-start | bytes 10756
  136.5 0.9 copy-start.9
  137.5 1.0 copy-start.15
  137.5 7.2 %copy-start.11 = (bf16[8,16,896]{2,1,0:T(8,128)(2,1)S(1)}, bf16[8,16,896]{2,1,0:T(8,128)(2,1)}, u32[]{:S(2)}) copy-start(bf16[8,16,896]{2,1,0:T(8,128)(2,1)} %enc.3) | copy-start | bytes 688132
  138.4 1.2 collective-permute-start.10
  139.6 7.1 %copy-start.12 = (bf16[256,512]{1,0:T(8,128)(2,1)S(1)}, bf16[256,512]{1,0:T(8,128)(2,1)}, u32[]{:S(2)}) copy-start(bf16[256,512]{1,0:T(8,128)(2,1)} %get-tuple-element.10) | copy-start | bytes 786436
  139.6 7.1 %copy-start.14 = (f32[512]{0:T(512)S(1)}, f32[512]{0:T(512)}, u32[]{:S(2)}) copy-start(f32[512]{0:T(512)} %dynamic_slice.3) | copy-start | bytes 6148
  139.6 7.0 %collective-permute-start.13 = (f32[256]{0:T(256)S(1)}, f32[256]{0:T(256)S(1)}, u32[]{:S(2)}, u32[]{:S(2)}) collective-permute-start(f32[256]{0:T(256)S(1)} %add.64), channel_id=1, source_target_pairs={{0,6},{1,7},{2,0},{3,1},{4,2},{5,3},{6,4},{7,5},{8,14},{9,15},{10,... | collective-permute-start | bytes 3080 | tf_op jit(solution)/shard_map/ppermute | solution.py:459
  140.2 6.4 %collective-permute-start.12 = (f32[256]{0:T(256)S(1)}, f32[256]{0:T(256)S(1)}, u32[]{:S(2)}, u32[]{:S(2)}) collective-permute-start(f32[256]{0:T(256)S(1)} %add.64), channel_id=1, source_target_pairs={{0,4},{1,5},{2,6},{3,7},{4,0},{5,1},{6,2},{7,3},{8,12},{9,13},{10,... | collective-permute-start | bytes 3080 | tf_op jit(solution)/shard_map/ppermute | solution.py:459
  140.2 6.4 %collective-permute-start.11 = (f32[256]{0:T(256)S(1)}, f32[256]{0:T(256)S(1)}, u32[]{:S(2)}, u32[]{:S(2)}) collective-permute-start(f32[256]{0:T(256)S(1)} %add.64), channel_id=1, source_target_pairs={{0,2},{1,3},{2,4},{3,5},{4,6},{5,7},{6,0},{7,1},{8,10},{9,11},{10,... | collective-permute-start | bytes 3080 | tf_op jit(solution)/shard_map/ppermute | solution.py:459
Sparse Core Ops, SparseCore 0:
  9.8 38.7 all-gather.1
  99.3 37.1 reduce-scatter.1

commit v3 on v1

--- a/solution.py
+++ b/solution.py
@@ -15,16 +15,16 @@
 BF16 = jnp.bfloat16
 IDS_WIDTH = 128
 GROUP = 8
-MIX_COST = 100
-VMEM_LIMIT = 48 * 1024 * 1024
+MIX_COST = 1
+MIB = 1024 * 1024
 
 
 def rms_scale(values):
     return lax.rsqrt(jnp.mean(values * values, axis=-1, keepdims=True) + EPS)
 
 
-def params():
-    return pltpu.CompilerParams(vmem_limit_bytes=VMEM_LIMIT)
+def params(mib=8):
+    return pltpu.CompilerParams(vmem_limit_bytes=mib * MIB)
 
 
 def cost(micros):
@@ -36,7 +36,7 @@
 
 
 def hbm():
-    return pl.BlockSpec(memory_space=pl.ANY)
+    return pl.BlockSpec(memory_space=pltpu.HBM)
 
 
 def smem():
@@ -59,8 +59,21 @@
     return lax.ppermute(x, "mp", core_swap(count))
 
 
-def pair_sum(send, keep, count):
-    return (keep.astype(F32) + swap(send, count).astype(F32)).astype(BF16)
+def pair_kernel(keep, other, *outs):
+    for k, out in enumerate(outs):
+        out[...] = (keep[k].astype(F32) + other[k].astype(F32)).astype(BF16)
+
+
+def pair_sum(keep, other):
+    return pl.pallas_call(
+        pair_kernel,
+        out_shape=[jax.ShapeDtypeStruct(keep.shape[1:], BF16)] * keep.shape[0],
+        in_specs=[vmem(), vmem()],
+        out_specs=[vmem()] * keep.shape[0],
+        compiler_params=params(12),
+        cost_estimate=cost(0.7),
+        name="pair_sums",
+    )(keep, other)
 
 
 def pair_shares(pair, count):
@@ -127,15 +140,15 @@
         in_specs=[smem()] + [vmem()] * (len(pieces) + 1) + [hbm()],
         out_specs=vmem(),
         scratch_shapes=[pltpu.VMEM((count, share, cols), BF16), pltpu.SemaphoreType.DMA((count,))],
-        compiler_params=params(),
-        cost_estimate=cost(2.25),
+        compiler_params=params(20),
+        cost_estimate=cost(4.5),
         name="queries",
     )(src, *pieces, gain.reshape(count, share), w_query)
 
 
 def back_kernel(count, src, *refs):
-    pieces, rest = views(count, refs)
-    w_hbm, out, w_buf, sems = rest
+    pieces = refs[:count]
+    w_hbm, out, w_buf, sems = refs[count:]
     share = pieces[0].shape[1]
     copies = []
     for k in range(count):
@@ -151,7 +164,7 @@
 
 
 def run_back(src, pieces, w_out):
-    count = 2 * (len(pieces) - 1)
+    count = len(pieces)
     rows, share = pieces[0].shape
     cols = w_out.shape[0]
     return pl.pallas_call(
@@ -160,8 +173,8 @@
         in_specs=[smem()] + [vmem()] * len(pieces) + [hbm()],
         out_specs=vmem(),
         scratch_shapes=[pltpu.VMEM((count, cols, share), BF16), pltpu.SemaphoreType.DMA((count,))],
-        compiler_params=params(),
-        cost_estimate=cost(2.25),
+        compiler_params=params(20),
+        cost_estimate=cost(4.5),
         name="d_attended",
     )(src, *pieces, w_out)
 
@@ -193,7 +206,7 @@
         in_specs=[smem(), vmem(), hbm()],
         out_specs=(vmem(), vmem()),
         scratch_shapes=[pltpu.VMEM((count, cols, share), BF16), pltpu.SemaphoreType.DMA((count,))],
-        compiler_params=params(),
+        compiler_params=params(20),
         cost_estimate=cost(4),
         name="branches",
     )(src, att, w_out)
@@ -201,8 +214,8 @@
 
 def attention_kernel(count, blocks, *refs):
     half = count // 2
-    pieces = list(refs[:half]) + [refs[half].at[0]] + [refs[half + 1].at[k] for k in range(half - 1)]
-    q_ref, d_ref, wk, wv, send, keep, att, mem, keys, values, k_grad, v_grad = refs[half + 2 :]
+    pieces = refs[:count]
+    q_ref, d_ref, wk, wv, send, keep, att, mem, keys, values, k_grad, v_grad = refs[count:]
     heads = q_ref.shape[1] // HD
     part = send.shape[1] // blocks
     span = part * count
@@ -254,7 +267,7 @@
 
 
 def run_attention(pieces, q, d, w_key, w_value, blocks):
-    count = 2 * (len(pieces) - 2)
+    count = len(pieces)
     rows, width = pieces[0].shape
     cols = q.shape[1]
     total = rows * count
@@ -266,7 +279,7 @@
         out_specs=(vmem(), vmem(), vmem()),
         scratch_shapes=[pltpu.VMEM((total, width), BF16)]
         + [pltpu.VMEM((total, cols), BF16)] * 4,
-        compiler_params=params(),
+        compiler_params=params(24),
         cost_estimate=cost(9),
         name="attention",
     )(*pieces, q, d, w_key, w_value)
@@ -287,7 +300,7 @@
         in_specs=[smem(), vmem(), vmem()],
         out_specs=vmem(),
         scratch_shapes=[pltpu.VMEM(encodings.shape, BF16)],
-        compiler_params=params(),
+        compiler_params=params(12),
         cost_estimate=cost(1.7),
         name="outgoing_rows",
     )(requested, encodings, gain.reshape(1, 1, -1))
@@ -312,7 +325,7 @@
         out_specs=vmem(),
         scratch_shapes=[pltpu.SemaphoreType.DMA((n,))],
         compiler_params=params(),
-        cost_estimate=cost(2.25),
+        cost_estimate=cost(4.5),
         name="picked_rows",
     )(owner, rows)
 
@@ -333,7 +346,7 @@
         in_specs=[smem()] + [vmem()] * len(parts),
         out_specs=vmem(),
         scratch_shapes=[pltpu.VMEM(shape, BF16)],
-        compiler_params=params(),
+        compiler_params=params(12),
         cost_estimate=cost(1.7),
         name="placed_grads",
     )(reading, *parts)
@@ -357,7 +370,7 @@
         ),
         in_specs=[vmem()] * (len(parts) + 1),
         out_specs=(vmem(), vmem()),
-        compiler_params=params(),
+        compiler_params=params(12),
         cost_estimate=cost(MIX_COST),
         name="mixed",
     )(tokens, *parts)
@@ -386,7 +399,7 @@
         in_specs=[smem(), hbm(), vmem(), vmem()],
         out_specs=vmem(),
         scratch_shapes=[pltpu.VMEM(encodings.shape, BF16), pltpu.SemaphoreType.DMA((rows,))],
-        compiler_params=params(),
+        compiler_params=params(12),
         cost_estimate=cost(1.9),
         name="d_encodings",
     )(slot, back, encodings, gain.reshape(1, 1, -1))
@@ -442,25 +455,28 @@
     incoming = lax.all_to_all(outgoing, "dp", split_axis=0, concat_axis=0, tiled=True)
     cot_own = over_chips(cot_in, count)
     q = run_query(src, tok_own + [swap(jnp.stack(tok_own), count)], gain_dec, w_query)
-    d = run_back(src, cot_own + [swap(jnp.stack(cot_own), count)], w_out)
+    d = run_back(src, cot_own + [swap(p, count) for p in cot_own], w_out)
     incoming, q, d = lax.optimization_barrier((incoming, q, d))
     picked = run_pick(owner, incoming).reshape(readings * own_tokens, width)
     row_own = over_chips(picked, count)
-    rows = row_own + [swap(picked, count)[None], swap(jnp.stack(row_own[1:]), count)]
+    rows = row_own + [swap(p, count) for p in row_own]
     send, keep, att = run_attention(rows, q, d, w_key, w_value, blocks)
-    pair = pair_sum(send, keep, count)
+    pair = pair_sum(keep, swap(send, count))
+    att, pair = lax.optimization_barrier((att, pair))
     parts = pair_shares(pair, count)
     b_send, b_keep = run_branch(src, att, w_out, count)
-    b_pair = pair_sum(b_send, b_keep, count)
-    parts, b_pair = lax.optimization_barrier((parts, b_pair))
-    b_parts = pair_shares(b_pair, count)
+    b_send, parts = lax.optimization_barrier((b_send, parts))
+    b_parts = pair_shares(pair_sum(b_keep, swap(b_send, count)), count)
     back_out = run_place(reading, [p.reshape(readings, own_tokens, width) for p in parts])
     back_in = lax.all_to_all(back_out, "dp", split_axis=0, concat_axis=0, tiled=True)
 
     mixed, squares = run_mix(tokens, b_parts)
     mixed_wide = mixed.astype(F32)
     squares = squares[:, 0]
-    total = jnp.sum(lax.all_gather(squares, "mp", axis=0), axis=0)
+    squares = squares + swap(squares, count)
+    total = squares
+    for k in range(1, half):
+        total = total + lax.ppermute(squares, "mp", chip_shift(count, k))
     post = lax.rsqrt(total / (share_cols * count) + EPS)[:, None]
     gain_here = lax.dynamic_slice_in_dim(gain_post, here * share_cols, share_cols, 0)
     ffn = (mixed_wide * post * gain_here).astype(BF16)

time: 152 us -> 148 us (0.974); the launches traced: 150 us -> 148 us
  waiting for transfers between devices: 43.3 us -> 58.5 us
  blocking collectives: 14 us -> 0 us
  local copies, waits for them, and re-layouts: 5.19 us -> 9.23 us
  other arithmetic: 6.78 us -> 3.34 us
  Pallas kernels: 30.4 us -> 27.8 us
    all_gather x1 -> x0, blocking collectives: 14 us -> none  [shards(): total = jnp.sum(lax.all_gather(squares, 'mp', axis=0), axis=0)]
    ppermute x6, waiting for transfers between devices: 12.7 us -> 19.6 us  [pair_shares(): lax.ppermute(pair[k], 'mp', chip_shift(count, -k))]
    all_to_all x1, waiting for transfers between devices: 6.72 us -> 0.01 us  [shards(): lax.all_to_all(back_out, 'dp', split_axis=0, concat_axis=0, tiled=True)]
    ppermute x9, waiting for transfers between devices: 19.9 us -> 25.2 us  [over_chips(): lax.ppermute(x, 'mp', chip_shift(count, k))]
    ppermute x6 -> x12, waiting for transfers between devices: 1.98 us -> 6.58 us  [swap(): return lax.ppermute(x, 'mp', core_swap(count))]
    unnamed x19 -> x29, local copies, waits for them, and re-layouts: 2.69 us -> 6.88 us
    ppermute x0 -> x3, waiting for transfers between devices: none -> 3.85 us  [shards(): total = total + lax.ppermute(squares, 'mp', chip_shift(count, k))]
    convert_element_type x2 -> x0, other arithmetic: 2.91 us -> none  [pair_sum(): return (keep.astype(F32) + swap(send, count).astype(F32)).astype(BF16)]
  transfers between devices with their start and end apart: 24 -> 33, of which waited for: 10 -> 19; matrix products, arithmetic and copies ran while one was open for 5% -> 3% of each run, Pallas kernels for 12% -> 12%
where the time goes in v3:
time: 148 us
  waiting for transfers between devices  58.5 us (40%)
  starting transfers between devices  47.9 us (32%)
  Pallas kernels  27.8 us (19%)
  local copies, waits for them, and re-layouts  9.23 us (6%)
  other arithmetic  3.34 us (2%)
    ppermute x9, waiting for transfers between devices, over_chips(): lax.ppermute(x, 'mp', chip_shift(count, k))  25.2 us
    ppermute x6, waiting for transfers between devices, pair_shares(): lax.ppermute(pair[k], 'mp', chip_shift(count, -k))  19.6 us
    all_to_all x1, starting transfers between devices, shards(): lax.all_to_all(jnp.broadcast_to(wanted[:, None], (dp_count, IDS_WIDTH)),...  11.7 us
    ppermute x9, starting transfers between devices, over_chips(): lax.ppermute(x, 'mp', chip_shift(count, k))  11.4 us
    all_to_all x1, starting transfers between devices, shards(): lax.all_to_all(back_out, 'dp', split_axis=0, concat_axis=0, tiled=True)  9.78 us
    pallas_call x1, Pallas kernels, run_attention(): pl.pallas_call(lambda *r: attention_kernel(count, blocks, *r), out_shape=...  6.92 us
    unnamed x29, local copies, waits for them, and re-layouts  6.88 us
    ppermute x12, waiting for transfers between devices, swap(): return lax.ppermute(x, 'mp', core_swap(count))  6.58 us
  transfers between devices with their start and end apart: 33, of which 19 were waited for; matrix products, arithmetic and copies ran while one was open for 3% of the time, Pallas kernels for 12%

profile of v3, /device:TPU:8, one launch (start us, length us, event | category | flops | bytes accessed | tf_op | source)
XLA Modules:
  0.0 147.9 jit_solution(1883686122569425683)
XLA Ops:
  0.6 0.8 copy.17
  1.6 0.7 broadcast_in_dim.46
  2.3 11.7 %all-to-all-start = ((s32[32,1,128]{2,1,0:T(1,128)}), s32[32,1,128]{2,1,0:T(1,128)S(1)}, u32[]{:S(2)}, u32[]{:S(2)}) async-start(s32[32,1,128]{2,1,0:T(1,128)} %broadcast_in_dim.46), calls=%async_computation | async-start | bytes 32768 | tf_op jit(solution)/shard_map/all_to_all | solution.py:442
  14.0 2.8 %collective-permute-start.2 = (bf16[256,512]{1,0:T(8,128)(2,1)}, bf16[256,512]{1,0:T(8,128)(2,1)S(1)}, u32[]{:S(2)}, u32[]{:S(2)}) collective-permute-start(bf16[256,512]{1,0:T(8,128)(2,1)} %tok.1), channel_id=1, source_target_pairs={{0,6},{1,7},{2,0},{3,1},{4,2},{5,3},{6,4},{7,5},{8,14},{9,15},{10,... | collective-permute-start | bytes 786440 | tf_op jit(solution)/shard_map/ppermute | solution.py:55
  16.8 0.8 collective-permute-start.1
  17.6 0.9 collective-permute-start
  18.5 0.7 reshape.94.gain
  19.2 3.2 %all-to-all-done = s32[32,1,128]{2,1,0:T(1,128)S(1)} async-done(((s32[32,1,128]{2,1,0:T(1,128)}), s32[32,1,128]{2,1,0:T(1,128)S(1)}, u32[]{:S(2)}, u32[]{:S(2)}) %all-to-all-start) | async-done | bytes 16416 | tf_op jit(solution)/shard_map/all_to_all | solution.py:442
  22.5 0.9 copy-done.7
  23.4 1.9 %outgoing_rows.1 = bf16[32,16,896]{2,1,0:T(8,128)(2,1)} custom-call(s32[32,128]{1,0:T(8,128)S(1)} %bitcast.14, bf16[8,16,896]{2,1,0:T(8,128)(2,1)S(1)} %copy-done.7, f32[1,1,896]{2,1,0:T(1,128)S(1)} %reshape.94.gain), custom_call_target="tpu_custom_call" | custom-call | flops 1870000000 | tf_op jit(solution)/shard_map/outgoing_rows/pallas_call | solution.py:297
  25.3 6.5 %all-to-all-start.1 = ((bf16[32,16,896]{2,1,0:T(8,128)(2,1)}), bf16[32,16,896]{2,1,0:T(8,128)(2,1)S(1)}, u32[]{:S(2)}, u32[]{:S(2)}) async-start(bf16[32,16,896]{2,1,0:T(8,128)(2,1)} %outgoing_rows.1), calls=%async_computation.1 | async-start | bytes 1835008 | tf_op jit(solution)/shard_map/all_to_all | solution.py:455
  31.9 1.1 pad_maximum_fusion
  33.1 2.4 %collective-permute-start.6 = (bf16[256,512]{1,0:T(8,128)(2,1)S(1)}, bf16[256,512]{1,0:T(8,128)(2,1)}, u32[]{:S(2)}, u32[]{:S(2)}) collective-permute-start(bf16[256,512]{1,0:T(8,128)(2,1)S(1)} %copy-done.6), channel_id=1, source_target_pairs={{0,6},{1,7},{2,0},{3,1},{4,2},{5,3},{6,4},{7,5},{8,14},{9,15},{10,... | collective-permute-start | bytes 786440 | tf_op jit(solution)/shard_map/ppermute | solution.py:55
  35.4 1.5 %collective-permute-start.5 = (bf16[256,512]{1,0:T(8,128)(2,1)S(1)}, bf16[256,512]{1,0:T(8,128)(2,1)}, u32[]{:S(2)}, u32[]{:S(2)}) collective-permute-start(bf16[256,512]{1,0:T(8,128)(2,1)S(1)} %copy-done.6), channel_id=1, source_target_pairs={{0,4},{1,5},{2,6},{3,7},{4,0},{5,1},{6,2},{7,3},{8,12},{9,13},{10,... | collective-permute-start | bytes 786440 | tf_op jit(solution)/shard_map/ppermute | solution.py:55
  36.9 10.4 %collective-permute-done.6.r_4_ = bf16[256,512]{1,0:T(8,128)(2,1)} collective-permute-done((bf16[256,512]{1,0:T(8,128)(2,1)S(1)}, bf16[256,512]{1,0:T(8,128)(2,1)}, u32[]{:S(2)}, u32[]{:S(2)}) %collective-permute-start.6) | collective-permute-done | bytes 262176 | tf_op jit(solution)/shard_map/ppermute | solution.py:55
  47.3 0.5 collective-permute-start.9
  47.8 3.3 %collective-permute-done.4.r_2_ = bf16[256,512]{1,0:T(8,128)(2,1)} collective-permute-done((bf16[256,512]{1,0:T(8,128)(2,1)S(1)}, bf16[256,512]{1,0:T(8,128)(2,1)}, u32[]{:S(2)}, u32[]{:S(2)}) %collective-permute-start.4) | collective-permute-done | bytes 262176 | tf_op jit(solution)/shard_map/ppermute | solution.py:55
  51.2 1.7 %collective-permute-done.8.r_6_ = bf16[256,512]{1,0:T(8,128)(2,1)} collective-permute-done((bf16[256,512]{1,0:T(8,128)(2,1)}, bf16[256,512]{1,0:T(8,128)(2,1)}, u32[]{:S(2)}, u32[]{:S(2)}) %collective-permute-start.8) | collective-permute-done | bytes 262176 | tf_op jit(solution)/shard_map/ppermute | solution.py:59
  53.0 2.2 %copy-done.2 = bf16[512,4096]{1,0:T(8,128)(2,1)S(1)} copy-done((bf16[512,4096]{1,0:T(8,128)(2,1)S(1)}, bf16[512,4096]{1,0:T(8,128)(2,1)}, u32[]{:S(2)}) %copy-start.2) | copy-done | bytes 4194328
  55.1 4.1 %d_attended.1.r_9_ = bf16[256,512]{1,0:T(8,128)(2,1)S(1)} custom-call(s32[8]{0:T(128)S(1)} %pad_add_fusion.r_0_, bf16[256,512]{1,0:T(8,128)(2,1)S(1)} %copy-done.6, bf16[256,512]{1,0:T(8,128)(2,1)} %collective-permute-done.4.r_2_, bf16[256,512]{1,0:T(8,128)(2,1)} %collective-permute-done.5.r_3_, bf16[256,512]{1,0:T(8,128)(2,1)} %collective-permute-done.6.r_4_, ...), custom_call_target="tpu_custom_call" | custom-call | flops 4950000128 | tf_op jit(solution)/shard_map/d_attended/pallas_call | solution.py:170
  59.3 0.7 copy-done.11
  60.0 3.7 %queries.1.r_8_ = bf16[256,512]{1,0:T(8,128)(2,1)S(1)} custom-call(s32[8]{0:T(128)S(1)} %pad_add_fusion.r_0_, bf16[256,512]{1,0:T(8,128)(2,1)S(1)} %copy-done, bf16[256,512]{1,0:T(8,128)(2,1)S(1)} %collective-permute-done.r_2_, bf16[256,512]{1,0:T(8,128)(2,1)S(1)} %collective-permute-done.1.r_3_, bf16[256,512]{1,0:T(8,128)(2,1)S(1)} %collective-permute-done.2.r_4_, ...), custom_call_target="tpu_custom_call" | custom-call | flops 4950000128 | tf_op jit(solution)/shard_map/queries/pallas_call | solution.py:137
  63.7 1.0 picked_rows.1
  64.7 0.8 collective-permute-start.13
  65.5 1.4 collective-permute-start.12
  66.9 0.8 collective-permute-start.11
  67.7 5.5 %collective-permute-done.13.r_3_ = bf16[128,896]{1,0:T(8,128)(2,1)S(1)} collective-permute-done((bf16[128,896]{1,0:T(8,128)(2,1)S(1)}, bf16[128,896]{1,0:T(8,128)(2,1)S(1)}, u32[]{:S(2)}, u32[]{:S(2)}) %collective-permute-start.13) | collective-permute-done | bytes 229408 | tf_op jit(solution)/shard_map/ppermute | solution.py:55
  73.2 2.3 %collective-permute-done.12.r_2_ = bf16[128,896]{1,0:T(8,128)(2,1)S(1)} collective-permute-done((bf16[128,896]{1,0:T(8,128)(2,1)S(1)}, bf16[128,896]{1,0:T(8,128)(2,1)S(1)}, u32[]{:S(2)}, u32[]{:S(2)}) %collective-permute-start.12) | collective-permute-done | bytes 229408 | tf_op jit(solution)/shard_map/ppermute | solution.py:55
  75.5 3.8 %collective-permute-done.11.r_1_ = bf16[128,896]{1,0:T(8,128)(2,1)S(1)} collective-permute-done((bf16[128,896]{1,0:T(8,128)(2,1)S(1)}, bf16[128,896]{1,0:T(8,128)(2,1)S(1)}, u32[]{:S(2)}, u32[]{:S(2)}) %collective-permute-start.11) | collective-permute-done | bytes 229408 | tf_op jit(solution)/shard_map/ppermute | solution.py:55
  79.3 1.5 collective-permute-done.15.r_5_
  80.8 6.9 %attention.1 = (bf16[4,128,896]{2,1,0:T(8,128)(2,1)S(1)}, bf16[4,128,896]{2,1,0:T(8,128)(2,1)S(1)}, bf16[256,512]{1,0:T(8,128)(2,1)S(1)}) custom-call(bf16[128,896]{1,0:T(8,128)(2,1)S(1)} %bitcast.20, bf16[128,896]{1,0:T(8,128)(2,1)S(1)} %collective-permute-done.11.r_1_, bf16[128,896]{1,0:T(8,128)(2,1)S(1)} %collective-permute-done.12.r_2_, ...), custom_call_target="tpu_custom_call" | custom-call | flops 9900000256 | tf_op jit(solution)/shard_map/attention/pallas_call | solution.py:275
  87.7 0.2 collective-permute-start.18
  87.9 2.3 %collective-permute-done.18.other = bf16[4,128,896]{2,1,0:T(8,128)(2,1)S(1)} collective-permute-done((bf16[4,128,896]{2,1,0:T(8,128)(2,1)S(1)}, bf16[4,128,896]{2,1,0:T(8,128)(2,1)S(1)}, u32[]{:S(2)}, u32[]{:S(2)}) %collective-permute-start.18) | collective-permute-done | bytes 917536 | tf_op jit(solution)/shard_map/ppermute | solution.py:59
  90.3 0.2 pair_sums.2
  90.5 1.1 collective-permute-start.19
  91.6 1.0 collective-permute-start.20
  92.6 0.8 collective-permute-start.21
  93.4 3.9 %branches.1 = (bf16[4,256,512]{2,1,0:T(8,128)(2,1)S(1)}, bf16[4,256,512]{2,1,0:T(8,128)(2,1)S(1)}) custom-call(s32[8]{0:T(128)S(1)} %pad_add_fusion.r_0_, bf16[256,512]{1,0:T(8,128)(2,1)S(1)} %get-tuple-element.45.r_1_, bf16[512,4096]{1,0:T(8,128)(2,1)S(1)} %copy-done.3), custom_call_target="tpu_custom_call" | custom-call | flops 4400000000 | tf_op jit(solution)/shard_map/branches/pallas_call | solution.py:203
  97.3 1.0 copy-done.9
  98.3 0.7 collective-permute-done.19
  99.0 2.6 %collective-permute-done.20 = bf16[128,896]{1,0:T(8,128)(2,1)S(1)} collective-permute-done((bf16[128,896]{1,0:T(8,128)(2,1)S(1)}, bf16[128,896]{1,0:T(8,128)(2,1)S(1)}, u32[]{:S(2)}, u32[]{:S(2)}) %collective-permute-start.20) | collective-permute-done | bytes 229408 | tf_op jit(solution)/shard_map/ppermute | solution.py:81
  101.6 3.8 %collective-permute-done.21 = bf16[128,896]{1,0:T(8,128)(2,1)S(1)} collective-permute-done((bf16[128,896]{1,0:T(8,128)(2,1)S(1)}, bf16[128,896]{1,0:T(8,128)(2,1)S(1)}, u32[]{:S(2)}, u32[]{:S(2)}) %collective-permute-start.21) | collective-permute-done | bytes 229408 | tf_op jit(solution)/shard_map/ppermute | solution.py:81
  105.5 1.7 %placed_grads.1 = bf16[32,16,896]{2,1,0:T(8,128)(2,1)} custom-call(s32[32]{0:T(128)S(1)} %get-tuple-element.63.reading, bf16[8,16,896]{2,1,0:T(8,128)(2,1)S(1)} %bitcast.24, bf16[8,16,896]{2,1,0:T(8,128)(2,1)S(1)} %bitcast.21, bf16[8,16,896]{2,1,0:T(8,128)(2,1)S(1)} %bitcast.22, bf16[8,16,896]{2,1,0:T(8,128)(2,1)S(1)} %bitcast.23), custom_call_target="tpu_custom_call" | custom-call | flops 1870000000 | tf_op jit(solution)/shard_map/placed_grads/pallas_call | solution.py:343
  107.2 9.8 %all-to-all-start.2 = ((bf16[32,16,896]{2,1,0:T(8,128)(2,1)}), bf16[32,16,896]{2,1,0:T(8,128)(2,1)S(1)}, u32[]{:S(2)}, u32[]{:S(2)}) async-start(bf16[32,16,896]{2,1,0:T(8,128)(2,1)} %placed_grads.1), calls=%async_computation.2 | async-start | bytes 1835008 | tf_op jit(solution)/shard_map/all_to_all | solution.py:471
  117.0 1.3 copy-done.10
  118.3 1.5 pair_sums.3
  119.8 0.7 collective-permute-start.23
  120.4 0.9 collective-permute-start.24
  121.3 0.8 collective-permute-start.25
  122.2 0.8 dynamic_slice.3
  122.9 6.1 %collective-permute-done.23.refs_1_ = bf16[256,512]{1,0:T(8,128)(2,1)S(1)} collective-permute-done((bf16[256,512]{1,0:T(8,128)(2,1)S(1)}, bf16[256,512]{1,0:T(8,128)(2,1)S(1)}, u32[]{:S(2)}, u32[]{:S(2)}) %collective-permute-start.23) | collective-permute-done | bytes 262176 | tf_op jit(solution)/shard_map/ppermute | solution.py:81
  129.0 2.2 %collective-permute-done.24.refs_2_ = bf16[256,512]{1,0:T(8,128)(2,1)S(1)} collective-permute-done((bf16[256,512]{1,0:T(8,128)(2,1)S(1)}, bf16[256,512]{1,0:T(8,128)(2,1)S(1)}, u32[]{:S(2)}, u32[]{:S(2)}) %collective-permute-start.24) | collective-permute-done | bytes 262176 | tf_op jit(solution)/shard_map/ppermute | solution.py:81
  131.2 4.2 %collective-permute-done.25.refs_3_ = bf16[256,512]{1,0:T(8,128)(2,1)S(1)} collective-permute-done((bf16[256,512]{1,0:T(8,128)(2,1)S(1)}, bf16[256,512]{1,0:T(8,128)(2,1)S(1)}, u32[]{:S(2)}, u32[]{:S(2)}) %collective-permute-start.25) | collective-permute-done | bytes 262176 | tf_op jit(solution)/shard_map/ppermute | solution.py:81
  135.4 0.9 mixed.1
  136.6 1.0 collective-permute-done.26
  137.7 0.8 collective-permute-start.29
  138.5 0.7 collective-permute-start.28
  139.2 0.8 collective-permute-start.27
  140.0 0.1 select_reduce_fusion.1.slot
  140.1 1.1 collective-permute-done.29
  141.2 2.4 %collective-permute-done.28 = f32[256]{0:T(256)S(1)} collective-permute-done((f32[256]{0:T(256)S(1)}, f32[256]{0:T(256)S(1)}, u32[]{:S(2)}, u32[]{:S(2)}) %collective-permute-start.28) | collective-permute-done | bytes 1056 | tf_op jit(solution)/shard_map/ppermute | solution.py:479
  143.6 0.4 collective-permute-done.27
  144.0 1.8 %multiply_convert_fusion = bf16[256,512]{1,0:T(8,128)(2,1)} fusion(bf16[256,512]{1,0:T(8,128)(2,1)} %get-tuple-element.30, f32[512]{0:T(512)S(1)} %dynamic_slice.3, f32[256]{0:T(256)S(1)} %add_rsqrt_fusion), kind=kLoop, calls=%fused_computation.1 | loop fusion | flops 524288 | bytes 527360 | tf_op jit(solution)/shard_map/convert_element_type | solution.py:482
  145.8 1.9 %d_encodings.1 = bf16[8,16,896]{2,1,0:T(8,128)(2,1)} custom-call(s32[8]{0:T(128)S(1)} %select_reduce_fusion.1.slot, bf16[32,16,896]{2,1,0:T(8,128)(2,1)S(1)} %all-to-all-done.2.back, bf16[8,16,896]{2,1,0:T(8,128)(2,1)S(1)} %copy-done.8, f32[1,1,896]{2,1,0:T(1,128)S(1)} %reshape.94.gain), custom_call_target="tpu_custom_call" | custom-call | flops 2090000000 | tf_op jit(solution)/shard_map/d_encodings/pallas_call | solution.py:396
  (59 shorter events, 0.8 us)
Async XLA Ops:
  2.3 20.2 %all-to-all-start = ((s32[32,1,128]{2,1,0:T(1,128)}), s32[32,1,128]{2,1,0:T(1,128)S(1)}, u32[]{:S(2)}, u32[]{:S(2)}) async-start(s32[32,1,128]{2,1,0:T(1,128)} %broadcast_in_dim.46), calls=%async_computation | async-start | bytes 32768 | tf_op jit(solution)/shard_map/all_to_all | solution.py:442
  14.0 17.9 %collective-permute-start.2 = (bf16[256,512]{1,0:T(8,128)(2,1)}, bf16[256,512]{1,0:T(8,128)(2,1)S(1)}, u32[]{:S(2)}, u32[]{:S(2)}) collective-permute-start(bf16[256,512]{1,0:T(8,128)(2,1)} %tok.1), channel_id=1, source_target_pairs={{0,6},{1,7},{2,0},{3,1},{4,2},{5,3},{6,4},{7,5},{8,14},{9,15},{10,... | collective-permute-start | bytes 786440 | tf_op jit(solution)/shard_map/ppermute | solution.py:55
  16.8 15.1 %collective-permute-start.1 = (bf16[256,512]{1,0:T(8,128)(2,1)}, bf16[256,512]{1,0:T(8,128)(2,1)S(1)}, u32[]{:S(2)}, u32[]{:S(2)}) collective-permute-start(bf16[256,512]{1,0:T(8,128)(2,1)} %tok.1), channel_id=1, source_target_pairs={{0,4},{1,5},{2,6},{3,7},{4,0},{5,1},{6,2},{7,3},{8,12},{9,13},{10,... | collective-permute-start | bytes 786440 | tf_op jit(solution)/shard_map/ppermute | solution.py:55
  17.6 14.3 %collective-permute-start = (bf16[256,512]{1,0:T(8,128)(2,1)}, bf16[256,512]{1,0:T(8,128)(2,1)S(1)}, u32[]{:S(2)}, u32[]{:S(2)}) collective-permute-start(bf16[256,512]{1,0:T(8,128)(2,1)} %tok.1), channel_id=1, source_target_pairs={{0,2},{1,3},{2,4},{3,5},{4,6},{5,7},{6,0},{7,1},{8,10},{9,11},{10,... | collective-permute-start | bytes 786440 | tf_op jit(solution)/shard_map/ppermute | solution.py:55
  22.5 0.9 copy-start.7
  23.4 8.5 %copy-start = (bf16[256,512]{1,0:T(8,128)(2,1)S(1)}, bf16[256,512]{1,0:T(8,128)(2,1)}, u32[]{:S(2)}) copy-start(bf16[256,512]{1,0:T(8,128)(2,1)} %tok.1) | copy-start | bytes 786436
  23.4 9.7 %copy-start.6 = (bf16[256,512]{1,0:T(8,128)(2,1)S(1)}, bf16[256,512]{1,0:T(8,128)(2,1)}, u32[]{:S(2)}) copy-start(bf16[256,512]{1,0:T(8,128)(2,1)} %r_1_.2) | copy-start | bytes 786436
  23.4 27.7 %copy-start.13 = (f32[4096]{0:T(1024)S(1)}, f32[4096]{0:T(1024)}, u32[]{:S(2)}) copy-start(f32[4096]{0:T(1024)} %param.13) | copy-start | bytes 49156
  25.3 38.3 %all-to-all-start.1 = ((bf16[32,16,896]{2,1,0:T(8,128)(2,1)}), bf16[32,16,896]{2,1,0:T(8,128)(2,1)S(1)}, u32[]{:S(2)}, u32[]{:S(2)}) async-start(bf16[32,16,896]{2,1,0:T(8,128)(2,1)} %outgoing_rows.1), calls=%async_computation.1 | async-start | bytes 1835008 | tf_op jit(solution)/shard_map/all_to_all | solution.py:455
  33.1 26.9 %collective-permute-start.3 = (bf16[4,256,512]{2,1,0:T(8,128)(2,1)}, bf16[4,256,512]{2,1,0:T(8,128)(2,1)S(1)}, u32[]{:S(2)}, u32[]{:S(2)}) collective-permute-start(bf16[4,256,512]{2,1,0:T(8,128)(2,1)} %pad_maximum_fusion), channel_id=1, source_target_pairs={{0,1},{1,0},{2,3},{3,2},{4,5},{5,4},{6,7},{7,6},{8,9},{9,8},{10,11... | collective-permute-start | bytes 3145736 | tf_op jit(solution)/shard_map/ppermute | solution.py:59
  33.1 14.2 %collective-permute-start.6 = (bf16[256,512]{1,0:T(8,128)(2,1)S(1)}, bf16[256,512]{1,0:T(8,128)(2,1)}, u32[]{:S(2)}, u32[]{:S(2)}) collective-permute-start(bf16[256,512]{1,0:T(8,128)(2,1)S(1)} %copy-done.6), channel_id=1, source_target_pairs={{0,6},{1,7},{2,0},{3,1},{4,2},{5,3},{6,4},{7,5},{8,14},{9,15},{10,... | collective-permute-start | bytes 786440 | tf_op jit(solution)/shard_map/ppermute | solution.py:55
  35.4 11.9 %collective-permute-start.5 = (bf16[256,512]{1,0:T(8,128)(2,1)S(1)}, bf16[256,512]{1,0:T(8,128)(2,1)}, u32[]{:S(2)}, u32[]{:S(2)}) collective-permute-start(bf16[256,512]{1,0:T(8,128)(2,1)S(1)} %copy-done.6), channel_id=1, source_target_pairs={{0,4},{1,5},{2,6},{3,7},{4,0},{5,1},{6,2},{7,3},{8,12},{9,13},{10,... | collective-permute-start | bytes 786440 | tf_op jit(solution)/shard_map/ppermute | solution.py:55
  36.9 14.1 %collective-permute-start.4 = (bf16[256,512]{1,0:T(8,128)(2,1)S(1)}, bf16[256,512]{1,0:T(8,128)(2,1)}, u32[]{:S(2)}, u32[]{:S(2)}) collective-permute-start(bf16[256,512]{1,0:T(8,128)(2,1)S(1)} %copy-done.6), channel_id=1, source_target_pairs={{0,2},{1,3},{2,4},{3,5},{4,6},{5,7},{6,0},{7,1},{8,10},{9,11},{10,... | collective-permute-start | bytes 786440 | tf_op jit(solution)/shard_map/ppermute | solution.py:55
  36.9 14.3 %collective-permute-start.7 = (bf16[256,512]{1,0:T(8,128)(2,1)S(1)}, bf16[256,512]{1,0:T(8,128)(2,1)}, u32[]{:S(2)}, u32[]{:S(2)}) collective-permute-start(bf16[256,512]{1,0:T(8,128)(2,1)S(1)} %copy-done.6), channel_id=1, source_target_pairs={{0,1},{1,0},{2,3},{3,2},{4,5},{5,4},{6,7},{7,6},{8,9},{9,8},{10,11... | collective-permute-start | bytes 786440 | tf_op jit(solution)/shard_map/ppermute | solution.py:59
  47.3 3.9 %collective-permute-start.10 = (bf16[256,512]{1,0:T(8,128)(2,1)}, bf16[256,512]{1,0:T(8,128)(2,1)}, u32[]{:S(2)}, u32[]{:S(2)}) collective-permute-start(bf16[256,512]{1,0:T(8,128)(2,1)} %collective-permute-done.6.r_4_), channel_id=1, source_target_pairs={{0,1},{1,0},{2,3},{3,2},{4,5},{5,4},{6,7},{7,6},{8,9},{9,8},{10,11... | collective-permute-start | bytes 786440 | tf_op jit(solution)/shard_map/ppermute | solution.py:59
  47.3 3.9 %collective-permute-start.9 = (bf16[256,512]{1,0:T(8,128)(2,1)}, bf16[256,512]{1,0:T(8,128)(2,1)}, u32[]{:S(2)}, u32[]{:S(2)}) collective-permute-start(bf16[256,512]{1,0:T(8,128)(2,1)} %collective-permute-done.5.r_3_), channel_id=1, source_target_pairs={{0,1},{1,0},{2,3},{3,2},{4,5},{5,4},{6,7},{7,6},{8,9},{9,8},{10,11... | collective-permute-start | bytes 786440 | tf_op jit(solution)/shard_map/ppermute | solution.py:59
  51.1 1.9 %collective-permute-start.8 = (bf16[256,512]{1,0:T(8,128)(2,1)}, bf16[256,512]{1,0:T(8,128)(2,1)}, u32[]{:S(2)}, u32[]{:S(2)}) collective-permute-start(bf16[256,512]{1,0:T(8,128)(2,1)} %collective-permute-done.4.r_2_), channel_id=1, source_target_pairs={{0,1},{1,0},{2,3},{3,2},{4,5},{5,4},{6,7},{7,6},{8,9},{9,8},{10,11... | collective-permute-start | bytes 786440 | tf_op jit(solution)/shard_map/ppermute | solution.py:59
  51.2 8.8 %copy-start.1 = (bf16[4096,512]{1,0:T(8,128)(2,1)S(1)}, bf16[4096,512]{1,0:T(8,128)(2,1)}, u32[]{:S(2)}) copy-start(bf16[4096,512]{1,0:T(8,128)(2,1)} %r_7_.1) | copy-start | bytes 12582916
  53.0 2.2 %copy-start.2 = (bf16[512,4096]{1,0:T(8,128)(2,1)S(1)}, bf16[512,4096]{1,0:T(8,128)(2,1)}, u32[]{:S(2)}) copy-start(bf16[512,4096]{1,0:T(8,128)(2,1)} %r_2_.1) | copy-start | bytes 12582916
  59.3 0.7 copy-start.11
  63.7 17.1 %copy-start.4 = (bf16[896,512]{1,0:T(8,128)(2,1)S(1)}, bf16[896,512]{1,0:T(8,128)(2,1)}, u32[]{:S(2)}) copy-start(bf16[896,512]{1,0:T(8,128)(2,1)} %r_10_.1) | copy-start | bytes 2752516
  63.7 17.1 %copy-start.12 = (bf16[256,512]{1,0:T(8,128)(2,1)S(1)}, bf16[256,512]{1,0:T(8,128)(2,1)}, u32[]{:S(2)}) copy-start(bf16[256,512]{1,0:T(8,128)(2,1)} %copy-done.11) | copy-start | bytes 786436
  63.7 17.1 %copy-start.5 = (bf16[896,512]{1,0:T(8,128)(2,1)S(1)}, bf16[896,512]{1,0:T(8,128)(2,1)}, u32[]{:S(2)}) copy-start(bf16[896,512]{1,0:T(8,128)(2,1)} %r_11_.1) | copy-start | bytes 2752516
  64.7 28.7 %copy-start.3 = (bf16[512,4096]{1,0:T(8,128)(2,1)S(1)}, bf16[512,4096]{1,0:T(8,128)(2,1)}, u32[]{:S(2)}) copy-start(bf16[512,4096]{1,0:T(8,128)(2,1)} %r_2_.1) | copy-start | bytes 12582916
  64.7 8.5 %collective-permute-start.13 = (bf16[128,896]{1,0:T(8,128)(2,1)S(1)}, bf16[128,896]{1,0:T(8,128)(2,1)S(1)}, u32[]{:S(2)}, u32[]{:S(2)}) collective-permute-start(bf16[128,896]{1,0:T(8,128)(2,1)S(1)} %bitcast.16), channel_id=1, source_target_pairs={{0,6},{1,7},{2,0},{3,1},{4,2},{5,3},{6,4},{7,5},{8,14},{9,15},{10,... | collective-permute-start | bytes 688136 | tf_op jit(solution)/shard_map/ppermute | solution.py:55
  65.5 10.0 %collective-permute-start.12 = (bf16[128,896]{1,0:T(8,128)(2,1)S(1)}, bf16[128,896]{1,0:T(8,128)(2,1)S(1)}, u32[]{:S(2)}, u32[]{:S(2)}) collective-permute-start(bf16[128,896]{1,0:T(8,128)(2,1)S(1)} %bitcast.17), channel_id=1, source_target_pairs={{0,4},{1,5},{2,6},{3,7},{4,0},{5,1},{6,2},{7,3},{8,12},{9,13},{10,... | collective-permute-start | bytes 688136 | tf_op jit(solution)/shard_map/ppermute | solution.py:55
  66.9 12.4 %collective-permute-start.11 = (bf16[128,896]{1,0:T(8,128)(2,1)S(1)}, bf16[128,896]{1,0:T(8,128)(2,1)S(1)}, u32[]{:S(2)}, u32[]{:S(2)}) collective-permute-start(bf16[128,896]{1,0:T(8,128)(2,1)S(1)} %bitcast.18), channel_id=1, source_target_pairs={{0,2},{1,3},{2,4},{3,5},{4,6},{5,7},{6,0},{7,1},{8,10},{9,11},{10,... | collective-permute-start | bytes 688136 | tf_op jit(solution)/shard_map/ppermute | solution.py:55
  67.7 11.6 %collective-permute-start.14 = (bf16[128,896]{1,0:T(8,128)(2,1)S(1)}, bf16[128,896]{1,0:T(8,128)(2,1)S(1)}, u32[]{:S(2)}, u32[]{:S(2)}) collective-permute-start(bf16[128,896]{1,0:T(8,128)(2,1)S(1)} %bitcast.19), channel_id=1, source_target_pairs={{0,1},{1,0},{2,3},{3,2},{4,5},{5,4},{6,7},{7,6},{8,9},{9,8},{10,11... | collective-permute-start | bytes 688136 | tf_op jit(solution)/shard_map/ppermute | solution.py:59
  73.2 6.1 %collective-permute-start.17 = (bf16[128,896]{1,0:T(8,128)(2,1)S(1)}, bf16[128,896]{1,0:T(8,128)(2,1)S(1)}, u32[]{:S(2)}, u32[]{:S(2)}) collective-permute-start(bf16[128,896]{1,0:T(8,128)(2,1)S(1)} %collective-permute-done.13.r_3_), channel_id=1, source_target_pairs={{0,1},{1,0},{2,3},{3,2},{4,5},{5,4},{6,7},{7,6},{8,9},{9,8},{10,11... | collective-permute-start | bytes 688136 | tf_op jit(solution)/shard_map/ppermute | solution.py:59
  75.5 3.8 %collective-permute-start.16 = (bf16[128,896]{1,0:T(8,128)(2,1)S(1)}, bf16[128,896]{1,0:T(8,128)(2,1)S(1)}, u32[]{:S(2)}, u32[]{:S(2)}) collective-permute-start(bf16[128,896]{1,0:T(8,128)(2,1)S(1)} %collective-permute-done.12.r_2_), channel_id=1, source_target_pairs={{0,1},{1,0},{2,3},{3,2},{4,5},{5,4},{6,7},{7,6},{8,9},{9,8},{10,11... | collective-permute-start | bytes 688136 | tf_op jit(solution)/shard_map/ppermute | solution.py:59
  79.3 1.5 %collective-permute-start.15 = (bf16[128,896]{1,0:T(8,128)(2,1)S(1)}, bf16[128,896]{1,0:T(8,128)(2,1)S(1)}, u32[]{:S(2)}, u32[]{:S(2)}) collective-permute-start(bf16[128,896]{1,0:T(8,128)(2,1)S(1)} %collective-permute-done.11.r_1_), channel_id=1, source_target_pairs={{0,1},{1,0},{2,3},{3,2},{4,5},{5,4},{6,7},{7,6},{8,9},{9,8},{10,11... | collective-permute-start | bytes 688136 | tf_op jit(solution)/shard_map/ppermute | solution.py:59
  87.7 2.6 %collective-permute-start.18 = (bf16[4,128,896]{2,1,0:T(8,128)(2,1)S(1)}, bf16[4,128,896]{2,1,0:T(8,128)(2,1)S(1)}, u32[]{:S(2)}, u32[]{:S(2)}) collective-permute-start(bf16[4,128,896]{2,1,0:T(8,128)(2,1)S(1)} %get-tuple-element.40), channel_id=1, source_target_pairs={{0,1},{1,0},{2,3},{3,2},{4,5},{5,4},{6,7},{7,6},{8,9},{9,8},{10,11... | collective-permute-start | bytes 2752520 | tf_op jit(solution)/shard_map/ppermute | solution.py:59
  90.5 8.5 %collective-permute-start.19 = (bf16[128,896]{1,0:T(8,128)(2,1)S(1)}, bf16[128,896]{1,0:T(8,128)(2,1)S(1)}, u32[]{:S(2)}, u32[]{:S(2)}) collective-permute-start(bf16[128,896]{1,0:T(8,128)(2,1)S(1)} %get-tuple-element.49), channel_id=1, source_target_pairs={{0,6},{1,7},{2,0},{3,1},{4,2},{5,3},{6,4},{7,5},{8,14},{9,15},{10,... | collective-permute-start | bytes 688136 | tf_op jit(solution)/shard_map/ppermute | solution.py:81
  91.6 10.0 %collective-permute-start.20 = (bf16[128,896]{1,0:T(8,128)(2,1)S(1)}, bf16[128,896]{1,0:T(8,128)(2,1)S(1)}, u32[]{:S(2)}, u32[]{:S(2)}) collective-permute-start(bf16[128,896]{1,0:T(8,128)(2,1)S(1)} %get-tuple-element.50), channel_id=1, source_target_pairs={{0,4},{1,5},{2,6},{3,7},{4,0},{5,1},{6,2},{7,3},{8,12},{9,13},{10,... | collective-permute-start | bytes 688136 | tf_op jit(solution)/shard_map/ppermute | solution.py:81
  92.6 12.9 %collective-permute-start.21 = (bf16[128,896]{1,0:T(8,128)(2,1)S(1)}, bf16[128,896]{1,0:T(8,128)(2,1)S(1)}, u32[]{:S(2)}, u32[]{:S(2)}) collective-permute-start(bf16[128,896]{1,0:T(8,128)(2,1)S(1)} %get-tuple-element.51), channel_id=1, source_target_pairs={{0,2},{1,3},{2,4},{3,5},{4,6},{5,7},{6,0},{7,1},{8,10},{9,11},{10,... | collective-permute-start | bytes 688136 | tf_op jit(solution)/shard_map/ppermute | solution.py:81
  97.3 1.0 copy-start.9
  105.5 11.6 %collective-permute-start.22 = (bf16[4,256,512]{2,1,0:T(8,128)(2,1)S(1)}, bf16[4,256,512]{2,1,0:T(8,128)(2,1)}, u32[]{:S(2)}, u32[]{:S(2)}) collective-permute-start(bf16[4,256,512]{2,1,0:T(8,128)(2,1)S(1)} %get-tuple-element.52), channel_id=1, source_target_pairs={{0,1},{1,0},{2,3},{3,2},{4,5},{5,4},{6,7},{7,6},{8,9},{9,8},{10,11... | collective-permute-start | bytes 3145736 | tf_op jit(solution)/shard_map/ppermute | solution.py:59
  107.2 38.5 %all-to-all-start.2 = ((bf16[32,16,896]{2,1,0:T(8,128)(2,1)}), bf16[32,16,896]{2,1,0:T(8,128)(2,1)S(1)}, u32[]{:S(2)}, u32[]{:S(2)}) async-start(bf16[32,16,896]{2,1,0:T(8,128)(2,1)} %placed_grads.1), calls=%async_computation.2 | async-start | bytes 1835008 | tf_op jit(solution)/shard_map/all_to_all | solution.py:471
  117.0 28.8 %copy-start.8 = (bf16[8,16,896]{2,1,0:T(8,128)(2,1)S(1)}, bf16[8,16,896]{2,1,0:T(8,128)(2,1)}, u32[]{:S(2)}) copy-start(bf16[8,16,896]{2,1,0:T(8,128)(2,1)} %enc.3) | copy-start | bytes 688132
  117.0 1.3 copy-start.10
  119.8 9.3 %collective-permute-start.23 = (bf16[256,512]{1,0:T(8,128)(2,1)S(1)}, bf16[256,512]{1,0:T(8,128)(2,1)S(1)}, u32[]{:S(2)}, u32[]{:S(2)}) collective-permute-start(bf16[256,512]{1,0:T(8,128)(2,1)S(1)} %get-tuple-element.54), channel_id=1, source_target_pairs={{0,6},{1,7},{2,0},{3,1},{4,2},{5,3},{6,4},{7,5},{8,14},{9,15},{10,... | collective-permute-start | bytes 786440 | tf_op jit(solution)/shard_map/ppermute | solution.py:81
  120.4 10.8 %collective-permute-start.24 = (bf16[256,512]{1,0:T(8,128)(2,1)S(1)}, bf16[256,512]{1,0:T(8,128)(2,1)S(1)}, u32[]{:S(2)}, u32[]{:S(2)}) collective-permute-start(bf16[256,512]{1,0:T(8,128)(2,1)S(1)} %get-tuple-element.55), channel_id=1, source_target_pairs={{0,4},{1,5},{2,6},{3,7},{4,0},{5,1},{6,2},{7,3},{8,12},{9,13},{10,... | collective-permute-start | bytes 786440 | tf_op jit(solution)/shard_map/ppermute | solution.py:81
  121.3 14.1 %collective-permute-start.25 = (bf16[256,512]{1,0:T(8,128)(2,1)S(1)}, bf16[256,512]{1,0:T(8,128)(2,1)S(1)}, u32[]{:S(2)}, u32[]{:S(2)}) collective-permute-start(bf16[256,512]{1,0:T(8,128)(2,1)S(1)} %get-tuple-element.56), channel_id=1, source_target_pairs={{0,2},{1,3},{2,4},{3,5},{4,6},{5,7},{6,0},{7,1},{8,10},{9,11},{10,... | collective-permute-start | bytes 786440 | tf_op jit(solution)/shard_map/ppermute | solution.py:81
  136.4 1.2 collective-permute-start.26
  137.7 3.6 %collective-permute-start.29 = (f32[256]{0:T(256)S(1)}, f32[256]{0:T(256)S(1)}, u32[]{:S(2)}, u32[]{:S(2)}) collective-permute-start(f32[256]{0:T(256)S(1)} %add.58), channel_id=1, source_target_pairs={{0,6},{1,7},{2,0},{3,1},{4,2},{5,3},{6,4},{7,5},{8,14},{9,15},{10,... | collective-permute-start | bytes 3080 | tf_op jit(solution)/shard_map/ppermute | solution.py:479
  138.5 5.1 %collective-permute-start.28 = (f32[256]{0:T(256)S(1)}, f32[256]{0:T(256)S(1)}, u32[]{:S(2)}, u32[]{:S(2)}) collective-permute-start(f32[256]{0:T(256)S(1)} %add.58), channel_id=1, source_target_pairs={{0,4},{1,5},{2,6},{3,7},{4,0},{5,1},{6,2},{7,3},{8,12},{9,13},{10,... | collective-permute-start | bytes 3080 | tf_op jit(solution)/shard_map/ppermute | solution.py:479
  139.2 4.8 %collective-permute-start.27 = (f32[256]{0:T(256)S(1)}, f32[256]{0:T(256)S(1)}, u32[]{:S(2)}, u32[]{:S(2)}) collective-permute-start(f32[256]{0:T(256)S(1)} %add.58), channel_id=1, source_target_pairs={{0,2},{1,3},{2,4},{3,5},{4,6},{5,7},{6,0},{7,1},{8,10},{9,11},{10,... | collective-permute-start | bytes 3080 | tf_op jit(solution)/shard_map/ppermute | solution.py:479

commit v4 on v3

--- a/solution.py
+++ b/solution.py
@@ -140,7 +140,7 @@
         in_specs=[smem()] + [vmem()] * (len(pieces) + 1) + [hbm()],
         out_specs=vmem(),
         scratch_shapes=[pltpu.VMEM((count, share, cols), BF16), pltpu.SemaphoreType.DMA((count,))],
-        compiler_params=params(20),
+        compiler_params=params(48),
         cost_estimate=cost(4.5),
         name="queries",
     )(src, *pieces, gain.reshape(count, share), w_query)
@@ -173,7 +173,7 @@
         in_specs=[smem()] + [vmem()] * len(pieces) + [hbm()],
         out_specs=vmem(),
         scratch_shapes=[pltpu.VMEM((count, cols, share), BF16), pltpu.SemaphoreType.DMA((count,))],
-        compiler_params=params(20),
+        compiler_params=params(48),
         cost_estimate=cost(4.5),
         name="d_attended",
     )(src, *pieces, w_out)
@@ -206,7 +206,7 @@
         in_specs=[smem(), vmem(), hbm()],
         out_specs=(vmem(), vmem()),
         scratch_shapes=[pltpu.VMEM((count, cols, share), BF16), pltpu.SemaphoreType.DMA((count,))],
-        compiler_params=params(20),
+        compiler_params=params(48),
         cost_estimate=cost(4),
         name="branches",
     )(src, att, w_out)
@@ -455,8 +455,8 @@
     incoming = lax.all_to_all(outgoing, "dp", split_axis=0, concat_axis=0, tiled=True)
     cot_own = over_chips(cot_in, count)
     q = run_query(src, tok_own + [swap(jnp.stack(tok_own), count)], gain_dec, w_query)
+    cot_own, q = lax.optimization_barrier((cot_own, q))
     d = run_back(src, cot_own + [swap(p, count) for p in cot_own], w_out)
-    incoming, q, d = lax.optimization_barrier((incoming, q, d))
     picked = run_pick(owner, incoming).reshape(readings * own_tokens, width)
     row_own = over_chips(picked, count)
     rows = row_own + [swap(p, count) for p in row_own]
@@ -477,11 +477,11 @@
     total = squares
     for k in range(1, half):
         total = total + lax.ppermute(squares, "mp", chip_shift(count, k))
+    d_encodings = run_finish(slot, back_in, encodings, gain_enc)
+    total, d_encodings = lax.optimization_barrier((total, d_encodings))
     post = lax.rsqrt(total / (share_cols * count) + EPS)[:, None]
     gain_here = lax.dynamic_slice_in_dim(gain_post, here * share_cols, share_cols, 0)
     ffn = (mixed_wide * post * gain_here).astype(BF16)
-
-    d_encodings = run_finish(slot, back_in, encodings, gain_enc)
     return (mixed, ffn, d_encodings)
 
 

time: 148 us -> 140 us (0.946)
  waiting for transfers between devices: 58.5 us -> 48.7 us
  starting transfers between devices: 47.9 us -> 51.4 us
  local copies, waits for them, and re-layouts: 9.23 us -> 6.99 us
    ppermute x9, waiting for transfers between devices: 25.2 us -> 15.2 us  [over_chips(): lax.ppermute(x, 'mp', chip_shift(count, k))]
    all_to_all x1, waiting for transfers between devices: 0.01 us -> 5.27 us  [shards(): lax.all_to_all(outgoing, 'dp', split_axis=0, concat_axis=0, tiled=True)]
    ppermute x12, waiting for transfers between devices: 6.58 us -> 3.14 us  [swap(): return lax.ppermute(x, 'mp', core_swap(count))]
    unnamed x29 -> x25, local copies, waits for them, and re-layouts: 6.88 us -> 4.64 us
    all_to_all x1, starting transfers between devices: 9.78 us -> 8.04 us  [shards(): lax.all_to_all(back_out, 'dp', split_axis=0, concat_axis=0, tiled=True)]
    ppermute x3, waiting for transfers between devices: 3.85 us -> 2.29 us  [shards(): total = total + lax.ppermute(squares, 'mp', chip_shift(count, k))]
  transfers between devices with their start and end apart: 33 -> 33, of which waited for: 19 -> 16; matrix products, arithmetic and copies ran while one was open for 3% -> 2% of each run, Pallas kernels for 12% -> 14%
where the time goes in v4:
time: 140 us; the launch traced here: 139 us
  starting transfers between devices  51.4 us (37%)
  waiting for transfers between devices  48.7 us (35%)
  Pallas kernels  28.5 us (20%)
  local copies, waits for them, and re-layouts  6.99 us (5%)
  other arithmetic  2.38 us (2%)
    ppermute x6, waiting for transfers between devices, pair_shares(): lax.ppermute(pair[k], 'mp', chip_shift(count, -k))  20.8 us
    ppermute x9, waiting for transfers between devices, over_chips(): lax.ppermute(x, 'mp', chip_shift(count, k))  15.2 us
    ppermute x9, starting transfers between devices, over_chips(): lax.ppermute(x, 'mp', chip_shift(count, k))  12.7 us
    all_to_all x1, starting transfers between devices, shards(): lax.all_to_all(jnp.broadcast_to(wanted[:, None], (dp_count, IDS_WIDTH)),...  11.7 us
    all_to_all x1, starting transfers between devices, shards(): lax.all_to_all(back_out, 'dp', split_axis=0, concat_axis=0, tiled=True)  8.04 us
    all_to_all x1, starting transfers between devices, shards(): lax.all_to_all(outgoing, 'dp', split_axis=0, concat_axis=0, tiled=True)  7.75 us
    pallas_call x1, Pallas kernels, run_attention(): pl.pallas_call(lambda *r: attention_kernel(count, blocks, *r), out_shape=...  6.97 us
    ppermute x6, starting transfers between devices, pair_shares(): lax.ppermute(pair[k], 'mp', chip_shift(count, -k))  5.7 us
  transfers between devices with their start and end apart: 33, of which 16 were waited for; matrix products, arithmetic and copies ran while one was open for 2% of the time, Pallas kernels for 14%

profile of v4, /device:TPU:8, one launch (start us, length us, event | category | flops | bytes accessed | tf_op | source)
XLA Modules:
  0.0 138.9 jit_solution(7503736356016463605)
XLA Ops:
  0.6 0.8 copy.17
  1.6 0.7 broadcast_in_dim.46
  2.3 11.7 %all-to-all-start = ((s32[32,1,128]{2,1,0:T(1,128)}), s32[32,1,128]{2,1,0:T(1,128)S(1)}, u32[]{:S(2)}, u32[]{:S(2)}) async-start(s32[32,1,128]{2,1,0:T(1,128)} %broadcast_in_dim.46), calls=%async_computation | async-start | bytes 32768 | tf_op jit(solution)/shard_map/all_to_all | solution.py:442
  14.0 1.6 %collective-permute-start.10 = (bf16[256,512]{1,0:T(8,128)(2,1)}, bf16[256,512]{1,0:T(8,128)(2,1)S(1)}, u32[]{:S(2)}, u32[]{:S(2)}) collective-permute-start(bf16[256,512]{1,0:T(8,128)(2,1)} %tok.1), channel_id=1, source_target_pairs={{0,2},{1,3},{2,4},{3,5},{4,6},{5,7},{6,0},{7,1},{8,10},{9,11},{10,... | collective-permute-start | bytes 786440 | tf_op jit(solution)/shard_map/ppermute | solution.py:55
  15.6 2.7 %collective-permute-start.11 = (bf16[256,512]{1,0:T(8,128)(2,1)}, bf16[256,512]{1,0:T(8,128)(2,1)S(1)}, u32[]{:S(2)}, u32[]{:S(2)}) collective-permute-start(bf16[256,512]{1,0:T(8,128)(2,1)} %tok.1), channel_id=1, source_target_pairs={{0,4},{1,5},{2,6},{3,7},{4,0},{5,1},{6,2},{7,3},{8,12},{9,13},{10,... | collective-permute-start | bytes 786440 | tf_op jit(solution)/shard_map/ppermute | solution.py:55
  18.3 1.4 %collective-permute-start.12 = (bf16[256,512]{1,0:T(8,128)(2,1)}, bf16[256,512]{1,0:T(8,128)(2,1)S(1)}, u32[]{:S(2)}, u32[]{:S(2)}) collective-permute-start(bf16[256,512]{1,0:T(8,128)(2,1)} %tok.1), channel_id=1, source_target_pairs={{0,6},{1,7},{2,0},{3,1},{4,2},{5,3},{6,4},{7,5},{8,14},{9,15},{10,... | collective-permute-start | bytes 786440 | tf_op jit(solution)/shard_map/ppermute | solution.py:55
  19.7 0.7 reshape.94.gain
  20.4 2.0 %all-to-all-done = s32[32,1,128]{2,1,0:T(1,128)S(1)} async-done(((s32[32,1,128]{2,1,0:T(1,128)}), s32[32,1,128]{2,1,0:T(1,128)S(1)}, u32[]{:S(2)}, u32[]{:S(2)}) %all-to-all-start) | async-done | bytes 16416 | tf_op jit(solution)/shard_map/all_to_all | solution.py:442
  22.5 0.9 copy-done.4
  23.4 1.9 %outgoing_rows.1 = bf16[32,16,896]{2,1,0:T(8,128)(2,1)} custom-call(s32[32,128]{1,0:T(8,128)S(1)} %bitcast.14, bf16[8,16,896]{2,1,0:T(8,128)(2,1)S(1)} %copy-done.4, f32[1,1,896]{2,1,0:T(1,128)S(1)} %reshape.94.gain), custom_call_target="tpu_custom_call" | custom-call | flops 1870000000 | tf_op jit(solution)/shard_map/outgoing_rows/pallas_call | solution.py:297
  25.3 7.8 %all-to-all-start.1 = ((bf16[32,16,896]{2,1,0:T(8,128)(2,1)}), bf16[32,16,896]{2,1,0:T(8,128)(2,1)S(1)}, u32[]{:S(2)}, u32[]{:S(2)}) async-start(bf16[32,16,896]{2,1,0:T(8,128)(2,1)} %outgoing_rows.1), calls=%async_computation.1 | async-start | bytes 1835008 | tf_op jit(solution)/shard_map/all_to_all | solution.py:455
  33.2 1.1 pad_maximum_fusion
  34.4 0.6 collective-permute-start.7
  35.0 0.9 collective-permute-start.8
  35.9 1.9 %collective-permute-start.9 = (bf16[256,512]{1,0:T(8,128)(2,1)S(1)}, bf16[256,512]{1,0:T(8,128)(2,1)}, u32[]{:S(2)}, u32[]{:S(2)}) collective-permute-start(bf16[256,512]{1,0:T(8,128)(2,1)S(1)} %copy-done.3), channel_id=1, source_target_pairs={{0,6},{1,7},{2,0},{3,1},{4,2},{5,3},{6,4},{7,5},{8,14},{9,15},{10,... | collective-permute-start | bytes 786440 | tf_op jit(solution)/shard_map/ppermute | solution.py:55
  37.8 3.9 %queries.1.r_8_ = bf16[256,512]{1,0:T(8,128)(2,1)S(1)} custom-call(s32[8]{0:T(128)S(1)} %pad_add_fusion.r_0_, bf16[256,512]{1,0:T(8,128)(2,1)S(1)} %copy-done, bf16[256,512]{1,0:T(8,128)(2,1)S(1)} %collective-permute-done.10.r_2_, bf16[256,512]{1,0:T(8,128)(2,1)S(1)} %collective-permute-done.11.r_3_, bf16[256,512]{1,0:T(8,128)(2,1)S(1)} %collective-permute-done.12.r_4_, ...), custom_call_target="tpu_custom_call" | custom-call | flops 4950000128 | tf_op jit(solution)/shard_map/queries/pallas_call | solution.py:137
  41.7 0.7 copy-done.8
  42.4 7.6 %collective-permute-done.7.r_2_ = bf16[256,512]{1,0:T(8,128)(2,1)} collective-permute-done((bf16[256,512]{1,0:T(8,128)(2,1)S(1)}, bf16[256,512]{1,0:T(8,128)(2,1)}, u32[]{:S(2)}, u32[]{:S(2)}) %collective-permute-start.7) | collective-permute-done | bytes 262176 | tf_op jit(solution)/shard_map/ppermute | solution.py:55
  50.1 0.6 collective-permute-done.9.r_4_
  50.7 0.5 collective-permute-start.15
  51.2 0.5 collective-permute-start.17
  51.7 5.3 %all-to-all-done.1.rows = bf16[32,16,896]{2,1,0:T(8,128)(2,1)S(1)} async-done(((bf16[32,16,896]{2,1,0:T(8,128)(2,1)}), bf16[32,16,896]{2,1,0:T(8,128)(2,1)S(1)}, u32[]{:S(2)}, u32[]{:S(2)}) %all-to-all-start.1) | async-done | bytes 917536 | tf_op jit(solution)/shard_map/all_to_all | solution.py:455
  57.0 1.0 picked_rows.1
  58.0 0.7 collective-permute-start
  58.6 1.2 collective-permute-start.1
  59.9 1.7 %collective-permute-start.2 = (bf16[128,896]{1,0:T(8,128)(2,1)S(1)}, bf16[128,896]{1,0:T(8,128)(2,1)S(1)}, u32[]{:S(2)}, u32[]{:S(2)}) collective-permute-start(bf16[128,896]{1,0:T(8,128)(2,1)S(1)} %bitcast.18), channel_id=1, source_target_pairs={{0,6},{1,7},{2,0},{3,1},{4,2},{5,3},{6,4},{7,5},{8,14},{9,15},{10,... | collective-permute-start | bytes 688136 | tf_op jit(solution)/shard_map/ppermute | solution.py:55
  61.6 6.8 %collective-permute-done.r_1_ = bf16[128,896]{1,0:T(8,128)(2,1)S(1)} collective-permute-done((bf16[128,896]{1,0:T(8,128)(2,1)S(1)}, bf16[128,896]{1,0:T(8,128)(2,1)S(1)}, u32[]{:S(2)}, u32[]{:S(2)}) %collective-permute-start) | collective-permute-done | bytes 229408 | tf_op jit(solution)/shard_map/ppermute | solution.py:55
  68.3 0.5 collective-permute-start.5
  68.8 0.2 collective-permute-done.2.r_3_
  69.0 4.4 %d_attended.1.r_9_ = bf16[256,512]{1,0:T(8,128)(2,1)S(1)} custom-call(s32[8]{0:T(128)S(1)} %pad_add_fusion.r_0_, bf16[256,512]{1,0:T(8,128)(2,1)S(1)} %copy-done.3, bf16[256,512]{1,0:T(8,128)(2,1)} %collective-permute-done.7.r_2_, bf16[256,512]{1,0:T(8,128)(2,1)} %collective-permute-done.8.r_3_, bf16[256,512]{1,0:T(8,128)(2,1)} %collective-permute-done.9.r_4_, ...), custom_call_target="tpu_custom_call" | custom-call | flops 4950000128 | tf_op jit(solution)/shard_map/d_attended/pallas_call | solution.py:170
  73.4 7.0 %attention.1 = (bf16[4,128,896]{2,1,0:T(8,128)(2,1)S(1)}, bf16[4,128,896]{2,1,0:T(8,128)(2,1)S(1)}, bf16[256,512]{1,0:T(8,128)(2,1)S(1)}) custom-call(bf16[128,896]{1,0:T(8,128)(2,1)S(1)} %bitcast.20, bf16[128,896]{1,0:T(8,128)(2,1)S(1)} %collective-permute-done.r_1_, bf16[128,896]{1,0:T(8,128)(2,1)S(1)} %collective-permute-done.1.r_2_, ...), custom_call_target="tpu_custom_call" | custom-call | flops 9900000256 | tf_op jit(solution)/shard_map/attention/pallas_call | solution.py:275
  80.4 0.6 collective-permute-start.18
  81.0 2.1 %collective-permute-done.18.other = bf16[4,128,896]{2,1,0:T(8,128)(2,1)S(1)} collective-permute-done((bf16[4,128,896]{2,1,0:T(8,128)(2,1)S(1)}, bf16[4,128,896]{2,1,0:T(8,128)(2,1)S(1)}, u32[]{:S(2)}, u32[]{:S(2)}) %collective-permute-start.18) | collective-permute-done | bytes 917536 | tf_op jit(solution)/shard_map/ppermute | solution.py:59
  83.1 0.2 pair_sums.2
  83.3 2.6 %collective-permute-start.19 = (bf16[128,896]{1,0:T(8,128)(2,1)S(1)}, bf16[128,896]{1,0:T(8,128)(2,1)S(1)}, u32[]{:S(2)}, u32[]{:S(2)}) collective-permute-start(bf16[128,896]{1,0:T(8,128)(2,1)S(1)} %get-tuple-element.55), channel_id=1, source_target_pairs={{0,6},{1,7},{2,0},{3,1},{4,2},{5,3},{6,4},{7,5},{8,14},{9,15},{10,... | collective-permute-start | bytes 688136 | tf_op jit(solution)/shard_map/ppermute | solution.py:81
  86.0 1.0 collective-permute-start.21
  86.9 4.1 %branches.1 = (bf16[4,256,512]{2,1,0:T(8,128)(2,1)S(1)}, bf16[4,256,512]{2,1,0:T(8,128)(2,1)S(1)}) custom-call(s32[8]{0:T(128)S(1)} %pad_add_fusion.r_0_, bf16[256,512]{1,0:T(8,128)(2,1)S(1)} %get-tuple-element.51.r_1_, bf16[512,4096]{1,0:T(8,128)(2,1)} %r_2_.1), custom_call_target="tpu_custom_call" | custom-call | flops 4400000000 | tf_op jit(solution)/shard_map/branches/pallas_call | solution.py:203
  91.1 1.0 copy-done.6
  92.0 4.3 %collective-permute-done.19 = bf16[128,896]{1,0:T(8,128)(2,1)S(1)} collective-permute-done((bf16[128,896]{1,0:T(8,128)(2,1)S(1)}, bf16[128,896]{1,0:T(8,128)(2,1)S(1)}, u32[]{:S(2)}, u32[]{:S(2)}) %collective-permute-start.19) | collective-permute-done | bytes 229408 | tf_op jit(solution)/shard_map/ppermute | solution.py:81
  96.3 3.4 %collective-permute-done.21 = bf16[128,896]{1,0:T(8,128)(2,1)S(1)} collective-permute-done((bf16[128,896]{1,0:T(8,128)(2,1)S(1)}, bf16[128,896]{1,0:T(8,128)(2,1)S(1)}, u32[]{:S(2)}, u32[]{:S(2)}) %collective-permute-start.21) | collective-permute-done | bytes 229408 | tf_op jit(solution)/shard_map/ppermute | solution.py:81
  99.7 1.7 %placed_grads.1 = bf16[32,16,896]{2,1,0:T(8,128)(2,1)} custom-call(s32[32]{0:T(128)S(1)} %get-tuple-element.71.reading, bf16[8,16,896]{2,1,0:T(8,128)(2,1)S(1)} %bitcast.24, bf16[8,16,896]{2,1,0:T(8,128)(2,1)S(1)} %bitcast.21, bf16[8,16,896]{2,1,0:T(8,128)(2,1)S(1)} %bitcast.22, bf16[8,16,896]{2,1,0:T(8,128)(2,1)S(1)} %bitcast.23), custom_call_target="tpu_custom_call" | custom-call | flops 1870000000 | tf_op jit(solution)/shard_map/placed_grads/pallas_call | solution.py:343
  101.4 8.0 %all-to-all-start.2 = ((bf16[32,16,896]{2,1,0:T(8,128)(2,1)}), bf16[32,16,896]{2,1,0:T(8,128)(2,1)S(1)}, u32[]{:S(2)}, u32[]{:S(2)}) async-start(bf16[32,16,896]{2,1,0:T(8,128)(2,1)} %placed_grads.1), calls=%async_computation.2 | async-start | bytes 1835008 | tf_op jit(solution)/shard_map/all_to_all | solution.py:471
  109.5 1.2 copy-done.7
  110.7 1.5 %pair_sums.3 = (bf16[256,512]{1,0:T(8,128)(2,1)S(1)}, bf16[256,512]{1,0:T(8,128)(2,1)S(1)}, bf16[256,512]{1,0:T(8,128)(2,1)S(1)}, bf16[256,512]{1,0:T(8,128)(2,1)S(1)}) custom-call(bf16[4,256,512]{2,1,0:T(8,128)(2,1)S(1)} %copy-done.7, bf16[4,256,512]{2,1,0:T(8,128)(2,1)} %collective-permute-done.22.other), custom_call_target="tpu_custom_call" | custom-call | flops 770000000 | tf_op jit(solution)/shard_map/pair_sums/pallas_call | solution.py:68
  112.2 1.0 collective-permute-start.23
  113.2 0.3 collective-permute-start.24
  113.4 0.8 collective-permute-start.25
  114.3 0.8 dynamic_slice.3
  115.1 6.4 %collective-permute-done.23.refs_1_ = bf16[256,512]{1,0:T(8,128)(2,1)S(1)} collective-permute-done((bf16[256,512]{1,0:T(8,128)(2,1)S(1)}, bf16[256,512]{1,0:T(8,128)(2,1)S(1)}, u32[]{:S(2)}, u32[]{:S(2)}) %collective-permute-start.23) | collective-permute-done | bytes 262176 | tf_op jit(solution)/shard_map/ppermute | solution.py:81
  121.4 2.5 %collective-permute-done.24.refs_2_ = bf16[256,512]{1,0:T(8,128)(2,1)S(1)} collective-permute-done((bf16[256,512]{1,0:T(8,128)(2,1)S(1)}, bf16[256,512]{1,0:T(8,128)(2,1)S(1)}, u32[]{:S(2)}, u32[]{:S(2)}) %collective-permute-start.24) | collective-permute-done | bytes 262176 | tf_op jit(solution)/shard_map/ppermute | solution.py:81
  123.9 4.2 %collective-permute-done.25.refs_3_ = bf16[256,512]{1,0:T(8,128)(2,1)S(1)} collective-permute-done((bf16[256,512]{1,0:T(8,128)(2,1)S(1)}, bf16[256,512]{1,0:T(8,128)(2,1)S(1)}, u32[]{:S(2)}, u32[]{:S(2)}) %collective-permute-start.25) | collective-permute-done | bytes 262176 | tf_op jit(solution)/shard_map/ppermute | solution.py:81
  128.2 0.9 mixed.1
  129.1 0.1 reduce
  129.2 0.1 collective-permute-start.26
  129.3 0.1 slice_reduce_fusion
  129.4 1.0 collective-permute-done.26
  130.4 2.1 %collective-permute-start.28 = (f32[256]{0:T(256)S(1)}, f32[256]{0:T(256)S(1)}, u32[]{:S(2)}, u32[]{:S(2)}) collective-permute-start(f32[256]{0:T(256)S(1)} %add.58), channel_id=1, source_target_pairs={{0,4},{1,5},{2,6},{3,7},{4,0},{5,1},{6,2},{7,3},{8,12},{9,13},{10,... | collective-permute-start | bytes 3080 | tf_op jit(solution)/shard_map/ppermute | solution.py:479
  132.5 1.2 collective-permute-start.29
  133.7 0.1 select_reduce_fusion.1.slot
  133.8 1.4 %collective-permute-done.27 = f32[256]{0:T(256)S(1)} collective-permute-done((f32[256]{0:T(256)S(1)}, f32[256]{0:T(256)S(1)}, u32[]{:S(2)}, u32[]{:S(2)}) %collective-permute-start.27) | collective-permute-done | bytes 1056 | tf_op jit(solution)/shard_map/ppermute | solution.py:479
  135.2 0.3 collective-permute-done.28
  135.5 0.6 collective-permute-done.29
  136.1 1.9 %d_encodings.1 = bf16[8,16,896]{2,1,0:T(8,128)(2,1)} custom-call(s32[8]{0:T(128)S(1)} %select_reduce_fusion.1.slot, bf16[32,16,896]{2,1,0:T(8,128)(2,1)S(1)} %all-to-all-done.2.back, bf16[8,16,896]{2,1,0:T(8,128)(2,1)S(1)} %copy-done.5, f32[1,1,896]{2,1,0:T(1,128)S(1)} %reshape.94.gain), custom_call_target="tpu_custom_call" | custom-call | flops 2090000000 | tf_op jit(solution)/shard_map/d_encodings/pallas_call | solution.py:396
  138.0 0.8 multiply_convert_fusion
  (56 shorter events, 0.4 us)
Async XLA Ops:
  2.3 20.2 %all-to-all-start = ((s32[32,1,128]{2,1,0:T(1,128)}), s32[32,1,128]{2,1,0:T(1,128)S(1)}, u32[]{:S(2)}, u32[]{:S(2)}) async-start(s32[32,1,128]{2,1,0:T(1,128)} %broadcast_in_dim.46), calls=%async_computation | async-start | bytes 32768 | tf_op jit(solution)/shard_map/all_to_all | solution.py:442
  14.0 19.1 %collective-permute-start.10 = (bf16[256,512]{1,0:T(8,128)(2,1)}, bf16[256,512]{1,0:T(8,128)(2,1)S(1)}, u32[]{:S(2)}, u32[]{:S(2)}) collective-permute-start(bf16[256,512]{1,0:T(8,128)(2,1)} %tok.1), channel_id=1, source_target_pairs={{0,2},{1,3},{2,4},{3,5},{4,6},{5,7},{6,0},{7,1},{8,10},{9,11},{10,... | collective-permute-start | bytes 786440 | tf_op jit(solution)/shard_map/ppermute | solution.py:55
  15.6 17.5 %collective-permute-start.11 = (bf16[256,512]{1,0:T(8,128)(2,1)}, bf16[256,512]{1,0:T(8,128)(2,1)S(1)}, u32[]{:S(2)}, u32[]{:S(2)}) collective-permute-start(bf16[256,512]{1,0:T(8,128)(2,1)} %tok.1), channel_id=1, source_target_pairs={{0,4},{1,5},{2,6},{3,7},{4,0},{5,1},{6,2},{7,3},{8,12},{9,13},{10,... | collective-permute-start | bytes 786440 | tf_op jit(solution)/shard_map/ppermute | solution.py:55
  18.3 14.8 %collective-permute-start.12 = (bf16[256,512]{1,0:T(8,128)(2,1)}, bf16[256,512]{1,0:T(8,128)(2,1)S(1)}, u32[]{:S(2)}, u32[]{:S(2)}) collective-permute-start(bf16[256,512]{1,0:T(8,128)(2,1)} %tok.1), channel_id=1, source_target_pairs={{0,6},{1,7},{2,0},{3,1},{4,2},{5,3},{6,4},{7,5},{8,14},{9,15},{10,... | collective-permute-start | bytes 786440 | tf_op jit(solution)/shard_map/ppermute | solution.py:55
  22.5 0.9 copy-start.4
  23.4 9.7 %copy-start = (bf16[256,512]{1,0:T(8,128)(2,1)S(1)}, bf16[256,512]{1,0:T(8,128)(2,1)}, u32[]{:S(2)}) copy-start(bf16[256,512]{1,0:T(8,128)(2,1)} %tok.1) | copy-start | bytes 786436
  23.4 10.9 %copy-start.11 = (f32[4096]{0:T(1024)S(1)}, f32[4096]{0:T(1024)}, u32[]{:S(2)}) copy-start(f32[4096]{0:T(1024)} %param.13) | copy-start | bytes 49156
  23.4 11.0 %copy-start.3 = (bf16[256,512]{1,0:T(8,128)(2,1)S(1)}, bf16[256,512]{1,0:T(8,128)(2,1)}, u32[]{:S(2)}) copy-start(bf16[256,512]{1,0:T(8,128)(2,1)} %r_1_.2) | copy-start | bytes 786436
  25.3 31.6 %all-to-all-start.1 = ((bf16[32,16,896]{2,1,0:T(8,128)(2,1)}), bf16[32,16,896]{2,1,0:T(8,128)(2,1)S(1)}, u32[]{:S(2)}, u32[]{:S(2)}) async-start(bf16[32,16,896]{2,1,0:T(8,128)(2,1)} %outgoing_rows.1), calls=%async_computation.1 | async-start | bytes 1835008 | tf_op jit(solution)/shard_map/all_to_all | solution.py:455
  34.3 3.5 %collective-permute-start.13 = (bf16[4,256,512]{2,1,0:T(8,128)(2,1)}, bf16[4,256,512]{2,1,0:T(8,128)(2,1)S(1)}, u32[]{:S(2)}, u32[]{:S(2)}) collective-permute-start(bf16[4,256,512]{2,1,0:T(8,128)(2,1)} %pad_maximum_fusion), channel_id=1, source_target_pairs={{0,1},{1,0},{2,3},{3,2},{4,5},{5,4},{6,7},{7,6},{8,9},{9,8},{10,11... | collective-permute-start | bytes 3145736 | tf_op jit(solution)/shard_map/ppermute | solution.py:59
  34.4 15.7 %collective-permute-start.7 = (bf16[256,512]{1,0:T(8,128)(2,1)S(1)}, bf16[256,512]{1,0:T(8,128)(2,1)}, u32[]{:S(2)}, u32[]{:S(2)}) collective-permute-start(bf16[256,512]{1,0:T(8,128)(2,1)S(1)} %copy-done.3), channel_id=1, source_target_pairs={{0,2},{1,3},{2,4},{3,5},{4,6},{5,7},{6,0},{7,1},{8,10},{9,11},{10,... | collective-permute-start | bytes 786440 | tf_op jit(solution)/shard_map/ppermute | solution.py:55
  35.0 15.1 %collective-permute-start.8 = (bf16[256,512]{1,0:T(8,128)(2,1)S(1)}, bf16[256,512]{1,0:T(8,128)(2,1)}, u32[]{:S(2)}, u32[]{:S(2)}) collective-permute-start(bf16[256,512]{1,0:T(8,128)(2,1)S(1)} %copy-done.3), channel_id=1, source_target_pairs={{0,4},{1,5},{2,6},{3,7},{4,0},{5,1},{6,2},{7,3},{8,12},{9,13},{10,... | collective-permute-start | bytes 786440 | tf_op jit(solution)/shard_map/ppermute | solution.py:55
  35.9 14.8 %collective-permute-start.9 = (bf16[256,512]{1,0:T(8,128)(2,1)S(1)}, bf16[256,512]{1,0:T(8,128)(2,1)}, u32[]{:S(2)}, u32[]{:S(2)}) collective-permute-start(bf16[256,512]{1,0:T(8,128)(2,1)S(1)} %copy-done.3), channel_id=1, source_target_pairs={{0,6},{1,7},{2,0},{3,1},{4,2},{5,3},{6,4},{7,5},{8,14},{9,15},{10,... | collective-permute-start | bytes 786440 | tf_op jit(solution)/shard_map/ppermute | solution.py:55
  41.7 0.7 copy-start.8
  50.7 8.0 %collective-permute-start.14 = (bf16[256,512]{1,0:T(8,128)(2,1)S(1)}, bf16[256,512]{1,0:T(8,128)(2,1)S(1)}, u32[]{:S(2)}, u32[]{:S(2)}) collective-permute-start(bf16[256,512]{1,0:T(8,128)(2,1)S(1)} %copy-done.3), channel_id=1, source_target_pairs={{0,1},{1,0},{2,3},{3,2},{4,5},{5,4},{6,7},{7,6},{8,9},{9,8},{10,11... | collective-permute-start | bytes 786440 | tf_op jit(solution)/shard_map/ppermute | solution.py:59
  50.7 9.2 %collective-permute-start.15 = (bf16[256,512]{1,0:T(8,128)(2,1)}, bf16[256,512]{1,0:T(8,128)(2,1)S(1)}, u32[]{:S(2)}, u32[]{:S(2)}) collective-permute-start(bf16[256,512]{1,0:T(8,128)(2,1)} %collective-permute-done.7.r_2_), channel_id=1, source_target_pairs={{0,1},{1,0},{2,3},{3,2},{4,5},{5,4},{6,7},{7,6},{8,9},{9,8},{10,11... | collective-permute-start | bytes 786440 | tf_op jit(solution)/shard_map/ppermute | solution.py:59
  51.2 10.4 %collective-permute-start.16 = (bf16[256,512]{1,0:T(8,128)(2,1)}, bf16[256,512]{1,0:T(8,128)(2,1)S(1)}, u32[]{:S(2)}, u32[]{:S(2)}) collective-permute-start(bf16[256,512]{1,0:T(8,128)(2,1)} %collective-permute-done.8.r_3_), channel_id=1, source_target_pairs={{0,1},{1,0},{2,3},{3,2},{4,5},{5,4},{6,7},{7,6},{8,9},{9,8},{10,11... | collective-permute-start | bytes 786440 | tf_op jit(solution)/shard_map/ppermute | solution.py:59
  51.2 17.8 %collective-permute-start.17 = (bf16[256,512]{1,0:T(8,128)(2,1)}, bf16[256,512]{1,0:T(8,128)(2,1)S(1)}, u32[]{:S(2)}, u32[]{:S(2)}) collective-permute-start(bf16[256,512]{1,0:T(8,128)(2,1)} %collective-permute-done.9.r_4_), channel_id=1, source_target_pairs={{0,1},{1,0},{2,3},{3,2},{4,5},{5,4},{6,7},{7,6},{8,9},{9,8},{10,11... | collective-permute-start | bytes 786440 | tf_op jit(solution)/shard_map/ppermute | solution.py:59
  57.9 15.5 %copy-start.1 = (bf16[896,512]{1,0:T(8,128)(2,1)S(1)}, bf16[896,512]{1,0:T(8,128)(2,1)}, u32[]{:S(2)}) copy-start(bf16[896,512]{1,0:T(8,128)(2,1)} %r_10_.1) | copy-start | bytes 2752516
  57.9 15.5 %copy-start.2 = (bf16[896,512]{1,0:T(8,128)(2,1)S(1)}, bf16[896,512]{1,0:T(8,128)(2,1)}, u32[]{:S(2)}) copy-start(bf16[896,512]{1,0:T(8,128)(2,1)} %r_11_.1) | copy-start | bytes 2752516
  58.0 15.5 %copy-start.9 = (bf16[256,512]{1,0:T(8,128)(2,1)S(1)}, bf16[256,512]{1,0:T(8,128)(2,1)}, u32[]{:S(2)}) copy-start(bf16[256,512]{1,0:T(8,128)(2,1)} %copy-done.8) | copy-start | bytes 786436
  58.0 10.3 %collective-permute-start = (bf16[128,896]{1,0:T(8,128)(2,1)S(1)}, bf16[128,896]{1,0:T(8,128)(2,1)S(1)}, u32[]{:S(2)}, u32[]{:S(2)}) collective-permute-start(bf16[128,896]{1,0:T(8,128)(2,1)S(1)} %bitcast.16), channel_id=1, source_target_pairs={{0,2},{1,3},{2,4},{3,5},{4,6},{5,7},{6,0},{7,1},{8,10},{9,11},{10,... | collective-permute-start | bytes 688136 | tf_op jit(solution)/shard_map/ppermute | solution.py:55
  58.6 9.7 %collective-permute-start.1 = (bf16[128,896]{1,0:T(8,128)(2,1)S(1)}, bf16[128,896]{1,0:T(8,128)(2,1)S(1)}, u32[]{:S(2)}, u32[]{:S(2)}) collective-permute-start(bf16[128,896]{1,0:T(8,128)(2,1)S(1)} %bitcast.17), channel_id=1, source_target_pairs={{0,4},{1,5},{2,6},{3,7},{4,0},{5,1},{6,2},{7,3},{8,12},{9,13},{10,... | collective-permute-start | bytes 688136 | tf_op jit(solution)/shard_map/ppermute | solution.py:55
  59.9 9.1 %collective-permute-start.2 = (bf16[128,896]{1,0:T(8,128)(2,1)S(1)}, bf16[128,896]{1,0:T(8,128)(2,1)S(1)}, u32[]{:S(2)}, u32[]{:S(2)}) collective-permute-start(bf16[128,896]{1,0:T(8,128)(2,1)S(1)} %bitcast.18), channel_id=1, source_target_pairs={{0,6},{1,7},{2,0},{3,1},{4,2},{5,3},{6,4},{7,5},{8,14},{9,15},{10,... | collective-permute-start | bytes 688136 | tf_op jit(solution)/shard_map/ppermute | solution.py:55
  61.6 11.8 %collective-permute-start.3 = (bf16[128,896]{1,0:T(8,128)(2,1)S(1)}, bf16[128,896]{1,0:T(8,128)(2,1)S(1)}, u32[]{:S(2)}, u32[]{:S(2)}) collective-permute-start(bf16[128,896]{1,0:T(8,128)(2,1)S(1)} %bitcast.19), channel_id=1, source_target_pairs={{0,1},{1,0},{2,3},{3,2},{4,5},{5,4},{6,7},{7,6},{8,9},{9,8},{10,11... | collective-permute-start | bytes 688136 | tf_op jit(solution)/shard_map/ppermute | solution.py:59
  68.3 5.1 %collective-permute-start.4 = (bf16[128,896]{1,0:T(8,128)(2,1)S(1)}, bf16[128,896]{1,0:T(8,128)(2,1)S(1)}, u32[]{:S(2)}, u32[]{:S(2)}) collective-permute-start(bf16[128,896]{1,0:T(8,128)(2,1)S(1)} %collective-permute-done.r_1_), channel_id=1, source_target_pairs={{0,1},{1,0},{2,3},{3,2},{4,5},{5,4},{6,7},{7,6},{8,9},{9,8},{10,11... | collective-permute-start | bytes 688136 | tf_op jit(solution)/shard_map/ppermute | solution.py:59
  68.3 5.1 %collective-permute-start.5 = (bf16[128,896]{1,0:T(8,128)(2,1)S(1)}, bf16[128,896]{1,0:T(8,128)(2,1)S(1)}, u32[]{:S(2)}, u32[]{:S(2)}) collective-permute-start(bf16[128,896]{1,0:T(8,128)(2,1)S(1)} %collective-permute-done.1.r_2_), channel_id=1, source_target_pairs={{0,1},{1,0},{2,3},{3,2},{4,5},{5,4},{6,7},{7,6},{8,9},{9,8},{10,11... | collective-permute-start | bytes 688136 | tf_op jit(solution)/shard_map/ppermute | solution.py:59
  69.0 4.4 %collective-permute-start.6 = (bf16[128,896]{1,0:T(8,128)(2,1)S(1)}, bf16[128,896]{1,0:T(8,128)(2,1)S(1)}, u32[]{:S(2)}, u32[]{:S(2)}) collective-permute-start(bf16[128,896]{1,0:T(8,128)(2,1)S(1)} %collective-permute-done.2.r_3_), channel_id=1, source_target_pairs={{0,1},{1,0},{2,3},{3,2},{4,5},{5,4},{6,7},{7,6},{8,9},{9,8},{10,11... | collective-permute-start | bytes 688136 | tf_op jit(solution)/shard_map/ppermute | solution.py:59
  80.4 2.7 %collective-permute-start.18 = (bf16[4,128,896]{2,1,0:T(8,128)(2,1)S(1)}, bf16[4,128,896]{2,1,0:T(8,128)(2,1)S(1)}, u32[]{:S(2)}, u32[]{:S(2)}) collective-permute-start(bf16[4,128,896]{2,1,0:T(8,128)(2,1)S(1)} %get-tuple-element.46), channel_id=1, source_target_pairs={{0,1},{1,0},{2,3},{3,2},{4,5},{5,4},{6,7},{7,6},{8,9},{9,8},{10,11... | collective-permute-start | bytes 2752520 | tf_op jit(solution)/shard_map/ppermute | solution.py:59
  83.3 13.0 %collective-permute-start.19 = (bf16[128,896]{1,0:T(8,128)(2,1)S(1)}, bf16[128,896]{1,0:T(8,128)(2,1)S(1)}, u32[]{:S(2)}, u32[]{:S(2)}) collective-permute-start(bf16[128,896]{1,0:T(8,128)(2,1)S(1)} %get-tuple-element.55), channel_id=1, source_target_pairs={{0,6},{1,7},{2,0},{3,1},{4,2},{5,3},{6,4},{7,5},{8,14},{9,15},{10,... | collective-permute-start | bytes 688136 | tf_op jit(solution)/shard_map/ppermute | solution.py:81
  86.0 10.3 %collective-permute-start.20 = (bf16[128,896]{1,0:T(8,128)(2,1)S(1)}, bf16[128,896]{1,0:T(8,128)(2,1)S(1)}, u32[]{:S(2)}, u32[]{:S(2)}) collective-permute-start(bf16[128,896]{1,0:T(8,128)(2,1)S(1)} %get-tuple-element.56), channel_id=1, source_target_pairs={{0,4},{1,5},{2,6},{3,7},{4,0},{5,1},{6,2},{7,3},{8,12},{9,13},{10,... | collective-permute-start | bytes 688136 | tf_op jit(solution)/shard_map/ppermute | solution.py:81
  86.0 13.7 %collective-permute-start.21 = (bf16[128,896]{1,0:T(8,128)(2,1)S(1)}, bf16[128,896]{1,0:T(8,128)(2,1)S(1)}, u32[]{:S(2)}, u32[]{:S(2)}) collective-permute-start(bf16[128,896]{1,0:T(8,128)(2,1)S(1)} %get-tuple-element.57), channel_id=1, source_target_pairs={{0,2},{1,3},{2,4},{3,5},{4,6},{5,7},{6,0},{7,1},{8,10},{9,11},{10,... | collective-permute-start | bytes 688136 | tf_op jit(solution)/shard_map/ppermute | solution.py:81
  91.0 1.0 copy-start.6
  99.7 9.8 %collective-permute-start.22 = (bf16[4,256,512]{2,1,0:T(8,128)(2,1)S(1)}, bf16[4,256,512]{2,1,0:T(8,128)(2,1)}, u32[]{:S(2)}, u32[]{:S(2)}) collective-permute-start(bf16[4,256,512]{2,1,0:T(8,128)(2,1)S(1)} %get-tuple-element.58), channel_id=1, source_target_pairs={{0,1},{1,0},{2,3},{3,2},{4,5},{5,4},{6,7},{7,6},{8,9},{9,8},{10,11... | collective-permute-start | bytes 3145736 | tf_op jit(solution)/shard_map/ppermute | solution.py:59
  101.4 34.6 %copy-start.5 = (bf16[8,16,896]{2,1,0:T(8,128)(2,1)S(1)}, bf16[8,16,896]{2,1,0:T(8,128)(2,1)}, u32[]{:S(2)}) copy-start(bf16[8,16,896]{2,1,0:T(8,128)(2,1)} %enc.3) | copy-start | bytes 688132
  101.4 34.6 %all-to-all-start.2 = ((bf16[32,16,896]{2,1,0:T(8,128)(2,1)}), bf16[32,16,896]{2,1,0:T(8,128)(2,1)S(1)}, u32[]{:S(2)}, u32[]{:S(2)}) async-start(bf16[32,16,896]{2,1,0:T(8,128)(2,1)} %placed_grads.1), calls=%async_computation.2 | async-start | bytes 1835008 | tf_op jit(solution)/shard_map/all_to_all | solution.py:471
  109.5 1.2 copy-start.7
  112.2 9.3 %collective-permute-start.23 = (bf16[256,512]{1,0:T(8,128)(2,1)S(1)}, bf16[256,512]{1,0:T(8,128)(2,1)S(1)}, u32[]{:S(2)}, u32[]{:S(2)}) collective-permute-start(bf16[256,512]{1,0:T(8,128)(2,1)S(1)} %get-tuple-element.60), channel_id=1, source_target_pairs={{0,6},{1,7},{2,0},{3,1},{4,2},{5,3},{6,4},{7,5},{8,14},{9,15},{10,... | collective-permute-start | bytes 786440 | tf_op jit(solution)/shard_map/ppermute | solution.py:81
  113.2 10.8 %collective-permute-start.24 = (bf16[256,512]{1,0:T(8,128)(2,1)S(1)}, bf16[256,512]{1,0:T(8,128)(2,1)S(1)}, u32[]{:S(2)}, u32[]{:S(2)}) collective-permute-start(bf16[256,512]{1,0:T(8,128)(2,1)S(1)} %get-tuple-element.61), channel_id=1, source_target_pairs={{0,4},{1,5},{2,6},{3,7},{4,0},{5,1},{6,2},{7,3},{8,12},{9,13},{10,... | collective-permute-start | bytes 786440 | tf_op jit(solution)/shard_map/ppermute | solution.py:81
  113.4 14.7 %collective-permute-start.25 = (bf16[256,512]{1,0:T(8,128)(2,1)S(1)}, bf16[256,512]{1,0:T(8,128)(2,1)S(1)}, u32[]{:S(2)}, u32[]{:S(2)}) collective-permute-start(bf16[256,512]{1,0:T(8,128)(2,1)S(1)} %get-tuple-element.62), channel_id=1, source_target_pairs={{0,2},{1,3},{2,4},{3,5},{4,6},{5,7},{6,0},{7,1},{8,10},{9,11},{10,... | collective-permute-start | bytes 786440 | tf_op jit(solution)/shard_map/ppermute | solution.py:81
  129.1 8.9 %copy-start.10 = (bf16[256,512]{1,0:T(8,128)(2,1)S(1)}, bf16[256,512]{1,0:T(8,128)(2,1)}, u32[]{:S(2)}) copy-start(bf16[256,512]{1,0:T(8,128)(2,1)} %get-tuple-element.34) | copy-start | bytes 786436
  129.2 1.2 collective-permute-start.26
  130.4 4.8 %collective-permute-start.27 = (f32[256]{0:T(256)S(1)}, f32[256]{0:T(256)S(1)}, u32[]{:S(2)}, u32[]{:S(2)}) collective-permute-start(f32[256]{0:T(256)S(1)} %add.58), channel_id=1, source_target_pairs={{0,2},{1,3},{2,4},{3,5},{4,6},{5,7},{6,0},{7,1},{8,10},{9,11},{10,... | collective-permute-start | bytes 3080 | tf_op jit(solution)/shard_map/ppermute | solution.py:479
  130.4 5.1 %collective-permute-start.28 = (f32[256]{0:T(256)S(1)}, f32[256]{0:T(256)S(1)}, u32[]{:S(2)}, u32[]{:S(2)}) collective-permute-start(f32[256]{0:T(256)S(1)} %add.58), channel_id=1, source_target_pairs={{0,4},{1,5},{2,6},{3,7},{4,0},{5,1},{6,2},{7,3},{8,12},{9,13},{10,... | collective-permute-start | bytes 3080 | tf_op jit(solution)/shard_map/ppermute | solution.py:479
  132.5 3.6 %collective-permute-start.29 = (f32[256]{0:T(256)S(1)}, f32[256]{0:T(256)S(1)}, u32[]{:S(2)}, u32[]{:S(2)}) collective-permute-start(f32[256]{0:T(256)S(1)} %add.58), channel_id=1, source_target_pairs={{0,6},{1,7},{2,0},{3,1},{4,2},{5,3},{6,4},{7,5},{8,14},{9,15},{10,... | collective-permute-start | bytes 3080 | tf_op jit(solution)/shard_map/ppermute | solution.py:479

commit v5 on v4

--- a/solution.py
+++ b/solution.py
@@ -141,7 +141,7 @@
         out_specs=vmem(),
         scratch_shapes=[pltpu.VMEM((count, share, cols), BF16), pltpu.SemaphoreType.DMA((count,))],
         compiler_params=params(48),
-        cost_estimate=cost(4.5),
+        cost_estimate=cost(3.4),
         name="queries",
     )(src, *pieces, gain.reshape(count, share), w_query)
 
@@ -174,7 +174,7 @@
         out_specs=vmem(),
         scratch_shapes=[pltpu.VMEM((count, cols, share), BF16), pltpu.SemaphoreType.DMA((count,))],
         compiler_params=params(48),
-        cost_estimate=cost(4.5),
+        cost_estimate=cost(3.4),
         name="d_attended",
     )(src, *pieces, w_out)
 
@@ -285,25 +285,39 @@
     )(*pieces, q, d, w_key, w_value)
 
 
-def outgoing_kernel(req, enc, gain, out, normed):
+def normed_kernel(enc, gain, out):
     wide = enc[...].astype(F32)
-    normed[...] = (wide * rms_scale(wide) * gain[...]).astype(BF16)
+    out[...] = (wide * rms_scale(wide) * gain[...]).astype(BF16)
+
+
+def run_normed(encodings, gain):
+    return pl.pallas_call(
+        normed_kernel,
+        out_shape=jax.ShapeDtypeStruct(encodings.shape, BF16),
+        in_specs=[vmem(), vmem()],
+        out_specs=vmem(),
+        compiler_params=params(8),
+        cost_estimate=cost(0.1),
+        name="normed_rows",
+    )(encodings, gain.reshape(1, 1, -1))
+
+
+def outgoing_kernel(req, normed, out):
     for s in range(out.shape[0]):
         out[s] = normed[jnp.maximum(req[s, 0], 0)]
 
 
-def run_outgoing(requested, encodings, gain):
+def run_outgoing(requested, normed):
     slots = requested.shape[0]
     return pl.pallas_call(
         outgoing_kernel,
-        out_shape=jax.ShapeDtypeStruct((slots,) + encodings.shape[1:], BF16),
-        in_specs=[smem(), vmem(), vmem()],
-        out_specs=vmem(),
-        scratch_shapes=[pltpu.VMEM(encodings.shape, BF16)],
-        compiler_params=params(12),
-        cost_estimate=cost(1.7),
+        out_shape=jax.ShapeDtypeStruct((slots,) + normed.shape[1:], BF16),
+        in_specs=[smem(), vmem()],
+        out_specs=vmem(),
+        compiler_params=params(8),
+        cost_estimate=cost(0.1),
         name="outgoing_rows",
-    )(requested, encodings, gain.reshape(1, 1, -1))
+    )(requested, normed)
 
 
 def pick_kernel(owner, rows, out, sems):
@@ -325,7 +339,7 @@
         out_specs=vmem(),
         scratch_shapes=[pltpu.SemaphoreType.DMA((n,))],
         compiler_params=params(),
-        cost_estimate=cost(4.5),
+        cost_estimate=cost(3.4),
         name="picked_rows",
     )(owner, rows)
 
@@ -450,7 +464,7 @@
     slot = jnp.sum(jnp.where(serves, slots[:, None], 0), axis=0)
 
     tok_own = over_chips(tokens, count)
-    outgoing = run_outgoing(requested, encodings, gain_enc)
+    outgoing = run_outgoing(requested, run_normed(encodings, gain_enc))
     outgoing, cot_in = lax.optimization_barrier((outgoing, cotangent))
     incoming = lax.all_to_all(outgoing, "dp", split_axis=0, concat_axis=0, tiled=True)
     cot_own = over_chips(cot_in, count)
@@ -459,6 +473,8 @@
     d = run_back(src, cot_own + [swap(p, count) for p in cot_own], w_out)
     picked = run_pick(owner, incoming).reshape(readings * own_tokens, width)
     row_own = over_chips(picked, count)
+    crossed, d = lax.optimization_barrier((row_own[1:], d))
+    row_own = [picked] + crossed
     rows = row_own + [swap(p, count) for p in row_own]
     send, keep, att = run_attention(rows, q, d, w_key, w_value, blocks)
     pair = pair_sum(keep, swap(send, count))

time: 140 us -> 140 us (level)
  waiting for transfers between devices: 48.7 us -> 44.3 us
  starting transfers between devices: 51.4 us -> 53.1 us
  local copies, waits for them, and re-layouts: 6.99 us -> 8.68 us
    ppermute x9, waiting for transfers between devices: 15.2 us -> 11.2 us  [over_chips(): lax.ppermute(x, 'mp', chip_shift(count, k))]
    ppermute x12, waiting for transfers between devices: 3.14 us -> 4.94 us  [swap(): return lax.ppermute(x, 'mp', core_swap(count))]
    unnamed x25 -> x29, local copies, waits for them, and re-layouts: 4.64 us -> 6.33 us
  transfers between devices with their start and end apart: 33 -> 33, of which waited for: 16 -> 19; matrix products, arithmetic and copies ran while one was open for 2% -> 3% of each run, Pallas kernels for 14% -> 14%
where the time goes in v5:
time: 140 us; the launch traced here: 139 us
  starting transfers between devices  53.1 us (38%)
  waiting for transfers between devices  44.3 us (32%)
  Pallas kernels  28.5 us (20%)
  local copies, waits for them, and re-layouts  8.68 us (6%)
  other arithmetic  3.34 us (2%)
    ppermute x6, waiting for transfers between devices, pair_shares(): lax.ppermute(pair[k], 'mp', chip_shift(count, -k))  20.6 us
    ppermute x9, starting transfers between devices, over_chips(): lax.ppermute(x, 'mp', chip_shift(count, k))  12.7 us
    all_to_all x1, starting transfers between devices, shards(): lax.all_to_all(jnp.broadcast_to(wanted[:, None], (dp_count, IDS_WIDTH)),...  11.7 us
    ppermute x9, waiting for transfers between devices, over_chips(): lax.ppermute(x, 'mp', chip_shift(count, k))  11.2 us
    all_to_all x1, starting transfers between devices, shards(): lax.all_to_all(back_out, 'dp', split_axis=0, concat_axis=0, tiled=True)  8.97 us
    all_to_all x1, starting transfers between devices, shards(): lax.all_to_all(outgoing, 'dp', split_axis=0, concat_axis=0, tiled=True)  8.85 us
    pallas_call x1, Pallas kernels, run_attention(): pl.pallas_call(lambda *r: attention_kernel(count, blocks, *r), out_shape=...  6.98 us
    unnamed x29, local copies, waits for them, and re-layouts  6.33 us
  transfers between devices with their start and end apart: 33, of which 19 were waited for; matrix products, arithmetic and copies ran while one was open for 3% of the time, Pallas kernels for 14%

profile of v5, /device:TPU:8, one launch (start us, length us, event | category | flops | bytes accessed | tf_op | source)
XLA Modules:
  0.0 138.8 jit_solution(2487501930381575610)
XLA Ops:
  0.6 0.8 copy.17
  1.6 0.7 broadcast_in_dim.46
  2.4 11.7 %all-to-all-start = ((s32[32,1,128]{2,1,0:T(1,128)}), s32[32,1,128]{2,1,0:T(1,128)S(1)}, u32[]{:S(2)}, u32[]{:S(2)}) async-start(s32[32,1,128]{2,1,0:T(1,128)} %broadcast_in_dim.46), calls=%async_computation | async-start | bytes 32768 | tf_op jit(solution)/shard_map/all_to_all | solution.py:456
  14.1 1.6 %collective-permute-start.6 = (bf16[256,512]{1,0:T(8,128)(2,1)}, bf16[256,512]{1,0:T(8,128)(2,1)S(1)}, u32[]{:S(2)}, u32[]{:S(2)}) collective-permute-start(bf16[256,512]{1,0:T(8,128)(2,1)} %tok.1), channel_id=1, source_target_pairs={{0,2},{1,3},{2,4},{3,5},{4,6},{5,7},{6,0},{7,1},{8,10},{9,11},{10,... | collective-permute-start | bytes 786440 | tf_op jit(solution)/shard_map/ppermute | solution.py:55
  15.6 2.7 %collective-permute-start.7 = (bf16[256,512]{1,0:T(8,128)(2,1)}, bf16[256,512]{1,0:T(8,128)(2,1)S(1)}, u32[]{:S(2)}, u32[]{:S(2)}) collective-permute-start(bf16[256,512]{1,0:T(8,128)(2,1)} %tok.1), channel_id=1, source_target_pairs={{0,4},{1,5},{2,6},{3,7},{4,0},{5,1},{6,2},{7,3},{8,12},{9,13},{10,... | collective-permute-start | bytes 786440 | tf_op jit(solution)/shard_map/ppermute | solution.py:55
  18.4 1.4 %collective-permute-start.8 = (bf16[256,512]{1,0:T(8,128)(2,1)}, bf16[256,512]{1,0:T(8,128)(2,1)S(1)}, u32[]{:S(2)}, u32[]{:S(2)}) collective-permute-start(bf16[256,512]{1,0:T(8,128)(2,1)} %tok.1), channel_id=1, source_target_pairs={{0,6},{1,7},{2,0},{3,1},{4,2},{5,3},{6,4},{7,5},{8,14},{9,15},{10,... | collective-permute-start | bytes 786440 | tf_op jit(solution)/shard_map/ppermute | solution.py:55
  19.8 0.7 reshape.94.gain
  20.5 0.9 copy-done.1
  21.6 0.9 all-to-all-done
  22.5 1.8 %outgoing_rows.1 = bf16[32,16,896]{2,1,0:T(8,128)(2,1)} custom-call(s32[32,128]{1,0:T(8,128)S(1)} %bitcast.14, bf16[8,16,896]{2,1,0:T(8,128)(2,1)S(1)} %normed_rows.1.normed), custom_call_target="tpu_custom_call" | custom-call | flops 110000000 | tf_op jit(solution)/shard_map/outgoing_rows/pallas_call | solution.py:312
  24.3 8.9 %all-to-all-start.1 = ((bf16[32,16,896]{2,1,0:T(8,128)(2,1)}), bf16[32,16,896]{2,1,0:T(8,128)(2,1)S(1)}, u32[]{:S(2)}, u32[]{:S(2)}) async-start(bf16[32,16,896]{2,1,0:T(8,128)(2,1)} %outgoing_rows.1), calls=%async_computation.1 | async-start | bytes 1835008 | tf_op jit(solution)/shard_map/all_to_all | solution.py:469
  33.2 2.1 %pad_maximum_fusion = bf16[4,256,512]{2,1,0:T(8,128)(2,1)} fusion(bf16[1,256,512]{2,1,0:T(8,128)(2,1)S(1)} %bitcast.13, bf16[1,256,512]{2,1,0:T(8,128)(2,1)S(1)} %bitcast.12, bf16[1,256,512]{2,1,0:T(8,128)(2,1)S(1)} %bitcast.11, bf16[1,256,512]{2,1,0:T(8,128)(2,1)} %bitcast.10), kind=kLoop, calls=%fused_computation | loop fusion | flops 1572864 | bytes 2097152 | tf_op jit(solution)/shard_map/stack | solution.py:471
  35.4 0.6 collective-permute-start.3
  36.0 0.9 collective-permute-start.4
  36.9 1.9 %collective-permute-start.5 = (bf16[256,512]{1,0:T(8,128)(2,1)S(1)}, bf16[256,512]{1,0:T(8,128)(2,1)}, u32[]{:S(2)}, u32[]{:S(2)}) collective-permute-start(bf16[256,512]{1,0:T(8,128)(2,1)S(1)} %copy-done.5), channel_id=1, source_target_pairs={{0,6},{1,7},{2,0},{3,1},{4,2},{5,3},{6,4},{7,5},{8,14},{9,15},{10,... | collective-permute-start | bytes 786440 | tf_op jit(solution)/shard_map/ppermute | solution.py:55
  38.8 3.9 %queries.1.r_8_ = bf16[256,512]{1,0:T(8,128)(2,1)S(1)} custom-call(s32[8]{0:T(128)S(1)} %pad_add_fusion.r_0_, bf16[256,512]{1,0:T(8,128)(2,1)S(1)} %copy-done, bf16[256,512]{1,0:T(8,128)(2,1)S(1)} %collective-permute-done.6.r_2_, bf16[256,512]{1,0:T(8,128)(2,1)S(1)} %collective-permute-done.7.r_3_, bf16[256,512]{1,0:T(8,128)(2,1)S(1)} %collective-permute-done.8.r_4_, ...), custom_call_target="tpu_custom_call" | custom-call | flops 3740000000 | tf_op jit(solution)/shard_map/queries/pallas_call | solution.py:137
  42.7 0.7 copy-done.10
  43.4 7.6 %collective-permute-done.3.r_2_ = bf16[256,512]{1,0:T(8,128)(2,1)} collective-permute-done((bf16[256,512]{1,0:T(8,128)(2,1)S(1)}, bf16[256,512]{1,0:T(8,128)(2,1)}, u32[]{:S(2)}, u32[]{:S(2)}) %collective-permute-start.3) | collective-permute-done | bytes 262176 | tf_op jit(solution)/shard_map/ppermute | solution.py:55
  51.1 0.6 collective-permute-done.5.r_4_
  51.7 0.5 collective-permute-start.11
  52.2 0.5 collective-permute-start.13
  52.7 4.3 %all-to-all-done.1.rows = bf16[32,16,896]{2,1,0:T(8,128)(2,1)S(1)} async-done(((bf16[32,16,896]{2,1,0:T(8,128)(2,1)}), bf16[32,16,896]{2,1,0:T(8,128)(2,1)S(1)}, u32[]{:S(2)}, u32[]{:S(2)}) %all-to-all-start.1) | async-done | bytes 917536 | tf_op jit(solution)/shard_map/all_to_all | solution.py:469
  57.0 1.0 picked_rows.1
  58.0 0.7 collective-permute-start
  58.7 1.2 collective-permute-start.1
  59.8 1.8 %collective-permute-start.2 = (bf16[128,896]{1,0:T(8,128)(2,1)S(1)}, bf16[128,896]{1,0:T(8,128)(2,1)S(1)}, u32[]{:S(2)}, u32[]{:S(2)}) collective-permute-start(bf16[128,896]{1,0:T(8,128)(2,1)S(1)} %bitcast.18), channel_id=1, source_target_pairs={{0,6},{1,7},{2,0},{3,1},{4,2},{5,3},{6,4},{7,5},{8,14},{9,15},{10,... | collective-permute-start | bytes 688136 | tf_op jit(solution)/shard_map/ppermute | solution.py:55
  61.6 4.4 %d_attended.1.r_9_ = bf16[256,512]{1,0:T(8,128)(2,1)S(1)} custom-call(s32[8]{0:T(128)S(1)} %pad_add_fusion.r_0_, bf16[256,512]{1,0:T(8,128)(2,1)S(1)} %copy-done.5, bf16[256,512]{1,0:T(8,128)(2,1)} %collective-permute-done.3.r_2_, bf16[256,512]{1,0:T(8,128)(2,1)} %collective-permute-done.4.r_3_, bf16[256,512]{1,0:T(8,128)(2,1)} %collective-permute-done.5.r_4_, ...), custom_call_target="tpu_custom_call" | custom-call | flops 3740000000 | tf_op jit(solution)/shard_map/d_attended/pallas_call | solution.py:170
  66.1 2.7 %collective-permute-done.r_1_ = bf16[128,896]{1,0:T(8,128)(2,1)S(1)} collective-permute-done((bf16[128,896]{1,0:T(8,128)(2,1)S(1)}, bf16[128,896]{1,0:T(8,128)(2,1)S(1)}, u32[]{:S(2)}, u32[]{:S(2)}) %collective-permute-start) | collective-permute-done | bytes 229408 | tf_op jit(solution)/shard_map/ppermute | solution.py:55
  69.0 0.5 collective-permute-start.16
  69.5 1.0 collective-permute-done.15.r_5_
  70.5 0.3 collective-permute-done.16.r_6_
  70.8 0.3 collective-permute-done.17.r_7_
  71.2 7.0 %attention.1 = (bf16[4,128,896]{2,1,0:T(8,128)(2,1)S(1)}, bf16[4,128,896]{2,1,0:T(8,128)(2,1)S(1)}, bf16[256,512]{1,0:T(8,128)(2,1)S(1)}) custom-call(bf16[128,896]{1,0:T(8,128)(2,1)S(1)} %bitcast.20, bf16[128,896]{1,0:T(8,128)(2,1)S(1)} %collective-permute-done.r_1_, bf16[128,896]{1,0:T(8,128)(2,1)S(1)} %collective-permute-done.1.r_2_, ...), custom_call_target="tpu_custom_call" | custom-call | flops 9900000256 | tf_op jit(solution)/shard_map/attention/pallas_call | solution.py:275
  78.2 0.3 collective-permute-start.18
  78.4 2.3 %collective-permute-done.18.other = bf16[4,128,896]{2,1,0:T(8,128)(2,1)S(1)} collective-permute-done((bf16[4,128,896]{2,1,0:T(8,128)(2,1)S(1)}, bf16[4,128,896]{2,1,0:T(8,128)(2,1)S(1)}, u32[]{:S(2)}, u32[]{:S(2)}) %collective-permute-start.18) | collective-permute-done | bytes 917536 | tf_op jit(solution)/shard_map/ppermute | solution.py:59
  80.7 0.2 pair_sums.2
  81.0 2.6 %collective-permute-start.19 = (bf16[128,896]{1,0:T(8,128)(2,1)S(1)}, bf16[128,896]{1,0:T(8,128)(2,1)S(1)}, u32[]{:S(2)}, u32[]{:S(2)}) collective-permute-start(bf16[128,896]{1,0:T(8,128)(2,1)S(1)} %get-tuple-element.63), channel_id=1, source_target_pairs={{0,6},{1,7},{2,0},{3,1},{4,2},{5,3},{6,4},{7,5},{8,14},{9,15},{10,... | collective-permute-start | bytes 688136 | tf_op jit(solution)/shard_map/ppermute | solution.py:81
  83.6 1.0 collective-permute-start.21
  84.6 4.1 %branches.1 = (bf16[4,256,512]{2,1,0:T(8,128)(2,1)S(1)}, bf16[4,256,512]{2,1,0:T(8,128)(2,1)S(1)}) custom-call(s32[8]{0:T(128)S(1)} %pad_add_fusion.r_0_, bf16[256,512]{1,0:T(8,128)(2,1)S(1)} %get-tuple-element.59.r_1_, bf16[512,4096]{1,0:T(8,128)(2,1)} %r_2_.1), custom_call_target="tpu_custom_call" | custom-call | flops 4400000000 | tf_op jit(solution)/shard_map/branches/pallas_call | solution.py:203
  88.7 1.0 copy-done.6
  89.6 4.1 %collective-permute-done.19 = bf16[128,896]{1,0:T(8,128)(2,1)S(1)} collective-permute-done((bf16[128,896]{1,0:T(8,128)(2,1)S(1)}, bf16[128,896]{1,0:T(8,128)(2,1)S(1)}, u32[]{:S(2)}, u32[]{:S(2)}) %collective-permute-start.19) | collective-permute-done | bytes 229408 | tf_op jit(solution)/shard_map/ppermute | solution.py:81
  93.8 3.4 %collective-permute-done.21 = bf16[128,896]{1,0:T(8,128)(2,1)S(1)} collective-permute-done((bf16[128,896]{1,0:T(8,128)(2,1)S(1)}, bf16[128,896]{1,0:T(8,128)(2,1)S(1)}, u32[]{:S(2)}, u32[]{:S(2)}) %collective-permute-start.21) | collective-permute-done | bytes 229408 | tf_op jit(solution)/shard_map/ppermute | solution.py:81
  97.1 1.7 %placed_grads.1 = bf16[32,16,896]{2,1,0:T(8,128)(2,1)} custom-call(s32[32]{0:T(128)S(1)} %get-tuple-element.79.reading, bf16[8,16,896]{2,1,0:T(8,128)(2,1)S(1)} %bitcast.24, bf16[8,16,896]{2,1,0:T(8,128)(2,1)S(1)} %bitcast.21, bf16[8,16,896]{2,1,0:T(8,128)(2,1)S(1)} %bitcast.22, bf16[8,16,896]{2,1,0:T(8,128)(2,1)S(1)} %bitcast.23), custom_call_target="tpu_custom_call" | custom-call | flops 1870000000 | tf_op jit(solution)/shard_map/placed_grads/pallas_call | solution.py:357
  98.9 9.0 %all-to-all-start.2 = ((bf16[32,16,896]{2,1,0:T(8,128)(2,1)}), bf16[32,16,896]{2,1,0:T(8,128)(2,1)S(1)}, u32[]{:S(2)}, u32[]{:S(2)}) async-start(bf16[32,16,896]{2,1,0:T(8,128)(2,1)} %placed_grads.1), calls=%async_computation.2 | async-start | bytes 1835008 | tf_op jit(solution)/shard_map/all_to_all | solution.py:487
  107.9 1.2 copy-done.7
  109.1 1.5 %pair_sums.3 = (bf16[256,512]{1,0:T(8,128)(2,1)S(1)}, bf16[256,512]{1,0:T(8,128)(2,1)S(1)}, bf16[256,512]{1,0:T(8,128)(2,1)S(1)}, bf16[256,512]{1,0:T(8,128)(2,1)S(1)}) custom-call(bf16[4,256,512]{2,1,0:T(8,128)(2,1)S(1)} %copy-done.7, bf16[4,256,512]{2,1,0:T(8,128)(2,1)} %collective-permute-done.22.other), custom_call_target="tpu_custom_call" | custom-call | flops 770000000 | tf_op jit(solution)/shard_map/pair_sums/pallas_call | solution.py:68
  110.6 0.7 copy-done.8
  111.3 0.9 collective-permute-start.23
  112.2 0.3 collective-permute-start.24
  112.5 0.8 collective-permute-start.25
  113.3 0.8 dynamic_slice.3
  114.1 6.4 %collective-permute-done.23.refs_1_ = bf16[256,512]{1,0:T(8,128)(2,1)S(1)} collective-permute-done((bf16[256,512]{1,0:T(8,128)(2,1)S(1)}, bf16[256,512]{1,0:T(8,128)(2,1)S(1)}, u32[]{:S(2)}, u32[]{:S(2)}) %collective-permute-start.23) | collective-permute-done | bytes 262176 | tf_op jit(solution)/shard_map/ppermute | solution.py:81
  120.5 2.5 %collective-permute-done.24.refs_2_ = bf16[256,512]{1,0:T(8,128)(2,1)S(1)} collective-permute-done((bf16[256,512]{1,0:T(8,128)(2,1)S(1)}, bf16[256,512]{1,0:T(8,128)(2,1)S(1)}, u32[]{:S(2)}, u32[]{:S(2)}) %collective-permute-start.24) | collective-permute-done | bytes 262176 | tf_op jit(solution)/shard_map/ppermute | solution.py:81
  122.9 4.2 %collective-permute-done.25.refs_3_ = bf16[256,512]{1,0:T(8,128)(2,1)S(1)} collective-permute-done((bf16[256,512]{1,0:T(8,128)(2,1)S(1)}, bf16[256,512]{1,0:T(8,128)(2,1)S(1)}, u32[]{:S(2)}, u32[]{:S(2)}) %collective-permute-start.25) | collective-permute-done | bytes 262176 | tf_op jit(solution)/shard_map/ppermute | solution.py:81
  127.2 0.9 copy-done.9
  128.1 0.9 mixed.1
  129.4 1.0 collective-permute-done.26
  130.4 2.1 %collective-permute-start.28 = (f32[256]{0:T(256)S(1)}, f32[256]{0:T(256)S(1)}, u32[]{:S(2)}, u32[]{:S(2)}) collective-permute-start(f32[256]{0:T(256)S(1)} %add.58), channel_id=1, source_target_pairs={{0,4},{1,5},{2,6},{3,7},{4,0},{5,1},{6,2},{7,3},{8,12},{9,13},{10,... | collective-permute-start | bytes 3080 | tf_op jit(solution)/shard_map/ppermute | solution.py:495
  132.4 1.2 collective-permute-start.29
  133.7 1.4 %collective-permute-done.27 = f32[256]{0:T(256)S(1)} collective-permute-done((f32[256]{0:T(256)S(1)}, f32[256]{0:T(256)S(1)}, u32[]{:S(2)}, u32[]{:S(2)}) %collective-permute-start.27) | collective-permute-done | bytes 1056 | tf_op jit(solution)/shard_map/ppermute | solution.py:495
  135.1 0.3 collective-permute-done.28
  135.4 0.6 collective-permute-done.29
  136.0 1.9 %d_encodings.1 = bf16[8,16,896]{2,1,0:T(8,128)(2,1)} custom-call(s32[8]{0:T(128)S(1)} %select_reduce_fusion.1.slot, bf16[32,16,896]{2,1,0:T(8,128)(2,1)S(1)} %all-to-all-done.2.back, bf16[8,16,896]{2,1,0:T(8,128)(2,1)S(1)} %copy-done.2, f32[1,1,896]{2,1,0:T(1,128)S(1)} %reshape.94.gain), custom_call_target="tpu_custom_call" | custom-call | flops 2090000000 | tf_op jit(solution)/shard_map/d_encodings/pallas_call | solution.py:410
  138.0 0.8 multiply_convert_fusion
  (61 shorter events, 1.3 us)
Async XLA Ops:
  0.6 38.1 %copy-start = (bf16[256,512]{1,0:T(8,128)(2,1)S(1)}, bf16[256,512]{1,0:T(8,128)(2,1)}, u32[]{:S(2)}) copy-start(bf16[256,512]{1,0:T(8,128)(2,1)} %tok.1) | copy-start | bytes 786436
  2.4 20.2 %all-to-all-start = ((s32[32,1,128]{2,1,0:T(1,128)}), s32[32,1,128]{2,1,0:T(1,128)S(1)}, u32[]{:S(2)}, u32[]{:S(2)}) async-start(s32[32,1,128]{2,1,0:T(1,128)} %broadcast_in_dim.46), calls=%async_computation | async-start | bytes 32768 | tf_op jit(solution)/shard_map/all_to_all | solution.py:456
  14.1 19.1 %collective-permute-start.6 = (bf16[256,512]{1,0:T(8,128)(2,1)}, bf16[256,512]{1,0:T(8,128)(2,1)S(1)}, u32[]{:S(2)}, u32[]{:S(2)}) collective-permute-start(bf16[256,512]{1,0:T(8,128)(2,1)} %tok.1), channel_id=1, source_target_pairs={{0,2},{1,3},{2,4},{3,5},{4,6},{5,7},{6,0},{7,1},{8,10},{9,11},{10,... | collective-permute-start | bytes 786440 | tf_op jit(solution)/shard_map/ppermute | solution.py:55
  15.6 17.5 %collective-permute-start.7 = (bf16[256,512]{1,0:T(8,128)(2,1)}, bf16[256,512]{1,0:T(8,128)(2,1)S(1)}, u32[]{:S(2)}, u32[]{:S(2)}) collective-permute-start(bf16[256,512]{1,0:T(8,128)(2,1)} %tok.1), channel_id=1, source_target_pairs={{0,4},{1,5},{2,6},{3,7},{4,0},{5,1},{6,2},{7,3},{8,12},{9,13},{10,... | collective-permute-start | bytes 786440 | tf_op jit(solution)/shard_map/ppermute | solution.py:55
  18.4 14.8 %collective-permute-start.8 = (bf16[256,512]{1,0:T(8,128)(2,1)}, bf16[256,512]{1,0:T(8,128)(2,1)S(1)}, u32[]{:S(2)}, u32[]{:S(2)}) collective-permute-start(bf16[256,512]{1,0:T(8,128)(2,1)} %tok.1), channel_id=1, source_target_pairs={{0,6},{1,7},{2,0},{3,1},{4,2},{5,3},{6,4},{7,5},{8,14},{9,15},{10,... | collective-permute-start | bytes 786440 | tf_op jit(solution)/shard_map/ppermute | solution.py:55
  20.5 0.9 copy-start.1
  21.4 13.9 %copy-start.13 = (f32[4096]{0:T(1024)S(1)}, f32[4096]{0:T(1024)}, u32[]{:S(2)}) copy-start(f32[4096]{0:T(1024)} %param.13) | copy-start | bytes 49156
  21.4 14.0 %copy-start.5 = (bf16[256,512]{1,0:T(8,128)(2,1)S(1)}, bf16[256,512]{1,0:T(8,128)(2,1)}, u32[]{:S(2)}) copy-start(bf16[256,512]{1,0:T(8,128)(2,1)} %r_1_.2) | copy-start | bytes 786436
  24.3 32.7 %all-to-all-start.1 = ((bf16[32,16,896]{2,1,0:T(8,128)(2,1)}), bf16[32,16,896]{2,1,0:T(8,128)(2,1)S(1)}, u32[]{:S(2)}, u32[]{:S(2)}) async-start(bf16[32,16,896]{2,1,0:T(8,128)(2,1)} %outgoing_rows.1), calls=%async_computation.1 | async-start | bytes 1835008 | tf_op jit(solution)/shard_map/all_to_all | solution.py:469
  35.3 3.5 %collective-permute-start.9 = (bf16[4,256,512]{2,1,0:T(8,128)(2,1)}, bf16[4,256,512]{2,1,0:T(8,128)(2,1)S(1)}, u32[]{:S(2)}, u32[]{:S(2)}) collective-permute-start(bf16[4,256,512]{2,1,0:T(8,128)(2,1)} %pad_maximum_fusion), channel_id=1, source_target_pairs={{0,1},{1,0},{2,3},{3,2},{4,5},{5,4},{6,7},{7,6},{8,9},{9,8},{10,11... | collective-permute-start | bytes 3145736 | tf_op jit(solution)/shard_map/ppermute | solution.py:59
  35.4 15.7 %collective-permute-start.3 = (bf16[256,512]{1,0:T(8,128)(2,1)S(1)}, bf16[256,512]{1,0:T(8,128)(2,1)}, u32[]{:S(2)}, u32[]{:S(2)}) collective-permute-start(bf16[256,512]{1,0:T(8,128)(2,1)S(1)} %copy-done.5), channel_id=1, source_target_pairs={{0,2},{1,3},{2,4},{3,5},{4,6},{5,7},{6,0},{7,1},{8,10},{9,11},{10,... | collective-permute-start | bytes 786440 | tf_op jit(solution)/shard_map/ppermute | solution.py:55
  36.0 15.1 %collective-permute-start.4 = (bf16[256,512]{1,0:T(8,128)(2,1)S(1)}, bf16[256,512]{1,0:T(8,128)(2,1)}, u32[]{:S(2)}, u32[]{:S(2)}) collective-permute-start(bf16[256,512]{1,0:T(8,128)(2,1)S(1)} %copy-done.5), channel_id=1, source_target_pairs={{0,4},{1,5},{2,6},{3,7},{4,0},{5,1},{6,2},{7,3},{8,12},{9,13},{10,... | collective-permute-start | bytes 786440 | tf_op jit(solution)/shard_map/ppermute | solution.py:55
  36.9 14.8 %collective-permute-start.5 = (bf16[256,512]{1,0:T(8,128)(2,1)S(1)}, bf16[256,512]{1,0:T(8,128)(2,1)}, u32[]{:S(2)}, u32[]{:S(2)}) collective-permute-start(bf16[256,512]{1,0:T(8,128)(2,1)S(1)} %copy-done.5), channel_id=1, source_target_pairs={{0,6},{1,7},{2,0},{3,1},{4,2},{5,3},{6,4},{7,5},{8,14},{9,15},{10,... | collective-permute-start | bytes 786440 | tf_op jit(solution)/shard_map/ppermute | solution.py:55
  42.7 0.7 copy-start.10
  51.7 7.0 %collective-permute-start.10 = (bf16[256,512]{1,0:T(8,128)(2,1)S(1)}, bf16[256,512]{1,0:T(8,128)(2,1)S(1)}, u32[]{:S(2)}, u32[]{:S(2)}) collective-permute-start(bf16[256,512]{1,0:T(8,128)(2,1)S(1)} %copy-done.5), channel_id=1, source_target_pairs={{0,1},{1,0},{2,3},{3,2},{4,5},{5,4},{6,7},{7,6},{8,9},{9,8},{10,11... | collective-permute-start | bytes 786440 | tf_op jit(solution)/shard_map/ppermute | solution.py:59
  51.7 8.2 %collective-permute-start.11 = (bf16[256,512]{1,0:T(8,128)(2,1)}, bf16[256,512]{1,0:T(8,128)(2,1)S(1)}, u32[]{:S(2)}, u32[]{:S(2)}) collective-permute-start(bf16[256,512]{1,0:T(8,128)(2,1)} %collective-permute-done.3.r_2_), channel_id=1, source_target_pairs={{0,1},{1,0},{2,3},{3,2},{4,5},{5,4},{6,7},{7,6},{8,9},{9,8},{10,11... | collective-permute-start | bytes 786440 | tf_op jit(solution)/shard_map/ppermute | solution.py:59
  52.2 9.4 %collective-permute-start.12 = (bf16[256,512]{1,0:T(8,128)(2,1)}, bf16[256,512]{1,0:T(8,128)(2,1)S(1)}, u32[]{:S(2)}, u32[]{:S(2)}) collective-permute-start(bf16[256,512]{1,0:T(8,128)(2,1)} %collective-permute-done.4.r_3_), channel_id=1, source_target_pairs={{0,1},{1,0},{2,3},{3,2},{4,5},{5,4},{6,7},{7,6},{8,9},{9,8},{10,11... | collective-permute-start | bytes 786440 | tf_op jit(solution)/shard_map/ppermute | solution.py:59
  52.2 9.4 %collective-permute-start.13 = (bf16[256,512]{1,0:T(8,128)(2,1)}, bf16[256,512]{1,0:T(8,128)(2,1)S(1)}, u32[]{:S(2)}, u32[]{:S(2)}) collective-permute-start(bf16[256,512]{1,0:T(8,128)(2,1)} %collective-permute-done.5.r_4_), channel_id=1, source_target_pairs={{0,1},{1,0},{2,3},{3,2},{4,5},{5,4},{6,7},{7,6},{8,9},{9,8},{10,11... | collective-permute-start | bytes 786440 | tf_op jit(solution)/shard_map/ppermute | solution.py:59
  58.0 13.2 %copy-start.3 = (bf16[896,512]{1,0:T(8,128)(2,1)S(1)}, bf16[896,512]{1,0:T(8,128)(2,1)}, u32[]{:S(2)}) copy-start(bf16[896,512]{1,0:T(8,128)(2,1)} %r_10_.1) | copy-start | bytes 2752516
  58.0 13.2 %copy-start.4 = (bf16[896,512]{1,0:T(8,128)(2,1)S(1)}, bf16[896,512]{1,0:T(8,128)(2,1)}, u32[]{:S(2)}) copy-start(bf16[896,512]{1,0:T(8,128)(2,1)} %r_11_.1) | copy-start | bytes 2752516
  58.0 13.2 %copy-start.11 = (bf16[256,512]{1,0:T(8,128)(2,1)S(1)}, bf16[256,512]{1,0:T(8,128)(2,1)}, u32[]{:S(2)}) copy-start(bf16[256,512]{1,0:T(8,128)(2,1)} %copy-done.10) | copy-start | bytes 786436
  58.0 10.8 %collective-permute-start = (bf16[128,896]{1,0:T(8,128)(2,1)S(1)}, bf16[128,896]{1,0:T(8,128)(2,1)S(1)}, u32[]{:S(2)}, u32[]{:S(2)}) collective-permute-start(bf16[128,896]{1,0:T(8,128)(2,1)S(1)} %bitcast.16), channel_id=1, source_target_pairs={{0,2},{1,3},{2,4},{3,5},{4,6},{5,7},{6,0},{7,1},{8,10},{9,11},{10,... | collective-permute-start | bytes 688136 | tf_op jit(solution)/shard_map/ppermute | solution.py:55
  58.7 10.1 %collective-permute-start.1 = (bf16[128,896]{1,0:T(8,128)(2,1)S(1)}, bf16[128,896]{1,0:T(8,128)(2,1)S(1)}, u32[]{:S(2)}, u32[]{:S(2)}) collective-permute-start(bf16[128,896]{1,0:T(8,128)(2,1)S(1)} %bitcast.17), channel_id=1, source_target_pairs={{0,4},{1,5},{2,6},{3,7},{4,0},{5,1},{6,2},{7,3},{8,12},{9,13},{10,... | collective-permute-start | bytes 688136 | tf_op jit(solution)/shard_map/ppermute | solution.py:55
  59.8 9.2 %collective-permute-start.2 = (bf16[128,896]{1,0:T(8,128)(2,1)S(1)}, bf16[128,896]{1,0:T(8,128)(2,1)S(1)}, u32[]{:S(2)}, u32[]{:S(2)}) collective-permute-start(bf16[128,896]{1,0:T(8,128)(2,1)S(1)} %bitcast.18), channel_id=1, source_target_pairs={{0,6},{1,7},{2,0},{3,1},{4,2},{5,3},{6,4},{7,5},{8,14},{9,15},{10,... | collective-permute-start | bytes 688136 | tf_op jit(solution)/shard_map/ppermute | solution.py:55
  66.0 3.6 %collective-permute-start.14 = (bf16[128,896]{1,0:T(8,128)(2,1)S(1)}, bf16[128,896]{1,0:T(8,128)(2,1)S(1)}, u32[]{:S(2)}, u32[]{:S(2)}) collective-permute-start(bf16[128,896]{1,0:T(8,128)(2,1)S(1)} %bitcast.19), channel_id=1, source_target_pairs={{0,1},{1,0},{2,3},{3,2},{4,5},{5,4},{6,7},{7,6},{8,9},{9,8},{10,11... | collective-permute-start | bytes 688136 | tf_op jit(solution)/shard_map/ppermute | solution.py:59
  69.0 1.5 %collective-permute-start.15 = (bf16[128,896]{1,0:T(8,128)(2,1)S(1)}, bf16[128,896]{1,0:T(8,128)(2,1)S(1)}, u32[]{:S(2)}, u32[]{:S(2)}) collective-permute-start(bf16[128,896]{1,0:T(8,128)(2,1)S(1)} %collective-permute-done.r_1_), channel_id=1, source_target_pairs={{0,1},{1,0},{2,3},{3,2},{4,5},{5,4},{6,7},{7,6},{8,9},{9,8},{10,11... | collective-permute-start | bytes 688136 | tf_op jit(solution)/shard_map/ppermute | solution.py:59
  69.0 1.8 %collective-permute-start.16 = (bf16[128,896]{1,0:T(8,128)(2,1)S(1)}, bf16[128,896]{1,0:T(8,128)(2,1)S(1)}, u32[]{:S(2)}, u32[]{:S(2)}) collective-permute-start(bf16[128,896]{1,0:T(8,128)(2,1)S(1)} %collective-permute-done.1.r_2_), channel_id=1, source_target_pairs={{0,1},{1,0},{2,3},{3,2},{4,5},{5,4},{6,7},{7,6},{8,9},{9,8},{10,11... | collective-permute-start | bytes 688136 | tf_op jit(solution)/shard_map/ppermute | solution.py:59
  69.5 1.6 %collective-permute-start.17 = (bf16[128,896]{1,0:T(8,128)(2,1)S(1)}, bf16[128,896]{1,0:T(8,128)(2,1)S(1)}, u32[]{:S(2)}, u32[]{:S(2)}) collective-permute-start(bf16[128,896]{1,0:T(8,128)(2,1)S(1)} %collective-permute-done.2.r_3_), channel_id=1, source_target_pairs={{0,1},{1,0},{2,3},{3,2},{4,5},{5,4},{6,7},{7,6},{8,9},{9,8},{10,11... | collective-permute-start | bytes 688136 | tf_op jit(solution)/shard_map/ppermute | solution.py:59
  78.2 2.6 %collective-permute-start.18 = (bf16[4,128,896]{2,1,0:T(8,128)(2,1)S(1)}, bf16[4,128,896]{2,1,0:T(8,128)(2,1)S(1)}, u32[]{:S(2)}, u32[]{:S(2)}) collective-permute-start(bf16[4,128,896]{2,1,0:T(8,128)(2,1)S(1)} %get-tuple-element.54), channel_id=1, source_target_pairs={{0,1},{1,0},{2,3},{3,2},{4,5},{5,4},{6,7},{7,6},{8,9},{9,8},{10,11... | collective-permute-start | bytes 2752520 | tf_op jit(solution)/shard_map/ppermute | solution.py:59
  81.0 12.8 %collective-permute-start.19 = (bf16[128,896]{1,0:T(8,128)(2,1)S(1)}, bf16[128,896]{1,0:T(8,128)(2,1)S(1)}, u32[]{:S(2)}, u32[]{:S(2)}) collective-permute-start(bf16[128,896]{1,0:T(8,128)(2,1)S(1)} %get-tuple-element.63), channel_id=1, source_target_pairs={{0,6},{1,7},{2,0},{3,1},{4,2},{5,3},{6,4},{7,5},{8,14},{9,15},{10,... | collective-permute-start | bytes 688136 | tf_op jit(solution)/shard_map/ppermute | solution.py:81
  83.6 10.2 %collective-permute-start.20 = (bf16[128,896]{1,0:T(8,128)(2,1)S(1)}, bf16[128,896]{1,0:T(8,128)(2,1)S(1)}, u32[]{:S(2)}, u32[]{:S(2)}) collective-permute-start(bf16[128,896]{1,0:T(8,128)(2,1)S(1)} %get-tuple-element.64), channel_id=1, source_target_pairs={{0,4},{1,5},{2,6},{3,7},{4,0},{5,1},{6,2},{7,3},{8,12},{9,13},{10,... | collective-permute-start | bytes 688136 | tf_op jit(solution)/shard_map/ppermute | solution.py:81
  83.6 13.5 %collective-permute-start.21 = (bf16[128,896]{1,0:T(8,128)(2,1)S(1)}, bf16[128,896]{1,0:T(8,128)(2,1)S(1)}, u32[]{:S(2)}, u32[]{:S(2)}) collective-permute-start(bf16[128,896]{1,0:T(8,128)(2,1)S(1)} %get-tuple-element.65), channel_id=1, source_target_pairs={{0,2},{1,3},{2,4},{3,5},{4,6},{5,7},{6,0},{7,1},{8,10},{9,11},{10,... | collective-permute-start | bytes 688136 | tf_op jit(solution)/shard_map/ppermute | solution.py:81
  88.7 1.0 copy-start.6
  97.1 10.7 %collective-permute-start.22 = (bf16[4,256,512]{2,1,0:T(8,128)(2,1)S(1)}, bf16[4,256,512]{2,1,0:T(8,128)(2,1)}, u32[]{:S(2)}, u32[]{:S(2)}) collective-permute-start(bf16[4,256,512]{2,1,0:T(8,128)(2,1)S(1)} %get-tuple-element.66), channel_id=1, source_target_pairs={{0,1},{1,0},{2,3},{3,2},{4,5},{5,4},{6,7},{7,6},{8,9},{9,8},{10,11... | collective-permute-start | bytes 3145736 | tf_op jit(solution)/shard_map/ppermute | solution.py:59
  98.9 37.1 %copy-start.2 = (bf16[8,16,896]{2,1,0:T(8,128)(2,1)S(1)}, bf16[8,16,896]{2,1,0:T(8,128)(2,1)}, u32[]{:S(2)}) copy-start(bf16[8,16,896]{2,1,0:T(8,128)(2,1)} %enc.3) | copy-start | bytes 688132
  98.9 37.1 %all-to-all-start.2 = ((bf16[32,16,896]{2,1,0:T(8,128)(2,1)}), bf16[32,16,896]{2,1,0:T(8,128)(2,1)S(1)}, u32[]{:S(2)}, u32[]{:S(2)}) async-start(bf16[32,16,896]{2,1,0:T(8,128)(2,1)} %placed_grads.1), calls=%async_computation.2 | async-start | bytes 1835008 | tf_op jit(solution)/shard_map/all_to_all | solution.py:487
  107.9 1.2 copy-start.7
  110.6 0.7 copy-start.8
  111.3 9.2 %collective-permute-start.23 = (bf16[256,512]{1,0:T(8,128)(2,1)S(1)}, bf16[256,512]{1,0:T(8,128)(2,1)S(1)}, u32[]{:S(2)}, u32[]{:S(2)}) collective-permute-start(bf16[256,512]{1,0:T(8,128)(2,1)S(1)} %get-tuple-element.68), channel_id=1, source_target_pairs={{0,6},{1,7},{2,0},{3,1},{4,2},{5,3},{6,4},{7,5},{8,14},{9,15},{10,... | collective-permute-start | bytes 786440 | tf_op jit(solution)/shard_map/ppermute | solution.py:81
  112.2 10.8 %collective-permute-start.24 = (bf16[256,512]{1,0:T(8,128)(2,1)S(1)}, bf16[256,512]{1,0:T(8,128)(2,1)S(1)}, u32[]{:S(2)}, u32[]{:S(2)}) collective-permute-start(bf16[256,512]{1,0:T(8,128)(2,1)S(1)} %get-tuple-element.69), channel_id=1, source_target_pairs={{0,4},{1,5},{2,6},{3,7},{4,0},{5,1},{6,2},{7,3},{8,12},{9,13},{10,... | collective-permute-start | bytes 786440 | tf_op jit(solution)/shard_map/ppermute | solution.py:81
  112.5 14.7 %collective-permute-start.25 = (bf16[256,512]{1,0:T(8,128)(2,1)S(1)}, bf16[256,512]{1,0:T(8,128)(2,1)S(1)}, u32[]{:S(2)}, u32[]{:S(2)}) collective-permute-start(bf16[256,512]{1,0:T(8,128)(2,1)S(1)} %get-tuple-element.70), channel_id=1, source_target_pairs={{0,2},{1,3},{2,4},{3,5},{4,6},{5,7},{6,0},{7,1},{8,10},{9,11},{10,... | collective-permute-start | bytes 786440 | tf_op jit(solution)/shard_map/ppermute | solution.py:81
  127.2 1.0 copy-start.9
  129.0 8.9 %copy-start.12 = (bf16[256,512]{1,0:T(8,128)(2,1)S(1)}, bf16[256,512]{1,0:T(8,128)(2,1)}, u32[]{:S(2)}) copy-start(bf16[256,512]{1,0:T(8,128)(2,1)} %get-tuple-element.38) | copy-start | bytes 786436
  129.1 1.2 collective-permute-start.26
  130.4 4.8 %collective-permute-start.27 = (f32[256]{0:T(256)S(1)}, f32[256]{0:T(256)S(1)}, u32[]{:S(2)}, u32[]{:S(2)}) collective-permute-start(f32[256]{0:T(256)S(1)} %add.58), channel_id=1, source_target_pairs={{0,2},{1,3},{2,4},{3,5},{4,6},{5,7},{6,0},{7,1},{8,10},{9,11},{10,... | collective-permute-start | bytes 3080 | tf_op jit(solution)/shard_map/ppermute | solution.py:495
  130.4 5.1 %collective-permute-start.28 = (f32[256]{0:T(256)S(1)}, f32[256]{0:T(256)S(1)}, u32[]{:S(2)}, u32[]{:S(2)}) collective-permute-start(f32[256]{0:T(256)S(1)} %add.58), channel_id=1, source_target_pairs={{0,4},{1,5},{2,6},{3,7},{4,0},{5,1},{6,2},{7,3},{8,12},{9,13},{10,... | collective-permute-start | bytes 3080 | tf_op jit(solution)/shard_map/ppermute | solution.py:495
  132.4 3.6 %collective-permute-start.29 = (f32[256]{0:T(256)S(1)}, f32[256]{0:T(256)S(1)}, u32[]{:S(2)}, u32[]{:S(2)}) collective-permute-start(f32[256]{0:T(256)S(1)} %add.58), channel_id=1, source_target_pairs={{0,6},{1,7},{2,0},{3,1},{4,2},{5,3},{6,4},{7,5},{8,14},{9,15},{10,... | collective-permute-start | bytes 3080 | tf_op jit(solution)/shard_map/ppermute | solution.py:495

commit v6 on v5

--- a/solution.py
+++ b/solution.py
@@ -15,7 +15,7 @@
 BF16 = jnp.bfloat16
 IDS_WIDTH = 128
 GROUP = 8
-MIX_COST = 1
+MIX_COST = 5
 MIB = 1024 * 1024
 
 
@@ -45,6 +45,10 @@
 
 def chip_shift(count, k):
     return [(i, (i + 2 * k) % count) for i in range(count)]
+
+
+def chip_flip(count, flip):
+    return [(i, i ^ (2 * flip)) for i in range(count)]
 
 
 def core_swap(count):
@@ -489,11 +493,10 @@
     mixed, squares = run_mix(tokens, b_parts)
     mixed_wide = mixed.astype(F32)
     squares = squares[:, 0]
-    squares = squares + swap(squares, count)
-    total = squares
-    for k in range(1, half):
-        total = total + lax.ppermute(squares, "mp", chip_shift(count, k))
     d_encodings = run_finish(slot, back_in, encodings, gain_enc)
+    total = squares + swap(squares, count)
+    for flip in range(1, half, 2):
+        total = total + lax.ppermute(total, "mp", chip_flip(count, flip))
     total, d_encodings = lax.optimization_barrier((total, d_encodings))
     post = lax.rsqrt(total / (share_cols * count) + EPS)[:, None]
     gain_here = lax.dynamic_slice_in_dim(gain_post, here * share_cols, share_cols, 0)

time: 140 us -> 140 us (level)
  waiting for transfers between devices: 44.3 us -> 49.6 us
  starting transfers between devices: 53.1 us -> 50.4 us
  local copies, waits for them, and re-layouts: 8.68 us -> 7.03 us
    ppermute x3 -> x2, waiting for transfers between devices: 2.29 us -> 7.51 us  [shards(): total = total + lax.ppermute(total, 'mp', chip_flip(count, flip))]
    ppermute x3 -> x2, starting transfers between devices: 3.24 us -> 0.61 us  [shards(): total = total + lax.ppermute(total, 'mp', chip_flip(count, flip))]
    unnamed x29 -> x25, local copies, waits for them, and re-layouts: 6.33 us -> 4.67 us
  transfers between devices with their start and end apart: 33 -> 32, of which waited for: 19 -> 18; matrix products, arithmetic and copies ran while one was open for 3% -> 3% of each run, Pallas kernels for 14% -> 14%
where the time goes in v6:
time: 140 us
  starting transfers between devices  50.4 us (36%)
  waiting for transfers between devices  49.6 us (35%)
  Pallas kernels  28.5 us (20%)
  local copies, waits for them, and re-layouts  7.03 us (5%)
  other arithmetic  3.32 us (2%)
    ppermute x6, waiting for transfers between devices, pair_shares(): lax.ppermute(pair[k], 'mp', chip_shift(count, -k))  21.4 us
    ppermute x9, starting transfers between devices, over_chips(): lax.ppermute(x, 'mp', chip_shift(count, k))  12.7 us
    all_to_all x1, starting transfers between devices, shards(): lax.all_to_all(jnp.broadcast_to(wanted[:, None], (dp_count, IDS_WIDTH)),...  11.7 us
    ppermute x9, waiting for transfers between devices, over_chips(): lax.ppermute(x, 'mp', chip_shift(count, k))  11.2 us
    all_to_all x1, starting transfers between devices, shards(): lax.all_to_all(outgoing, 'dp', split_axis=0, concat_axis=0, tiled=True)  8.85 us
    all_to_all x1, starting transfers between devices, shards(): lax.all_to_all(back_out, 'dp', split_axis=0, concat_axis=0, tiled=True)  8.84 us
    ppermute x2, waiting for transfers between devices, shards(): total = total + lax.ppermute(total, 'mp', chip_flip(count, flip))  7.51 us
    pallas_call x1, Pallas kernels, run_attention(): pl.pallas_call(lambda *r: attention_kernel(count, blocks, *r), out_shape=...  6.98 us
  transfers between devices with their start and end apart: 32, of which 18 were waited for; matrix products, arithmetic and copies ran while one was open for 3% of the time, Pallas kernels for 14%

profile of v6, /device:TPU:8, one launch (start us, length us, event | category | flops | bytes accessed | tf_op | source)
XLA Modules:
  0.0 139.8 jit_solution(2172434100522852289)
XLA Ops:
  0.6 0.8 copy.17
  1.6 0.7 broadcast_in_dim.46
  2.4 11.7 %all-to-all-start = ((s32[32,1,128]{2,1,0:T(1,128)}), s32[32,1,128]{2,1,0:T(1,128)S(1)}, u32[]{:S(2)}, u32[]{:S(2)}) async-start(s32[32,1,128]{2,1,0:T(1,128)} %broadcast_in_dim.46), calls=%async_computation | async-start | bytes 32768 | tf_op jit(solution)/shard_map/all_to_all | solution.py:460
  14.1 1.6 %collective-permute-start.6 = (bf16[256,512]{1,0:T(8,128)(2,1)}, bf16[256,512]{1,0:T(8,128)(2,1)S(1)}, u32[]{:S(2)}, u32[]{:S(2)}) collective-permute-start(bf16[256,512]{1,0:T(8,128)(2,1)} %tok.1), channel_id=1, source_target_pairs={{0,2},{1,3},{2,4},{3,5},{4,6},{5,7},{6,0},{7,1},{8,10},{9,11},{10,... | collective-permute-start | bytes 786440 | tf_op jit(solution)/shard_map/ppermute | solution.py:59
  15.6 2.7 %collective-permute-start.7 = (bf16[256,512]{1,0:T(8,128)(2,1)}, bf16[256,512]{1,0:T(8,128)(2,1)S(1)}, u32[]{:S(2)}, u32[]{:S(2)}) collective-permute-start(bf16[256,512]{1,0:T(8,128)(2,1)} %tok.1), channel_id=1, source_target_pairs={{0,4},{1,5},{2,6},{3,7},{4,0},{5,1},{6,2},{7,3},{8,12},{9,13},{10,... | collective-permute-start | bytes 786440 | tf_op jit(solution)/shard_map/ppermute | solution.py:59
  18.4 1.4 %collective-permute-start.8 = (bf16[256,512]{1,0:T(8,128)(2,1)}, bf16[256,512]{1,0:T(8,128)(2,1)S(1)}, u32[]{:S(2)}, u32[]{:S(2)}) collective-permute-start(bf16[256,512]{1,0:T(8,128)(2,1)} %tok.1), channel_id=1, source_target_pairs={{0,6},{1,7},{2,0},{3,1},{4,2},{5,3},{6,4},{7,5},{8,14},{9,15},{10,... | collective-permute-start | bytes 786440 | tf_op jit(solution)/shard_map/ppermute | solution.py:59
  19.8 0.7 reshape.94.gain
  20.5 0.9 copy-done.1
  21.4 0.1 normed_rows.1.normed
  21.6 0.9 all-to-all-done
  22.5 1.8 %outgoing_rows.1 = bf16[32,16,896]{2,1,0:T(8,128)(2,1)} custom-call(s32[32,128]{1,0:T(8,128)S(1)} %bitcast.14, bf16[8,16,896]{2,1,0:T(8,128)(2,1)S(1)} %normed_rows.1.normed), custom_call_target="tpu_custom_call" | custom-call | flops 110000000 | tf_op jit(solution)/shard_map/outgoing_rows/pallas_call | solution.py:316
  24.3 8.9 %all-to-all-start.1 = ((bf16[32,16,896]{2,1,0:T(8,128)(2,1)}), bf16[32,16,896]{2,1,0:T(8,128)(2,1)S(1)}, u32[]{:S(2)}, u32[]{:S(2)}) async-start(bf16[32,16,896]{2,1,0:T(8,128)(2,1)} %outgoing_rows.1), calls=%async_computation.1 | async-start | bytes 1835008 | tf_op jit(solution)/shard_map/all_to_all | solution.py:473
  33.2 2.1 %pad_maximum_fusion = bf16[4,256,512]{2,1,0:T(8,128)(2,1)} fusion(bf16[1,256,512]{2,1,0:T(8,128)(2,1)S(1)} %bitcast.13, bf16[1,256,512]{2,1,0:T(8,128)(2,1)S(1)} %bitcast.12, bf16[1,256,512]{2,1,0:T(8,128)(2,1)S(1)} %bitcast.11, bf16[1,256,512]{2,1,0:T(8,128)(2,1)} %bitcast.10), kind=kLoop, calls=%fused_computation | loop fusion | flops 1572864 | bytes 2097152 | tf_op jit(solution)/shard_map/stack | solution.py:475
  35.4 0.6 collective-permute-start.3
  36.0 0.9 collective-permute-start.4
  36.9 1.9 %collective-permute-start.5 = (bf16[256,512]{1,0:T(8,128)(2,1)S(1)}, bf16[256,512]{1,0:T(8,128)(2,1)}, u32[]{:S(2)}, u32[]{:S(2)}) collective-permute-start(bf16[256,512]{1,0:T(8,128)(2,1)S(1)} %copy-done.5), channel_id=1, source_target_pairs={{0,6},{1,7},{2,0},{3,1},{4,2},{5,3},{6,4},{7,5},{8,14},{9,15},{10,... | collective-permute-start | bytes 786440 | tf_op jit(solution)/shard_map/ppermute | solution.py:59
  38.8 3.9 %queries.1.r_8_ = bf16[256,512]{1,0:T(8,128)(2,1)S(1)} custom-call(s32[8]{0:T(128)S(1)} %pad_add_fusion.r_0_, bf16[256,512]{1,0:T(8,128)(2,1)S(1)} %copy-done, bf16[256,512]{1,0:T(8,128)(2,1)S(1)} %collective-permute-done.6.r_2_, bf16[256,512]{1,0:T(8,128)(2,1)S(1)} %collective-permute-done.7.r_3_, bf16[256,512]{1,0:T(8,128)(2,1)S(1)} %collective-permute-done.8.r_4_, ...), custom_call_target="tpu_custom_call" | custom-call | flops 3740000000 | tf_op jit(solution)/shard_map/queries/pallas_call | solution.py:141
  42.7 0.7 copy-done.8
  43.4 7.6 %collective-permute-done.3.r_2_ = bf16[256,512]{1,0:T(8,128)(2,1)} collective-permute-done((bf16[256,512]{1,0:T(8,128)(2,1)S(1)}, bf16[256,512]{1,0:T(8,128)(2,1)}, u32[]{:S(2)}, u32[]{:S(2)}) %collective-permute-start.3) | collective-permute-done | bytes 262176 | tf_op jit(solution)/shard_map/ppermute | solution.py:59
  51.1 0.6 collective-permute-done.5.r_4_
  51.7 0.5 collective-permute-start.11
  52.2 0.5 collective-permute-start.13
  52.7 4.3 %all-to-all-done.1.rows = bf16[32,16,896]{2,1,0:T(8,128)(2,1)S(1)} async-done(((bf16[32,16,896]{2,1,0:T(8,128)(2,1)}), bf16[32,16,896]{2,1,0:T(8,128)(2,1)S(1)}, u32[]{:S(2)}, u32[]{:S(2)}) %all-to-all-start.1) | async-done | bytes 917536 | tf_op jit(solution)/shard_map/all_to_all | solution.py:473
  57.0 1.0 picked_rows.1
  58.0 0.7 collective-permute-start
  58.7 1.2 collective-permute-start.1
  59.9 1.8 %collective-permute-start.2 = (bf16[128,896]{1,0:T(8,128)(2,1)S(1)}, bf16[128,896]{1,0:T(8,128)(2,1)S(1)}, u32[]{:S(2)}, u32[]{:S(2)}) collective-permute-start(bf16[128,896]{1,0:T(8,128)(2,1)S(1)} %bitcast.18), channel_id=1, source_target_pairs={{0,6},{1,7},{2,0},{3,1},{4,2},{5,3},{6,4},{7,5},{8,14},{9,15},{10,... | collective-permute-start | bytes 688136 | tf_op jit(solution)/shard_map/ppermute | solution.py:59
  61.6 4.4 %d_attended.1.r_9_ = bf16[256,512]{1,0:T(8,128)(2,1)S(1)} custom-call(s32[8]{0:T(128)S(1)} %pad_add_fusion.r_0_, bf16[256,512]{1,0:T(8,128)(2,1)S(1)} %copy-done.5, bf16[256,512]{1,0:T(8,128)(2,1)} %collective-permute-done.3.r_2_, bf16[256,512]{1,0:T(8,128)(2,1)} %collective-permute-done.4.r_3_, bf16[256,512]{1,0:T(8,128)(2,1)} %collective-permute-done.5.r_4_, ...), custom_call_target="tpu_custom_call" | custom-call | flops 3740000000 | tf_op jit(solution)/shard_map/d_attended/pallas_call | solution.py:174
  66.1 2.7 %collective-permute-done.r_1_ = bf16[128,896]{1,0:T(8,128)(2,1)S(1)} collective-permute-done((bf16[128,896]{1,0:T(8,128)(2,1)S(1)}, bf16[128,896]{1,0:T(8,128)(2,1)S(1)}, u32[]{:S(2)}, u32[]{:S(2)}) %collective-permute-start) | collective-permute-done | bytes 229408 | tf_op jit(solution)/shard_map/ppermute | solution.py:59
  68.8 0.2 collective-permute-done.2.r_3_
  69.0 0.5 collective-permute-start.16
  69.6 1.0 collective-permute-done.15.r_5_
  70.5 0.3 collective-permute-done.16.r_6_
  70.9 0.3 collective-permute-done.17.r_7_
  71.2 7.0 %attention.1 = (bf16[4,128,896]{2,1,0:T(8,128)(2,1)S(1)}, bf16[4,128,896]{2,1,0:T(8,128)(2,1)S(1)}, bf16[256,512]{1,0:T(8,128)(2,1)S(1)}) custom-call(bf16[128,896]{1,0:T(8,128)(2,1)S(1)} %bitcast.20, bf16[128,896]{1,0:T(8,128)(2,1)S(1)} %collective-permute-done.r_1_, bf16[128,896]{1,0:T(8,128)(2,1)S(1)} %collective-permute-done.1.r_2_, ...), custom_call_target="tpu_custom_call" | custom-call | flops 9900000256 | tf_op jit(solution)/shard_map/attention/pallas_call | solution.py:279
  78.2 0.3 collective-permute-start.18
  78.5 2.3 %collective-permute-done.18.other = bf16[4,128,896]{2,1,0:T(8,128)(2,1)S(1)} collective-permute-done((bf16[4,128,896]{2,1,0:T(8,128)(2,1)S(1)}, bf16[4,128,896]{2,1,0:T(8,128)(2,1)S(1)}, u32[]{:S(2)}, u32[]{:S(2)}) %collective-permute-start.18) | collective-permute-done | bytes 917536 | tf_op jit(solution)/shard_map/ppermute | solution.py:63
  80.7 0.2 pair_sums.2
  81.0 2.6 %collective-permute-start.19 = (bf16[128,896]{1,0:T(8,128)(2,1)S(1)}, bf16[128,896]{1,0:T(8,128)(2,1)S(1)}, u32[]{:S(2)}, u32[]{:S(2)}) collective-permute-start(bf16[128,896]{1,0:T(8,128)(2,1)S(1)} %get-tuple-element.63), channel_id=1, source_target_pairs={{0,6},{1,7},{2,0},{3,1},{4,2},{5,3},{6,4},{7,5},{8,14},{9,15},{10,... | collective-permute-start | bytes 688136 | tf_op jit(solution)/shard_map/ppermute | solution.py:85
  83.6 1.0 collective-permute-start.21
  84.6 4.1 %branches.1 = (bf16[4,256,512]{2,1,0:T(8,128)(2,1)S(1)}, bf16[4,256,512]{2,1,0:T(8,128)(2,1)S(1)}) custom-call(s32[8]{0:T(128)S(1)} %pad_add_fusion.r_0_, bf16[256,512]{1,0:T(8,128)(2,1)S(1)} %get-tuple-element.59.r_1_, bf16[512,4096]{1,0:T(8,128)(2,1)} %r_2_.1), custom_call_target="tpu_custom_call" | custom-call | flops 4400000000 | tf_op jit(solution)/shard_map/branches/pallas_call | solution.py:207
  88.7 1.0 copy-done.6
  89.6 4.1 %collective-permute-done.19 = bf16[128,896]{1,0:T(8,128)(2,1)S(1)} collective-permute-done((bf16[128,896]{1,0:T(8,128)(2,1)S(1)}, bf16[128,896]{1,0:T(8,128)(2,1)S(1)}, u32[]{:S(2)}, u32[]{:S(2)}) %collective-permute-start.19) | collective-permute-done | bytes 229408 | tf_op jit(solution)/shard_map/ppermute | solution.py:85
  93.8 3.4 %collective-permute-done.21 = bf16[128,896]{1,0:T(8,128)(2,1)S(1)} collective-permute-done((bf16[128,896]{1,0:T(8,128)(2,1)S(1)}, bf16[128,896]{1,0:T(8,128)(2,1)S(1)}, u32[]{:S(2)}, u32[]{:S(2)}) %collective-permute-start.21) | collective-permute-done | bytes 229408 | tf_op jit(solution)/shard_map/ppermute | solution.py:85
  97.1 1.7 %placed_grads.1 = bf16[32,16,896]{2,1,0:T(8,128)(2,1)} custom-call(s32[32]{0:T(128)S(1)} %get-tuple-element.79.reading, bf16[8,16,896]{2,1,0:T(8,128)(2,1)S(1)} %bitcast.24, bf16[8,16,896]{2,1,0:T(8,128)(2,1)S(1)} %bitcast.21, bf16[8,16,896]{2,1,0:T(8,128)(2,1)S(1)} %bitcast.22, bf16[8,16,896]{2,1,0:T(8,128)(2,1)S(1)} %bitcast.23), custom_call_target="tpu_custom_call" | custom-call | flops 1870000000 | tf_op jit(solution)/shard_map/placed_grads/pallas_call | solution.py:361
  98.9 8.8 %all-to-all-start.2 = ((bf16[32,16,896]{2,1,0:T(8,128)(2,1)}), bf16[32,16,896]{2,1,0:T(8,128)(2,1)S(1)}, u32[]{:S(2)}, u32[]{:S(2)}) async-start(bf16[32,16,896]{2,1,0:T(8,128)(2,1)} %placed_grads.1), calls=%async_computation.2 | async-start | bytes 1835008 | tf_op jit(solution)/shard_map/all_to_all | solution.py:491
  107.8 1.2 copy-done.7
  109.0 1.5 %pair_sums.3 = (bf16[256,512]{1,0:T(8,128)(2,1)S(1)}, bf16[256,512]{1,0:T(8,128)(2,1)S(1)}, bf16[256,512]{1,0:T(8,128)(2,1)S(1)}, bf16[256,512]{1,0:T(8,128)(2,1)S(1)}) custom-call(bf16[4,256,512]{2,1,0:T(8,128)(2,1)S(1)} %copy-done.7, bf16[4,256,512]{2,1,0:T(8,128)(2,1)} %collective-permute-done.22.other), custom_call_target="tpu_custom_call" | custom-call | flops 770000000 | tf_op jit(solution)/shard_map/pair_sums/pallas_call | solution.py:72
  110.4 1.0 collective-permute-start.23
  111.4 0.3 collective-permute-start.24
  111.7 0.8 collective-permute-start.25
  112.5 7.1 %collective-permute-done.23.refs_1_ = bf16[256,512]{1,0:T(8,128)(2,1)S(1)} collective-permute-done((bf16[256,512]{1,0:T(8,128)(2,1)S(1)}, bf16[256,512]{1,0:T(8,128)(2,1)S(1)}, u32[]{:S(2)}, u32[]{:S(2)}) %collective-permute-start.23) | collective-permute-done | bytes 262176 | tf_op jit(solution)/shard_map/ppermute | solution.py:85
  119.7 2.5 %collective-permute-done.24.refs_2_ = bf16[256,512]{1,0:T(8,128)(2,1)S(1)} collective-permute-done((bf16[256,512]{1,0:T(8,128)(2,1)S(1)}, bf16[256,512]{1,0:T(8,128)(2,1)S(1)}, u32[]{:S(2)}, u32[]{:S(2)}) %collective-permute-start.24) | collective-permute-done | bytes 262176 | tf_op jit(solution)/shard_map/ppermute | solution.py:85
  122.2 4.2 %collective-permute-done.25.refs_3_ = bf16[256,512]{1,0:T(8,128)(2,1)S(1)} collective-permute-done((bf16[256,512]{1,0:T(8,128)(2,1)S(1)}, bf16[256,512]{1,0:T(8,128)(2,1)S(1)}, u32[]{:S(2)}, u32[]{:S(2)}) %collective-permute-start.25) | collective-permute-done | bytes 262176 | tf_op jit(solution)/shard_map/ppermute | solution.py:85
  126.4 0.9 mixed.1
  127.5 0.8 dynamic_slice.3
  128.3 0.4 collective-permute-done.26
  128.6 0.1 slice_reduce_fusion
  128.8 3.5 %collective-permute-done.27 = f32[256]{0:T(256)S(1)} collective-permute-done((f32[256]{0:T(256)S(1)}, f32[256]{0:T(256)S(1)}, u32[]{:S(2)}, u32[]{:S(2)}) %collective-permute-start.27) | collective-permute-done | bytes 1056 | tf_op jit(solution)/shard_map/ppermute | solution.py:499
  132.2 0.6 collective-permute-start.28
  132.8 0.1 select_reduce_fusion.1.slot
  132.9 4.1 %collective-permute-done.28 = f32[256]{0:T(256)S(1)} collective-permute-done((f32[256]{0:T(256)S(1)}, f32[256]{0:T(256)S(1)}, u32[]{:S(2)}, u32[]{:S(2)}) %collective-permute-start.28) | collective-permute-done | bytes 1056 | tf_op jit(solution)/shard_map/ppermute | solution.py:499
  137.0 1.9 %d_encodings.1 = bf16[8,16,896]{2,1,0:T(8,128)(2,1)} custom-call(s32[8]{0:T(128)S(1)} %select_reduce_fusion.1.slot, bf16[32,16,896]{2,1,0:T(8,128)(2,1)S(1)} %all-to-all-done.2.back, bf16[8,16,896]{2,1,0:T(8,128)(2,1)S(1)} %copy-done.2, f32[1,1,896]{2,1,0:T(1,128)S(1)} %reshape.94.gain), custom_call_target="tpu_custom_call" | custom-call | flops 2090000000 | tf_op jit(solution)/shard_map/d_encodings/pallas_call | solution.py:414
  139.0 0.8 multiply_convert_fusion
  (56 shorter events, 0.7 us)
Async XLA Ops:
  0.6 38.1 %copy-start = (bf16[256,512]{1,0:T(8,128)(2,1)S(1)}, bf16[256,512]{1,0:T(8,128)(2,1)}, u32[]{:S(2)}) copy-start(bf16[256,512]{1,0:T(8,128)(2,1)} %tok.1) | copy-start | bytes 786436
  2.4 20.2 %all-to-all-start = ((s32[32,1,128]{2,1,0:T(1,128)}), s32[32,1,128]{2,1,0:T(1,128)S(1)}, u32[]{:S(2)}, u32[]{:S(2)}) async-start(s32[32,1,128]{2,1,0:T(1,128)} %broadcast_in_dim.46), calls=%async_computation | async-start | bytes 32768 | tf_op jit(solution)/shard_map/all_to_all | solution.py:460
  14.1 19.1 %collective-permute-start.6 = (bf16[256,512]{1,0:T(8,128)(2,1)}, bf16[256,512]{1,0:T(8,128)(2,1)S(1)}, u32[]{:S(2)}, u32[]{:S(2)}) collective-permute-start(bf16[256,512]{1,0:T(8,128)(2,1)} %tok.1), channel_id=1, source_target_pairs={{0,2},{1,3},{2,4},{3,5},{4,6},{5,7},{6,0},{7,1},{8,10},{9,11},{10,... | collective-permute-start | bytes 786440 | tf_op jit(solution)/shard_map/ppermute | solution.py:59
  15.6 17.6 %collective-permute-start.7 = (bf16[256,512]{1,0:T(8,128)(2,1)}, bf16[256,512]{1,0:T(8,128)(2,1)S(1)}, u32[]{:S(2)}, u32[]{:S(2)}) collective-permute-start(bf16[256,512]{1,0:T(8,128)(2,1)} %tok.1), channel_id=1, source_target_pairs={{0,4},{1,5},{2,6},{3,7},{4,0},{5,1},{6,2},{7,3},{8,12},{9,13},{10,... | collective-permute-start | bytes 786440 | tf_op jit(solution)/shard_map/ppermute | solution.py:59
  18.4 14.8 %collective-permute-start.8 = (bf16[256,512]{1,0:T(8,128)(2,1)}, bf16[256,512]{1,0:T(8,128)(2,1)S(1)}, u32[]{:S(2)}, u32[]{:S(2)}) collective-permute-start(bf16[256,512]{1,0:T(8,128)(2,1)} %tok.1), channel_id=1, source_target_pairs={{0,6},{1,7},{2,0},{3,1},{4,2},{5,3},{6,4},{7,5},{8,14},{9,15},{10,... | collective-permute-start | bytes 786440 | tf_op jit(solution)/shard_map/ppermute | solution.py:59
  20.5 0.9 copy-start.1
  21.4 13.9 %copy-start.11 = (f32[4096]{0:T(1024)S(1)}, f32[4096]{0:T(1024)}, u32[]{:S(2)}) copy-start(f32[4096]{0:T(1024)} %param.13) | copy-start | bytes 49156
  21.4 14.0 %copy-start.5 = (bf16[256,512]{1,0:T(8,128)(2,1)S(1)}, bf16[256,512]{1,0:T(8,128)(2,1)}, u32[]{:S(2)}) copy-start(bf16[256,512]{1,0:T(8,128)(2,1)} %r_1_.2) | copy-start | bytes 786436
  24.3 32.7 %all-to-all-start.1 = ((bf16[32,16,896]{2,1,0:T(8,128)(2,1)}), bf16[32,16,896]{2,1,0:T(8,128)(2,1)S(1)}, u32[]{:S(2)}, u32[]{:S(2)}) async-start(bf16[32,16,896]{2,1,0:T(8,128)(2,1)} %outgoing_rows.1), calls=%async_computation.1 | async-start | bytes 1835008 | tf_op jit(solution)/shard_map/all_to_all | solution.py:473
  35.3 3.5 %collective-permute-start.9 = (bf16[4,256,512]{2,1,0:T(8,128)(2,1)}, bf16[4,256,512]{2,1,0:T(8,128)(2,1)S(1)}, u32[]{:S(2)}, u32[]{:S(2)}) collective-permute-start(bf16[4,256,512]{2,1,0:T(8,128)(2,1)} %pad_maximum_fusion), channel_id=1, source_target_pairs={{0,1},{1,0},{2,3},{3,2},{4,5},{5,4},{6,7},{7,6},{8,9},{9,8},{10,11... | collective-permute-start | bytes 3145736 | tf_op jit(solution)/shard_map/ppermute | solution.py:63
  35.4 15.7 %collective-permute-start.3 = (bf16[256,512]{1,0:T(8,128)(2,1)S(1)}, bf16[256,512]{1,0:T(8,128)(2,1)}, u32[]{:S(2)}, u32[]{:S(2)}) collective-permute-start(bf16[256,512]{1,0:T(8,128)(2,1)S(1)} %copy-done.5), channel_id=1, source_target_pairs={{0,2},{1,3},{2,4},{3,5},{4,6},{5,7},{6,0},{7,1},{8,10},{9,11},{10,... | collective-permute-start | bytes 786440 | tf_op jit(solution)/shard_map/ppermute | solution.py:59
  36.0 15.1 %collective-permute-start.4 = (bf16[256,512]{1,0:T(8,128)(2,1)S(1)}, bf16[256,512]{1,0:T(8,128)(2,1)}, u32[]{:S(2)}, u32[]{:S(2)}) collective-permute-start(bf16[256,512]{1,0:T(8,128)(2,1)S(1)} %copy-done.5), channel_id=1, source_target_pairs={{0,4},{1,5},{2,6},{3,7},{4,0},{5,1},{6,2},{7,3},{8,12},{9,13},{10,... | collective-permute-start | bytes 786440 | tf_op jit(solution)/shard_map/ppermute | solution.py:59
  36.9 14.8 %collective-permute-start.5 = (bf16[256,512]{1,0:T(8,128)(2,1)S(1)}, bf16[256,512]{1,0:T(8,128)(2,1)}, u32[]{:S(2)}, u32[]{:S(2)}) collective-permute-start(bf16[256,512]{1,0:T(8,128)(2,1)S(1)} %copy-done.5), channel_id=1, source_target_pairs={{0,6},{1,7},{2,0},{3,1},{4,2},{5,3},{6,4},{7,5},{8,14},{9,15},{10,... | collective-permute-start | bytes 786440 | tf_op jit(solution)/shard_map/ppermute | solution.py:59
  42.7 0.7 copy-start.8
  51.7 7.0 %collective-permute-start.10 = (bf16[256,512]{1,0:T(8,128)(2,1)S(1)}, bf16[256,512]{1,0:T(8,128)(2,1)S(1)}, u32[]{:S(2)}, u32[]{:S(2)}) collective-permute-start(bf16[256,512]{1,0:T(8,128)(2,1)S(1)} %copy-done.5), channel_id=1, source_target_pairs={{0,1},{1,0},{2,3},{3,2},{4,5},{5,4},{6,7},{7,6},{8,9},{9,8},{10,11... | collective-permute-start | bytes 786440 | tf_op jit(solution)/shard_map/ppermute | solution.py:63
  51.7 8.2 %collective-permute-start.11 = (bf16[256,512]{1,0:T(8,128)(2,1)}, bf16[256,512]{1,0:T(8,128)(2,1)S(1)}, u32[]{:S(2)}, u32[]{:S(2)}) collective-permute-start(bf16[256,512]{1,0:T(8,128)(2,1)} %collective-permute-done.3.r_2_), channel_id=1, source_target_pairs={{0,1},{1,0},{2,3},{3,2},{4,5},{5,4},{6,7},{7,6},{8,9},{9,8},{10,11... | collective-permute-start | bytes 786440 | tf_op jit(solution)/shard_map/ppermute | solution.py:63
  52.2 9.4 %collective-permute-start.12 = (bf16[256,512]{1,0:T(8,128)(2,1)}, bf16[256,512]{1,0:T(8,128)(2,1)S(1)}, u32[]{:S(2)}, u32[]{:S(2)}) collective-permute-start(bf16[256,512]{1,0:T(8,128)(2,1)} %collective-permute-done.4.r_3_), channel_id=1, source_target_pairs={{0,1},{1,0},{2,3},{3,2},{4,5},{5,4},{6,7},{7,6},{8,9},{9,8},{10,11... | collective-permute-start | bytes 786440 | tf_op jit(solution)/shard_map/ppermute | solution.py:63
  52.2 9.4 %collective-permute-start.13 = (bf16[256,512]{1,0:T(8,128)(2,1)}, bf16[256,512]{1,0:T(8,128)(2,1)S(1)}, u32[]{:S(2)}, u32[]{:S(2)}) collective-permute-start(bf16[256,512]{1,0:T(8,128)(2,1)} %collective-permute-done.5.r_4_), channel_id=1, source_target_pairs={{0,1},{1,0},{2,3},{3,2},{4,5},{5,4},{6,7},{7,6},{8,9},{9,8},{10,11... | collective-permute-start | bytes 786440 | tf_op jit(solution)/shard_map/ppermute | solution.py:63
  58.0 13.2 %copy-start.3 = (bf16[896,512]{1,0:T(8,128)(2,1)S(1)}, bf16[896,512]{1,0:T(8,128)(2,1)}, u32[]{:S(2)}) copy-start(bf16[896,512]{1,0:T(8,128)(2,1)} %r_10_.1) | copy-start | bytes 2752516
  58.0 13.2 %copy-start.4 = (bf16[896,512]{1,0:T(8,128)(2,1)S(1)}, bf16[896,512]{1,0:T(8,128)(2,1)}, u32[]{:S(2)}) copy-start(bf16[896,512]{1,0:T(8,128)(2,1)} %r_11_.1) | copy-start | bytes 2752516
  58.0 13.2 %copy-start.9 = (bf16[256,512]{1,0:T(8,128)(2,1)S(1)}, bf16[256,512]{1,0:T(8,128)(2,1)}, u32[]{:S(2)}) copy-start(bf16[256,512]{1,0:T(8,128)(2,1)} %copy-done.8) | copy-start | bytes 786436
  58.0 10.8 %collective-permute-start = (bf16[128,896]{1,0:T(8,128)(2,1)S(1)}, bf16[128,896]{1,0:T(8,128)(2,1)S(1)}, u32[]{:S(2)}, u32[]{:S(2)}) collective-permute-start(bf16[128,896]{1,0:T(8,128)(2,1)S(1)} %bitcast.16), channel_id=1, source_target_pairs={{0,2},{1,3},{2,4},{3,5},{4,6},{5,7},{6,0},{7,1},{8,10},{9,11},{10,... | collective-permute-start | bytes 688136 | tf_op jit(solution)/shard_map/ppermute | solution.py:59
  58.7 10.1 %collective-permute-start.1 = (bf16[128,896]{1,0:T(8,128)(2,1)S(1)}, bf16[128,896]{1,0:T(8,128)(2,1)S(1)}, u32[]{:S(2)}, u32[]{:S(2)}) collective-permute-start(bf16[128,896]{1,0:T(8,128)(2,1)S(1)} %bitcast.17), channel_id=1, source_target_pairs={{0,4},{1,5},{2,6},{3,7},{4,0},{5,1},{6,2},{7,3},{8,12},{9,13},{10,... | collective-permute-start | bytes 688136 | tf_op jit(solution)/shard_map/ppermute | solution.py:59
  59.9 9.2 %collective-permute-start.2 = (bf16[128,896]{1,0:T(8,128)(2,1)S(1)}, bf16[128,896]{1,0:T(8,128)(2,1)S(1)}, u32[]{:S(2)}, u32[]{:S(2)}) collective-permute-start(bf16[128,896]{1,0:T(8,128)(2,1)S(1)} %bitcast.18), channel_id=1, source_target_pairs={{0,6},{1,7},{2,0},{3,1},{4,2},{5,3},{6,4},{7,5},{8,14},{9,15},{10,... | collective-permute-start | bytes 688136 | tf_op jit(solution)/shard_map/ppermute | solution.py:59
  66.0 3.6 %collective-permute-start.14 = (bf16[128,896]{1,0:T(8,128)(2,1)S(1)}, bf16[128,896]{1,0:T(8,128)(2,1)S(1)}, u32[]{:S(2)}, u32[]{:S(2)}) collective-permute-start(bf16[128,896]{1,0:T(8,128)(2,1)S(1)} %bitcast.19), channel_id=1, source_target_pairs={{0,1},{1,0},{2,3},{3,2},{4,5},{5,4},{6,7},{7,6},{8,9},{9,8},{10,11... | collective-permute-start | bytes 688136 | tf_op jit(solution)/shard_map/ppermute | solution.py:63
  69.0 1.5 %collective-permute-start.15 = (bf16[128,896]{1,0:T(8,128)(2,1)S(1)}, bf16[128,896]{1,0:T(8,128)(2,1)S(1)}, u32[]{:S(2)}, u32[]{:S(2)}) collective-permute-start(bf16[128,896]{1,0:T(8,128)(2,1)S(1)} %collective-permute-done.r_1_), channel_id=1, source_target_pairs={{0,1},{1,0},{2,3},{3,2},{4,5},{5,4},{6,7},{7,6},{8,9},{9,8},{10,11... | collective-permute-start | bytes 688136 | tf_op jit(solution)/shard_map/ppermute | solution.py:63
  69.0 1.8 %collective-permute-start.16 = (bf16[128,896]{1,0:T(8,128)(2,1)S(1)}, bf16[128,896]{1,0:T(8,128)(2,1)S(1)}, u32[]{:S(2)}, u32[]{:S(2)}) collective-permute-start(bf16[128,896]{1,0:T(8,128)(2,1)S(1)} %collective-permute-done.1.r_2_), channel_id=1, source_target_pairs={{0,1},{1,0},{2,3},{3,2},{4,5},{5,4},{6,7},{7,6},{8,9},{9,8},{10,11... | collective-permute-start | bytes 688136 | tf_op jit(solution)/shard_map/ppermute | solution.py:63
  69.6 1.6 %collective-permute-start.17 = (bf16[128,896]{1,0:T(8,128)(2,1)S(1)}, bf16[128,896]{1,0:T(8,128)(2,1)S(1)}, u32[]{:S(2)}, u32[]{:S(2)}) collective-permute-start(bf16[128,896]{1,0:T(8,128)(2,1)S(1)} %collective-permute-done.2.r_3_), channel_id=1, source_target_pairs={{0,1},{1,0},{2,3},{3,2},{4,5},{5,4},{6,7},{7,6},{8,9},{9,8},{10,11... | collective-permute-start | bytes 688136 | tf_op jit(solution)/shard_map/ppermute | solution.py:63
  78.2 2.6 %collective-permute-start.18 = (bf16[4,128,896]{2,1,0:T(8,128)(2,1)S(1)}, bf16[4,128,896]{2,1,0:T(8,128)(2,1)S(1)}, u32[]{:S(2)}, u32[]{:S(2)}) collective-permute-start(bf16[4,128,896]{2,1,0:T(8,128)(2,1)S(1)} %get-tuple-element.54), channel_id=1, source_target_pairs={{0,1},{1,0},{2,3},{3,2},{4,5},{5,4},{6,7},{7,6},{8,9},{9,8},{10,11... | collective-permute-start | bytes 2752520 | tf_op jit(solution)/shard_map/ppermute | solution.py:63
  81.0 12.8 %collective-permute-start.19 = (bf16[128,896]{1,0:T(8,128)(2,1)S(1)}, bf16[128,896]{1,0:T(8,128)(2,1)S(1)}, u32[]{:S(2)}, u32[]{:S(2)}) collective-permute-start(bf16[128,896]{1,0:T(8,128)(2,1)S(1)} %get-tuple-element.63), channel_id=1, source_target_pairs={{0,6},{1,7},{2,0},{3,1},{4,2},{5,3},{6,4},{7,5},{8,14},{9,15},{10,... | collective-permute-start | bytes 688136 | tf_op jit(solution)/shard_map/ppermute | solution.py:85
  83.6 10.2 %collective-permute-start.20 = (bf16[128,896]{1,0:T(8,128)(2,1)S(1)}, bf16[128,896]{1,0:T(8,128)(2,1)S(1)}, u32[]{:S(2)}, u32[]{:S(2)}) collective-permute-start(bf16[128,896]{1,0:T(8,128)(2,1)S(1)} %get-tuple-element.64), channel_id=1, source_target_pairs={{0,4},{1,5},{2,6},{3,7},{4,0},{5,1},{6,2},{7,3},{8,12},{9,13},{10,... | collective-permute-start | bytes 688136 | tf_op jit(solution)/shard_map/ppermute | solution.py:85
  83.6 13.5 %collective-permute-start.21 = (bf16[128,896]{1,0:T(8,128)(2,1)S(1)}, bf16[128,896]{1,0:T(8,128)(2,1)S(1)}, u32[]{:S(2)}, u32[]{:S(2)}) collective-permute-start(bf16[128,896]{1,0:T(8,128)(2,1)S(1)} %get-tuple-element.65), channel_id=1, source_target_pairs={{0,2},{1,3},{2,4},{3,5},{4,6},{5,7},{6,0},{7,1},{8,10},{9,11},{10,... | collective-permute-start | bytes 688136 | tf_op jit(solution)/shard_map/ppermute | solution.py:85
  88.7 1.0 copy-start.6
  97.1 10.6 %collective-permute-start.22 = (bf16[4,256,512]{2,1,0:T(8,128)(2,1)S(1)}, bf16[4,256,512]{2,1,0:T(8,128)(2,1)}, u32[]{:S(2)}, u32[]{:S(2)}) collective-permute-start(bf16[4,256,512]{2,1,0:T(8,128)(2,1)S(1)} %get-tuple-element.66), channel_id=1, source_target_pairs={{0,1},{1,0},{2,3},{3,2},{4,5},{5,4},{6,7},{7,6},{8,9},{9,8},{10,11... | collective-permute-start | bytes 3145736 | tf_op jit(solution)/shard_map/ppermute | solution.py:63
  98.9 38.1 %all-to-all-start.2 = ((bf16[32,16,896]{2,1,0:T(8,128)(2,1)}), bf16[32,16,896]{2,1,0:T(8,128)(2,1)S(1)}, u32[]{:S(2)}, u32[]{:S(2)}) async-start(bf16[32,16,896]{2,1,0:T(8,128)(2,1)} %placed_grads.1), calls=%async_computation.2 | async-start | bytes 1835008 | tf_op jit(solution)/shard_map/all_to_all | solution.py:491
  107.7 1.2 copy-start.7
  110.4 9.3 %collective-permute-start.23 = (bf16[256,512]{1,0:T(8,128)(2,1)S(1)}, bf16[256,512]{1,0:T(8,128)(2,1)S(1)}, u32[]{:S(2)}, u32[]{:S(2)}) collective-permute-start(bf16[256,512]{1,0:T(8,128)(2,1)S(1)} %get-tuple-element.68), channel_id=1, source_target_pairs={{0,6},{1,7},{2,0},{3,1},{4,2},{5,3},{6,4},{7,5},{8,14},{9,15},{10,... | collective-permute-start | bytes 786440 | tf_op jit(solution)/shard_map/ppermute | solution.py:85
  111.4 10.8 %collective-permute-start.24 = (bf16[256,512]{1,0:T(8,128)(2,1)S(1)}, bf16[256,512]{1,0:T(8,128)(2,1)S(1)}, u32[]{:S(2)}, u32[]{:S(2)}) collective-permute-start(bf16[256,512]{1,0:T(8,128)(2,1)S(1)} %get-tuple-element.69), channel_id=1, source_target_pairs={{0,4},{1,5},{2,6},{3,7},{4,0},{5,1},{6,2},{7,3},{8,12},{9,13},{10,... | collective-permute-start | bytes 786440 | tf_op jit(solution)/shard_map/ppermute | solution.py:85
  111.7 14.7 %collective-permute-start.25 = (bf16[256,512]{1,0:T(8,128)(2,1)S(1)}, bf16[256,512]{1,0:T(8,128)(2,1)S(1)}, u32[]{:S(2)}, u32[]{:S(2)}) collective-permute-start(bf16[256,512]{1,0:T(8,128)(2,1)S(1)} %get-tuple-element.70), channel_id=1, source_target_pairs={{0,2},{1,3},{2,4},{3,5},{4,6},{5,7},{6,0},{7,1},{8,10},{9,11},{10,... | collective-permute-start | bytes 786440 | tf_op jit(solution)/shard_map/ppermute | solution.py:85
  126.4 10.6 %copy-start.2 = (bf16[8,16,896]{2,1,0:T(8,128)(2,1)S(1)}, bf16[8,16,896]{2,1,0:T(8,128)(2,1)}, u32[]{:S(2)}) copy-start(bf16[8,16,896]{2,1,0:T(8,128)(2,1)} %enc.3) | copy-start | bytes 688132
  127.3 11.6 %copy-start.10 = (bf16[256,512]{1,0:T(8,128)(2,1)S(1)}, bf16[256,512]{1,0:T(8,128)(2,1)}, u32[]{:S(2)}) copy-start(bf16[256,512]{1,0:T(8,128)(2,1)} %get-tuple-element.38) | copy-start | bytes 786436
  127.4 1.2 collective-permute-start.26
  128.6 3.6 %collective-permute-start.27 = (f32[256]{0:T(256)S(1)}, f32[256]{0:T(256)S(1)}, u32[]{:S(2)}, u32[]{:S(2)}) collective-permute-start(f32[256]{0:T(256)S(1)} %add.55), channel_id=1, source_target_pairs={{0,2},{1,3},{2,0},{3,1},{4,6},{5,7},{6,4},{7,5},{8,10},{9,11},{10,... | collective-permute-start | bytes 3080 | tf_op jit(solution)/shard_map/ppermute | solution.py:499
  132.2 4.8 %collective-permute-start.28 = (f32[256]{0:T(256)S(1)}, f32[256]{0:T(256)S(1)}, u32[]{:S(2)}, u32[]{:S(2)}) collective-permute-start(f32[256]{0:T(256)S(1)} %add.56), channel_id=1, source_target_pairs={{0,6},{1,7},{2,4},{3,5},{4,2},{5,3},{6,0},{7,1},{8,14},{9,15},{10,... | collective-permute-start | bytes 3080 | tf_op jit(solution)/shard_map/ppermute | solution.py:499

commit v7 on v6

--- a/solution.py
+++ b/solution.py
@@ -306,9 +306,14 @@
     )(encodings, gain.reshape(1, 1, -1))
 
 
-def outgoing_kernel(req, normed, out):
+def outgoing_kernel(req, normed, out, sems):
+    copies = []
     for s in range(out.shape[0]):
-        out[s] = normed[jnp.maximum(req[s, 0], 0)]
+        cp = pltpu.make_async_copy(normed.at[jnp.maximum(req[s, 0], 0)], out.at[s], sems.at[s])
+        cp.start()
+        copies.append(cp)
+    for cp in copies:
+        cp.wait()
 
 
 def run_outgoing(requested, normed):
@@ -317,7 +322,8 @@
         outgoing_kernel,
         out_shape=jax.ShapeDtypeStruct((slots,) + normed.shape[1:], BF16),
         in_specs=[smem(), vmem()],
-        out_specs=vmem(),
+        out_specs=pl.BlockSpec(memory_space=pl.ANY),
+        scratch_shapes=[pltpu.SemaphoreType.DMA((slots,))],
         compiler_params=params(8),
         cost_estimate=cost(0.1),
         name="outgoing_rows",
@@ -349,10 +355,15 @@
 
 
 def place_kernel(reading, *refs):
-    parts, out, total = refs[:-2], refs[-2], refs[-1]
+    parts, out, total, sems = refs[:-3], refs[-3], refs[-2], refs[-1]
     total[...] = sum(p[...].astype(F32) for p in parts).astype(BF16)
+    copies = []
     for s in range(out.shape[0]):
-        out[s] = total[reading[s]]
+        cp = pltpu.make_async_copy(total.at[reading[s]], out.at[s], sems.at[s])
+        cp.start()
+        copies.append(cp)
+    for cp in copies:
+        cp.wait()
 
 
 def run_place(reading, parts):
@@ -362,8 +373,8 @@
         place_kernel,
         out_shape=jax.ShapeDtypeStruct((slots,) + shape[1:], BF16),
         in_specs=[smem()] + [vmem()] * len(parts),
-        out_specs=vmem(),
-        scratch_shapes=[pltpu.VMEM(shape, BF16)],
+        out_specs=pl.BlockSpec(memory_space=pl.ANY),
+        scratch_shapes=[pltpu.VMEM(shape, BF16), pltpu.SemaphoreType.DMA((slots,))],
         compiler_params=params(12),
         cost_estimate=cost(1.7),
         name="placed_grads",

time: 140 us -> 141 us (level)
  no operation moved by 1% of the time
where the time goes in v7:
time: 141 us; the launch traced here: 140 us
  starting transfers between devices  50.4 us (36%)
  waiting for transfers between devices  49.6 us (35%)
  Pallas kernels  28.9 us (20%)
  local copies, waits for them, and re-layouts  7.03 us (5%)
  other arithmetic  3.32 us (2%)
    ppermute x6, waiting for transfers between devices, pair_shares(): lax.ppermute(pair[k], 'mp', chip_shift(count, -k))  21.4 us
    ppermute x9, starting transfers between devices, over_chips(): lax.ppermute(x, 'mp', chip_shift(count, k))  12.7 us
    all_to_all x1, starting transfers between devices, shards(): lax.all_to_all(jnp.broadcast_to(wanted[:, None], (dp_count, IDS_WIDTH)),...  11.7 us
    ppermute x9, waiting for transfers between devices, over_chips(): lax.ppermute(x, 'mp', chip_shift(count, k))  11.2 us
    all_to_all x1, starting transfers between devices, shards(): lax.all_to_all(outgoing, 'dp', split_axis=0, concat_axis=0, tiled=True)  8.86 us
    all_to_all x1, starting transfers between devices, shards(): lax.all_to_all(back_out, 'dp', split_axis=0, concat_axis=0, tiled=True)  8.84 us
    ppermute x2, waiting for transfers between devices, shards(): total = total + lax.ppermute(total, 'mp', chip_flip(count, flip))  7.51 us
    pallas_call x1, Pallas kernels, run_attention(): pl.pallas_call(lambda *r: attention_kernel(count, blocks, *r), out_shape=...  6.98 us
  transfers between devices with their start and end apart: 32, of which 18 were waited for; matrix products, arithmetic and copies ran while one was open for 3% of the time, Pallas kernels for 14%

profile of v7, /device:TPU:8, one launch (start us, length us, event | category | flops | bytes accessed | tf_op | source)
XLA Modules:
  0.0 140.2 jit_solution(8591896348015335282)
XLA Ops:
  0.6 0.8 copy.17
  1.6 0.7 broadcast_in_dim.46
  2.4 11.7 %all-to-all-start = ((s32[32,1,128]{2,1,0:T(1,128)}), s32[32,1,128]{2,1,0:T(1,128)S(1)}, u32[]{:S(2)}, u32[]{:S(2)}) async-start(s32[32,1,128]{2,1,0:T(1,128)} %broadcast_in_dim.46), calls=%async_computation | async-start | bytes 32768 | tf_op jit(solution)/shard_map/all_to_all | solution.py:471
  14.1 1.6 %collective-permute-start.6 = (bf16[256,512]{1,0:T(8,128)(2,1)}, bf16[256,512]{1,0:T(8,128)(2,1)S(1)}, u32[]{:S(2)}, u32[]{:S(2)}) collective-permute-start(bf16[256,512]{1,0:T(8,128)(2,1)} %tok.1), channel_id=1, source_target_pairs={{0,2},{1,3},{2,4},{3,5},{4,6},{5,7},{6,0},{7,1},{8,10},{9,11},{10,... | collective-permute-start | bytes 786440 | tf_op jit(solution)/shard_map/ppermute | solution.py:59
  15.6 2.7 %collective-permute-start.7 = (bf16[256,512]{1,0:T(8,128)(2,1)}, bf16[256,512]{1,0:T(8,128)(2,1)S(1)}, u32[]{:S(2)}, u32[]{:S(2)}) collective-permute-start(bf16[256,512]{1,0:T(8,128)(2,1)} %tok.1), channel_id=1, source_target_pairs={{0,4},{1,5},{2,6},{3,7},{4,0},{5,1},{6,2},{7,3},{8,12},{9,13},{10,... | collective-permute-start | bytes 786440 | tf_op jit(solution)/shard_map/ppermute | solution.py:59
  18.4 1.4 %collective-permute-start.8 = (bf16[256,512]{1,0:T(8,128)(2,1)}, bf16[256,512]{1,0:T(8,128)(2,1)S(1)}, u32[]{:S(2)}, u32[]{:S(2)}) collective-permute-start(bf16[256,512]{1,0:T(8,128)(2,1)} %tok.1), channel_id=1, source_target_pairs={{0,6},{1,7},{2,0},{3,1},{4,2},{5,3},{6,4},{7,5},{8,14},{9,15},{10,... | collective-permute-start | bytes 786440 | tf_op jit(solution)/shard_map/ppermute | solution.py:59
  19.8 0.7 reshape.94.gain
  20.5 0.9 copy-done.1
  21.4 0.1 normed_rows.1.normed
  21.6 0.9 all-to-all-done
  22.5 2.0 %outgoing_rows.1 = bf16[32,16,896]{2,1,0:T(8,128)(2,1)} custom-call(s32[32,128]{1,0:T(8,128)S(1)} %bitcast.14, bf16[8,16,896]{2,1,0:T(8,128)(2,1)S(1)} %normed_rows.1.normed), custom_call_target="tpu_custom_call" | custom-call | flops 110000000 | tf_op jit(solution)/shard_map/outgoing_rows/pallas_call | solution.py:321
  24.5 8.9 %all-to-all-start.1 = ((bf16[32,16,896]{2,1,0:T(8,128)(2,1)}), bf16[32,16,896]{2,1,0:T(8,128)(2,1)S(1)}, u32[]{:S(2)}, u32[]{:S(2)}) async-start(bf16[32,16,896]{2,1,0:T(8,128)(2,1)} %outgoing_rows.1), calls=%async_computation.1 | async-start | bytes 1835008 | tf_op jit(solution)/shard_map/all_to_all | solution.py:484
  33.4 2.1 %pad_maximum_fusion = bf16[4,256,512]{2,1,0:T(8,128)(2,1)} fusion(bf16[1,256,512]{2,1,0:T(8,128)(2,1)S(1)} %bitcast.13, bf16[1,256,512]{2,1,0:T(8,128)(2,1)S(1)} %bitcast.12, bf16[1,256,512]{2,1,0:T(8,128)(2,1)S(1)} %bitcast.11, bf16[1,256,512]{2,1,0:T(8,128)(2,1)} %bitcast.10), kind=kLoop, calls=%fused_computation | loop fusion | flops 1572864 | bytes 2097152 | tf_op jit(solution)/shard_map/stack | solution.py:486
  35.6 0.6 collective-permute-start.3
  36.2 0.9 collective-permute-start.4
  37.1 1.9 %collective-permute-start.5 = (bf16[256,512]{1,0:T(8,128)(2,1)S(1)}, bf16[256,512]{1,0:T(8,128)(2,1)}, u32[]{:S(2)}, u32[]{:S(2)}) collective-permute-start(bf16[256,512]{1,0:T(8,128)(2,1)S(1)} %copy-done.5), channel_id=1, source_target_pairs={{0,6},{1,7},{2,0},{3,1},{4,2},{5,3},{6,4},{7,5},{8,14},{9,15},{10,... | collective-permute-start | bytes 786440 | tf_op jit(solution)/shard_map/ppermute | solution.py:59
  39.0 3.9 %queries.1.r_8_ = bf16[256,512]{1,0:T(8,128)(2,1)S(1)} custom-call(s32[8]{0:T(128)S(1)} %pad_add_fusion.r_0_, bf16[256,512]{1,0:T(8,128)(2,1)S(1)} %copy-done, bf16[256,512]{1,0:T(8,128)(2,1)S(1)} %collective-permute-done.6.r_2_, bf16[256,512]{1,0:T(8,128)(2,1)S(1)} %collective-permute-done.7.r_3_, bf16[256,512]{1,0:T(8,128)(2,1)S(1)} %collective-permute-done.8.r_4_, ...), custom_call_target="tpu_custom_call" | custom-call | flops 3740000000 | tf_op jit(solution)/shard_map/queries/pallas_call | solution.py:141
  43.0 0.7 copy-done.8
  43.7 7.6 %collective-permute-done.3.r_2_ = bf16[256,512]{1,0:T(8,128)(2,1)} collective-permute-done((bf16[256,512]{1,0:T(8,128)(2,1)S(1)}, bf16[256,512]{1,0:T(8,128)(2,1)}, u32[]{:S(2)}, u32[]{:S(2)}) %collective-permute-start.3) | collective-permute-done | bytes 262176 | tf_op jit(solution)/shard_map/ppermute | solution.py:59
  51.3 0.6 collective-permute-done.5.r_4_
  51.9 0.5 collective-permute-start.11
  52.4 0.5 collective-permute-start.13
  52.9 4.3 %all-to-all-done.1.rows = bf16[32,16,896]{2,1,0:T(8,128)(2,1)S(1)} async-done(((bf16[32,16,896]{2,1,0:T(8,128)(2,1)}), bf16[32,16,896]{2,1,0:T(8,128)(2,1)S(1)}, u32[]{:S(2)}, u32[]{:S(2)}) %all-to-all-start.1) | async-done | bytes 917536 | tf_op jit(solution)/shard_map/all_to_all | solution.py:484
  57.3 1.0 picked_rows.1
  58.3 0.7 collective-permute-start
  58.9 1.2 collective-permute-start.1
  60.1 1.8 %collective-permute-start.2 = (bf16[128,896]{1,0:T(8,128)(2,1)S(1)}, bf16[128,896]{1,0:T(8,128)(2,1)S(1)}, u32[]{:S(2)}, u32[]{:S(2)}) collective-permute-start(bf16[128,896]{1,0:T(8,128)(2,1)S(1)} %bitcast.18), channel_id=1, source_target_pairs={{0,6},{1,7},{2,0},{3,1},{4,2},{5,3},{6,4},{7,5},{8,14},{9,15},{10,... | collective-permute-start | bytes 688136 | tf_op jit(solution)/shard_map/ppermute | solution.py:59
  61.9 4.4 %d_attended.1.r_9_ = bf16[256,512]{1,0:T(8,128)(2,1)S(1)} custom-call(s32[8]{0:T(128)S(1)} %pad_add_fusion.r_0_, bf16[256,512]{1,0:T(8,128)(2,1)S(1)} %copy-done.5, bf16[256,512]{1,0:T(8,128)(2,1)} %collective-permute-done.3.r_2_, bf16[256,512]{1,0:T(8,128)(2,1)} %collective-permute-done.4.r_3_, bf16[256,512]{1,0:T(8,128)(2,1)} %collective-permute-done.5.r_4_, ...), custom_call_target="tpu_custom_call" | custom-call | flops 3740000000 | tf_op jit(solution)/shard_map/d_attended/pallas_call | solution.py:174
  66.3 2.7 %collective-permute-done.r_1_ = bf16[128,896]{1,0:T(8,128)(2,1)S(1)} collective-permute-done((bf16[128,896]{1,0:T(8,128)(2,1)S(1)}, bf16[128,896]{1,0:T(8,128)(2,1)S(1)}, u32[]{:S(2)}, u32[]{:S(2)}) %collective-permute-start) | collective-permute-done | bytes 229408 | tf_op jit(solution)/shard_map/ppermute | solution.py:59
  69.1 0.2 collective-permute-done.2.r_3_
  69.3 0.5 collective-permute-start.16
  69.8 1.0 collective-permute-done.15.r_5_
  70.8 0.3 collective-permute-done.16.r_6_
  71.1 0.3 collective-permute-done.17.r_7_
  71.4 7.0 %attention.1 = (bf16[4,128,896]{2,1,0:T(8,128)(2,1)S(1)}, bf16[4,128,896]{2,1,0:T(8,128)(2,1)S(1)}, bf16[256,512]{1,0:T(8,128)(2,1)S(1)}) custom-call(bf16[128,896]{1,0:T(8,128)(2,1)S(1)} %bitcast.20, bf16[128,896]{1,0:T(8,128)(2,1)S(1)} %collective-permute-done.r_1_, bf16[128,896]{1,0:T(8,128)(2,1)S(1)} %collective-permute-done.1.r_2_, ...), custom_call_target="tpu_custom_call" | custom-call | flops 9900000256 | tf_op jit(solution)/shard_map/attention/pallas_call | solution.py:279
  78.4 0.3 collective-permute-start.18
  78.7 2.3 %collective-permute-done.18.other = bf16[4,128,896]{2,1,0:T(8,128)(2,1)S(1)} collective-permute-done((bf16[4,128,896]{2,1,0:T(8,128)(2,1)S(1)}, bf16[4,128,896]{2,1,0:T(8,128)(2,1)S(1)}, u32[]{:S(2)}, u32[]{:S(2)}) %collective-permute-start.18) | collective-permute-done | bytes 917536 | tf_op jit(solution)/shard_map/ppermute | solution.py:63
  81.0 0.2 pair_sums.2
  81.2 2.6 %collective-permute-start.19 = (bf16[128,896]{1,0:T(8,128)(2,1)S(1)}, bf16[128,896]{1,0:T(8,128)(2,1)S(1)}, u32[]{:S(2)}, u32[]{:S(2)}) collective-permute-start(bf16[128,896]{1,0:T(8,128)(2,1)S(1)} %get-tuple-element.63), channel_id=1, source_target_pairs={{0,6},{1,7},{2,0},{3,1},{4,2},{5,3},{6,4},{7,5},{8,14},{9,15},{10,... | collective-permute-start | bytes 688136 | tf_op jit(solution)/shard_map/ppermute | solution.py:85
  83.8 1.0 collective-permute-start.21
  84.8 4.1 %branches.1 = (bf16[4,256,512]{2,1,0:T(8,128)(2,1)S(1)}, bf16[4,256,512]{2,1,0:T(8,128)(2,1)S(1)}) custom-call(s32[8]{0:T(128)S(1)} %pad_add_fusion.r_0_, bf16[256,512]{1,0:T(8,128)(2,1)S(1)} %get-tuple-element.59.r_1_, bf16[512,4096]{1,0:T(8,128)(2,1)} %r_2_.1), custom_call_target="tpu_custom_call" | custom-call | flops 4400000000 | tf_op jit(solution)/shard_map/branches/pallas_call | solution.py:207
  88.9 1.0 copy-done.6
  89.9 4.1 %collective-permute-done.19 = bf16[128,896]{1,0:T(8,128)(2,1)S(1)} collective-permute-done((bf16[128,896]{1,0:T(8,128)(2,1)S(1)}, bf16[128,896]{1,0:T(8,128)(2,1)S(1)}, u32[]{:S(2)}, u32[]{:S(2)}) %collective-permute-start.19) | collective-permute-done | bytes 229408 | tf_op jit(solution)/shard_map/ppermute | solution.py:85
  94.0 3.4 %collective-permute-done.21 = bf16[128,896]{1,0:T(8,128)(2,1)S(1)} collective-permute-done((bf16[128,896]{1,0:T(8,128)(2,1)S(1)}, bf16[128,896]{1,0:T(8,128)(2,1)S(1)}, u32[]{:S(2)}, u32[]{:S(2)}) %collective-permute-start.21) | collective-permute-done | bytes 229408 | tf_op jit(solution)/shard_map/ppermute | solution.py:85
  97.4 1.9 %placed_grads.1 = bf16[32,16,896]{2,1,0:T(8,128)(2,1)} custom-call(s32[32]{0:T(128)S(1)} %get-tuple-element.79.reading, bf16[8,16,896]{2,1,0:T(8,128)(2,1)S(1)} %bitcast.24, bf16[8,16,896]{2,1,0:T(8,128)(2,1)S(1)} %bitcast.21, bf16[8,16,896]{2,1,0:T(8,128)(2,1)S(1)} %bitcast.22, bf16[8,16,896]{2,1,0:T(8,128)(2,1)S(1)} %bitcast.23), custom_call_target="tpu_custom_call" | custom-call | flops 1870000000 | tf_op jit(solution)/shard_map/placed_grads/pallas_call | solution.py:372
  99.3 8.8 %all-to-all-start.2 = ((bf16[32,16,896]{2,1,0:T(8,128)(2,1)}), bf16[32,16,896]{2,1,0:T(8,128)(2,1)S(1)}, u32[]{:S(2)}, u32[]{:S(2)}) async-start(bf16[32,16,896]{2,1,0:T(8,128)(2,1)} %placed_grads.1), calls=%async_computation.2 | async-start | bytes 1835008 | tf_op jit(solution)/shard_map/all_to_all | solution.py:502
  108.1 1.2 copy-done.7
  109.4 1.5 %pair_sums.3 = (bf16[256,512]{1,0:T(8,128)(2,1)S(1)}, bf16[256,512]{1,0:T(8,128)(2,1)S(1)}, bf16[256,512]{1,0:T(8,128)(2,1)S(1)}, bf16[256,512]{1,0:T(8,128)(2,1)S(1)}) custom-call(bf16[4,256,512]{2,1,0:T(8,128)(2,1)S(1)} %copy-done.7, bf16[4,256,512]{2,1,0:T(8,128)(2,1)} %collective-permute-done.22.other), custom_call_target="tpu_custom_call" | custom-call | flops 770000000 | tf_op jit(solution)/shard_map/pair_sums/pallas_call | solution.py:72
  110.8 1.0 collective-permute-start.23
  111.8 0.3 collective-permute-start.24
  112.1 0.8 collective-permute-start.25
  112.9 7.1 %collective-permute-done.23.refs_1_ = bf16[256,512]{1,0:T(8,128)(2,1)S(1)} collective-permute-done((bf16[256,512]{1,0:T(8,128)(2,1)S(1)}, bf16[256,512]{1,0:T(8,128)(2,1)S(1)}, u32[]{:S(2)}, u32[]{:S(2)}) %collective-permute-start.23) | collective-permute-done | bytes 262176 | tf_op jit(solution)/shard_map/ppermute | solution.py:85
  120.1 2.5 %collective-permute-done.24.refs_2_ = bf16[256,512]{1,0:T(8,128)(2,1)S(1)} collective-permute-done((bf16[256,512]{1,0:T(8,128)(2,1)S(1)}, bf16[256,512]{1,0:T(8,128)(2,1)S(1)}, u32[]{:S(2)}, u32[]{:S(2)}) %collective-permute-start.24) | collective-permute-done | bytes 262176 | tf_op jit(solution)/shard_map/ppermute | solution.py:85
  122.6 4.2 %collective-permute-done.25.refs_3_ = bf16[256,512]{1,0:T(8,128)(2,1)S(1)} collective-permute-done((bf16[256,512]{1,0:T(8,128)(2,1)S(1)}, bf16[256,512]{1,0:T(8,128)(2,1)S(1)}, u32[]{:S(2)}, u32[]{:S(2)}) %collective-permute-start.25) | collective-permute-done | bytes 262176 | tf_op jit(solution)/shard_map/ppermute | solution.py:85
  126.8 0.9 mixed.1
  127.9 0.8 dynamic_slice.3
  128.7 0.4 collective-permute-done.26
  129.0 0.1 slice_reduce_fusion
  129.1 3.5 %collective-permute-done.27 = f32[256]{0:T(256)S(1)} collective-permute-done((f32[256]{0:T(256)S(1)}, f32[256]{0:T(256)S(1)}, u32[]{:S(2)}, u32[]{:S(2)}) %collective-permute-start.27) | collective-permute-done | bytes 1056 | tf_op jit(solution)/shard_map/ppermute | solution.py:510
  132.6 0.6 collective-permute-start.28
  133.2 0.1 select_reduce_fusion.1.slot
  133.3 4.1 %collective-permute-done.28 = f32[256]{0:T(256)S(1)} collective-permute-done((f32[256]{0:T(256)S(1)}, f32[256]{0:T(256)S(1)}, u32[]{:S(2)}, u32[]{:S(2)}) %collective-permute-start.28) | collective-permute-done | bytes 1056 | tf_op jit(solution)/shard_map/ppermute | solution.py:510
  137.4 1.9 %d_encodings.1 = bf16[8,16,896]{2,1,0:T(8,128)(2,1)} custom-call(s32[8]{0:T(128)S(1)} %select_reduce_fusion.1.slot, bf16[32,16,896]{2,1,0:T(8,128)(2,1)S(1)} %all-to-all-done.2.back, bf16[8,16,896]{2,1,0:T(8,128)(2,1)S(1)} %copy-done.2, f32[1,1,896]{2,1,0:T(1,128)S(1)} %reshape.94.gain), custom_call_target="tpu_custom_call" | custom-call | flops 2090000000 | tf_op jit(solution)/shard_map/d_encodings/pallas_call | solution.py:425
  139.3 0.8 multiply_convert_fusion
  (56 shorter events, 0.7 us)
Async XLA Ops:
  0.6 38.4 %copy-start = (bf16[256,512]{1,0:T(8,128)(2,1)S(1)}, bf16[256,512]{1,0:T(8,128)(2,1)}, u32[]{:S(2)}) copy-start(bf16[256,512]{1,0:T(8,128)(2,1)} %tok.1) | copy-start | bytes 786436
  2.4 20.2 %all-to-all-start = ((s32[32,1,128]{2,1,0:T(1,128)}), s32[32,1,128]{2,1,0:T(1,128)S(1)}, u32[]{:S(2)}, u32[]{:S(2)}) async-start(s32[32,1,128]{2,1,0:T(1,128)} %broadcast_in_dim.46), calls=%async_computation | async-start | bytes 32768 | tf_op jit(solution)/shard_map/all_to_all | solution.py:471
  14.1 19.4 %collective-permute-start.6 = (bf16[256,512]{1,0:T(8,128)(2,1)}, bf16[256,512]{1,0:T(8,128)(2,1)S(1)}, u32[]{:S(2)}, u32[]{:S(2)}) collective-permute-start(bf16[256,512]{1,0:T(8,128)(2,1)} %tok.1), channel_id=1, source_target_pairs={{0,2},{1,3},{2,4},{3,5},{4,6},{5,7},{6,0},{7,1},{8,10},{9,11},{10,... | collective-permute-start | bytes 786440 | tf_op jit(solution)/shard_map/ppermute | solution.py:59
  15.6 17.8 %collective-permute-start.7 = (bf16[256,512]{1,0:T(8,128)(2,1)}, bf16[256,512]{1,0:T(8,128)(2,1)S(1)}, u32[]{:S(2)}, u32[]{:S(2)}) collective-permute-start(bf16[256,512]{1,0:T(8,128)(2,1)} %tok.1), channel_id=1, source_target_pairs={{0,4},{1,5},{2,6},{3,7},{4,0},{5,1},{6,2},{7,3},{8,12},{9,13},{10,... | collective-permute-start | bytes 786440 | tf_op jit(solution)/shard_map/ppermute | solution.py:59
  18.4 15.1 %collective-permute-start.8 = (bf16[256,512]{1,0:T(8,128)(2,1)}, bf16[256,512]{1,0:T(8,128)(2,1)S(1)}, u32[]{:S(2)}, u32[]{:S(2)}) collective-permute-start(bf16[256,512]{1,0:T(8,128)(2,1)} %tok.1), channel_id=1, source_target_pairs={{0,6},{1,7},{2,0},{3,1},{4,2},{5,3},{6,4},{7,5},{8,14},{9,15},{10,... | collective-permute-start | bytes 786440 | tf_op jit(solution)/shard_map/ppermute | solution.py:59
  20.5 0.9 copy-start.1
  21.4 14.1 %copy-start.11 = (f32[4096]{0:T(1024)S(1)}, f32[4096]{0:T(1024)}, u32[]{:S(2)}) copy-start(f32[4096]{0:T(1024)} %param.13) | copy-start | bytes 49156
  21.4 14.2 %copy-start.5 = (bf16[256,512]{1,0:T(8,128)(2,1)S(1)}, bf16[256,512]{1,0:T(8,128)(2,1)}, u32[]{:S(2)}) copy-start(bf16[256,512]{1,0:T(8,128)(2,1)} %r_1_.2) | copy-start | bytes 786436
  24.5 32.7 %all-to-all-start.1 = ((bf16[32,16,896]{2,1,0:T(8,128)(2,1)}), bf16[32,16,896]{2,1,0:T(8,128)(2,1)S(1)}, u32[]{:S(2)}, u32[]{:S(2)}) async-start(bf16[32,16,896]{2,1,0:T(8,128)(2,1)} %outgoing_rows.1), calls=%async_computation.1 | async-start | bytes 1835008 | tf_op jit(solution)/shard_map/all_to_all | solution.py:484
  35.5 3.5 %collective-permute-start.9 = (bf16[4,256,512]{2,1,0:T(8,128)(2,1)}, bf16[4,256,512]{2,1,0:T(8,128)(2,1)S(1)}, u32[]{:S(2)}, u32[]{:S(2)}) collective-permute-start(bf16[4,256,512]{2,1,0:T(8,128)(2,1)} %pad_maximum_fusion), channel_id=1, source_target_pairs={{0,1},{1,0},{2,3},{3,2},{4,5},{5,4},{6,7},{7,6},{8,9},{9,8},{10,11... | collective-permute-start | bytes 3145736 | tf_op jit(solution)/shard_map/ppermute | solution.py:63
  35.6 15.7 %collective-permute-start.3 = (bf16[256,512]{1,0:T(8,128)(2,1)S(1)}, bf16[256,512]{1,0:T(8,128)(2,1)}, u32[]{:S(2)}, u32[]{:S(2)}) collective-permute-start(bf16[256,512]{1,0:T(8,128)(2,1)S(1)} %copy-done.5), channel_id=1, source_target_pairs={{0,2},{1,3},{2,4},{3,5},{4,6},{5,7},{6,0},{7,1},{8,10},{9,11},{10,... | collective-permute-start | bytes 786440 | tf_op jit(solution)/shard_map/ppermute | solution.py:59
  36.2 15.1 %collective-permute-start.4 = (bf16[256,512]{1,0:T(8,128)(2,1)S(1)}, bf16[256,512]{1,0:T(8,128)(2,1)}, u32[]{:S(2)}, u32[]{:S(2)}) collective-permute-start(bf16[256,512]{1,0:T(8,128)(2,1)S(1)} %copy-done.5), channel_id=1, source_target_pairs={{0,4},{1,5},{2,6},{3,7},{4,0},{5,1},{6,2},{7,3},{8,12},{9,13},{10,... | collective-permute-start | bytes 786440 | tf_op jit(solution)/shard_map/ppermute | solution.py:59
  37.1 14.8 %collective-permute-start.5 = (bf16[256,512]{1,0:T(8,128)(2,1)S(1)}, bf16[256,512]{1,0:T(8,128)(2,1)}, u32[]{:S(2)}, u32[]{:S(2)}) collective-permute-start(bf16[256,512]{1,0:T(8,128)(2,1)S(1)} %copy-done.5), channel_id=1, source_target_pairs={{0,6},{1,7},{2,0},{3,1},{4,2},{5,3},{6,4},{7,5},{8,14},{9,15},{10,... | collective-permute-start | bytes 786440 | tf_op jit(solution)/shard_map/ppermute | solution.py:59
  43.0 0.7 copy-start.8
  51.9 7.0 %collective-permute-start.10 = (bf16[256,512]{1,0:T(8,128)(2,1)S(1)}, bf16[256,512]{1,0:T(8,128)(2,1)S(1)}, u32[]{:S(2)}, u32[]{:S(2)}) collective-permute-start(bf16[256,512]{1,0:T(8,128)(2,1)S(1)} %copy-done.5), channel_id=1, source_target_pairs={{0,1},{1,0},{2,3},{3,2},{4,5},{5,4},{6,7},{7,6},{8,9},{9,8},{10,11... | collective-permute-start | bytes 786440 | tf_op jit(solution)/shard_map/ppermute | solution.py:63
  51.9 8.2 %collective-permute-start.11 = (bf16[256,512]{1,0:T(8,128)(2,1)}, bf16[256,512]{1,0:T(8,128)(2,1)S(1)}, u32[]{:S(2)}, u32[]{:S(2)}) collective-permute-start(bf16[256,512]{1,0:T(8,128)(2,1)} %collective-permute-done.3.r_2_), channel_id=1, source_target_pairs={{0,1},{1,0},{2,3},{3,2},{4,5},{5,4},{6,7},{7,6},{8,9},{9,8},{10,11... | collective-permute-start | bytes 786440 | tf_op jit(solution)/shard_map/ppermute | solution.py:63
  52.4 9.4 %collective-permute-start.12 = (bf16[256,512]{1,0:T(8,128)(2,1)}, bf16[256,512]{1,0:T(8,128)(2,1)S(1)}, u32[]{:S(2)}, u32[]{:S(2)}) collective-permute-start(bf16[256,512]{1,0:T(8,128)(2,1)} %collective-permute-done.4.r_3_), channel_id=1, source_target_pairs={{0,1},{1,0},{2,3},{3,2},{4,5},{5,4},{6,7},{7,6},{8,9},{9,8},{10,11... | collective-permute-start | bytes 786440 | tf_op jit(solution)/shard_map/ppermute | solution.py:63
  52.4 9.4 %collective-permute-start.13 = (bf16[256,512]{1,0:T(8,128)(2,1)}, bf16[256,512]{1,0:T(8,128)(2,1)S(1)}, u32[]{:S(2)}, u32[]{:S(2)}) collective-permute-start(bf16[256,512]{1,0:T(8,128)(2,1)} %collective-permute-done.5.r_4_), channel_id=1, source_target_pairs={{0,1},{1,0},{2,3},{3,2},{4,5},{5,4},{6,7},{7,6},{8,9},{9,8},{10,11... | collective-permute-start | bytes 786440 | tf_op jit(solution)/shard_map/ppermute | solution.py:63
  58.2 13.2 %copy-start.3 = (bf16[896,512]{1,0:T(8,128)(2,1)S(1)}, bf16[896,512]{1,0:T(8,128)(2,1)}, u32[]{:S(2)}) copy-start(bf16[896,512]{1,0:T(8,128)(2,1)} %r_10_.1) | copy-start | bytes 2752516
  58.2 13.2 %copy-start.4 = (bf16[896,512]{1,0:T(8,128)(2,1)S(1)}, bf16[896,512]{1,0:T(8,128)(2,1)}, u32[]{:S(2)}) copy-start(bf16[896,512]{1,0:T(8,128)(2,1)} %r_11_.1) | copy-start | bytes 2752516
  58.3 13.2 %copy-start.9 = (bf16[256,512]{1,0:T(8,128)(2,1)S(1)}, bf16[256,512]{1,0:T(8,128)(2,1)}, u32[]{:S(2)}) copy-start(bf16[256,512]{1,0:T(8,128)(2,1)} %copy-done.8) | copy-start | bytes 786436
  58.3 10.8 %collective-permute-start = (bf16[128,896]{1,0:T(8,128)(2,1)S(1)}, bf16[128,896]{1,0:T(8,128)(2,1)S(1)}, u32[]{:S(2)}, u32[]{:S(2)}) collective-permute-start(bf16[128,896]{1,0:T(8,128)(2,1)S(1)} %bitcast.16), channel_id=1, source_target_pairs={{0,2},{1,3},{2,4},{3,5},{4,6},{5,7},{6,0},{7,1},{8,10},{9,11},{10,... | collective-permute-start | bytes 688136 | tf_op jit(solution)/shard_map/ppermute | solution.py:59
  58.9 10.1 %collective-permute-start.1 = (bf16[128,896]{1,0:T(8,128)(2,1)S(1)}, bf16[128,896]{1,0:T(8,128)(2,1)S(1)}, u32[]{:S(2)}, u32[]{:S(2)}) collective-permute-start(bf16[128,896]{1,0:T(8,128)(2,1)S(1)} %bitcast.17), channel_id=1, source_target_pairs={{0,4},{1,5},{2,6},{3,7},{4,0},{5,1},{6,2},{7,3},{8,12},{9,13},{10,... | collective-permute-start | bytes 688136 | tf_op jit(solution)/shard_map/ppermute | solution.py:59
  60.1 9.2 %collective-permute-start.2 = (bf16[128,896]{1,0:T(8,128)(2,1)S(1)}, bf16[128,896]{1,0:T(8,128)(2,1)S(1)}, u32[]{:S(2)}, u32[]{:S(2)}) collective-permute-start(bf16[128,896]{1,0:T(8,128)(2,1)S(1)} %bitcast.18), channel_id=1, source_target_pairs={{0,6},{1,7},{2,0},{3,1},{4,2},{5,3},{6,4},{7,5},{8,14},{9,15},{10,... | collective-permute-start | bytes 688136 | tf_op jit(solution)/shard_map/ppermute | solution.py:59
  66.2 3.6 %collective-permute-start.14 = (bf16[128,896]{1,0:T(8,128)(2,1)S(1)}, bf16[128,896]{1,0:T(8,128)(2,1)S(1)}, u32[]{:S(2)}, u32[]{:S(2)}) collective-permute-start(bf16[128,896]{1,0:T(8,128)(2,1)S(1)} %bitcast.19), channel_id=1, source_target_pairs={{0,1},{1,0},{2,3},{3,2},{4,5},{5,4},{6,7},{7,6},{8,9},{9,8},{10,11... | collective-permute-start | bytes 688136 | tf_op jit(solution)/shard_map/ppermute | solution.py:63
  69.3 1.5 %collective-permute-start.15 = (bf16[128,896]{1,0:T(8,128)(2,1)S(1)}, bf16[128,896]{1,0:T(8,128)(2,1)S(1)}, u32[]{:S(2)}, u32[]{:S(2)}) collective-permute-start(bf16[128,896]{1,0:T(8,128)(2,1)S(1)} %collective-permute-done.r_1_), channel_id=1, source_target_pairs={{0,1},{1,0},{2,3},{3,2},{4,5},{5,4},{6,7},{7,6},{8,9},{9,8},{10,11... | collective-permute-start | bytes 688136 | tf_op jit(solution)/shard_map/ppermute | solution.py:63
  69.3 1.8 %collective-permute-start.16 = (bf16[128,896]{1,0:T(8,128)(2,1)S(1)}, bf16[128,896]{1,0:T(8,128)(2,1)S(1)}, u32[]{:S(2)}, u32[]{:S(2)}) collective-permute-start(bf16[128,896]{1,0:T(8,128)(2,1)S(1)} %collective-permute-done.1.r_2_), channel_id=1, source_target_pairs={{0,1},{1,0},{2,3},{3,2},{4,5},{5,4},{6,7},{7,6},{8,9},{9,8},{10,11... | collective-permute-start | bytes 688136 | tf_op jit(solution)/shard_map/ppermute | solution.py:63
  69.8 1.6 %collective-permute-start.17 = (bf16[128,896]{1,0:T(8,128)(2,1)S(1)}, bf16[128,896]{1,0:T(8,128)(2,1)S(1)}, u32[]{:S(2)}, u32[]{:S(2)}) collective-permute-start(bf16[128,896]{1,0:T(8,128)(2,1)S(1)} %collective-permute-done.2.r_3_), channel_id=1, source_target_pairs={{0,1},{1,0},{2,3},{3,2},{4,5},{5,4},{6,7},{7,6},{8,9},{9,8},{10,11... | collective-permute-start | bytes 688136 | tf_op jit(solution)/shard_map/ppermute | solution.py:63
  78.4 2.6 %collective-permute-start.18 = (bf16[4,128,896]{2,1,0:T(8,128)(2,1)S(1)}, bf16[4,128,896]{2,1,0:T(8,128)(2,1)S(1)}, u32[]{:S(2)}, u32[]{:S(2)}) collective-permute-start(bf16[4,128,896]{2,1,0:T(8,128)(2,1)S(1)} %get-tuple-element.54), channel_id=1, source_target_pairs={{0,1},{1,0},{2,3},{3,2},{4,5},{5,4},{6,7},{7,6},{8,9},{9,8},{10,11... | collective-permute-start | bytes 2752520 | tf_op jit(solution)/shard_map/ppermute | solution.py:63
  81.2 12.8 %collective-permute-start.19 = (bf16[128,896]{1,0:T(8,128)(2,1)S(1)}, bf16[128,896]{1,0:T(8,128)(2,1)S(1)}, u32[]{:S(2)}, u32[]{:S(2)}) collective-permute-start(bf16[128,896]{1,0:T(8,128)(2,1)S(1)} %get-tuple-element.63), channel_id=1, source_target_pairs={{0,6},{1,7},{2,0},{3,1},{4,2},{5,3},{6,4},{7,5},{8,14},{9,15},{10,... | collective-permute-start | bytes 688136 | tf_op jit(solution)/shard_map/ppermute | solution.py:85
  83.8 10.2 %collective-permute-start.20 = (bf16[128,896]{1,0:T(8,128)(2,1)S(1)}, bf16[128,896]{1,0:T(8,128)(2,1)S(1)}, u32[]{:S(2)}, u32[]{:S(2)}) collective-permute-start(bf16[128,896]{1,0:T(8,128)(2,1)S(1)} %get-tuple-element.64), channel_id=1, source_target_pairs={{0,4},{1,5},{2,6},{3,7},{4,0},{5,1},{6,2},{7,3},{8,12},{9,13},{10,... | collective-permute-start | bytes 688136 | tf_op jit(solution)/shard_map/ppermute | solution.py:85
  83.8 13.5 %collective-permute-start.21 = (bf16[128,896]{1,0:T(8,128)(2,1)S(1)}, bf16[128,896]{1,0:T(8,128)(2,1)S(1)}, u32[]{:S(2)}, u32[]{:S(2)}) collective-permute-start(bf16[128,896]{1,0:T(8,128)(2,1)S(1)} %get-tuple-element.65), channel_id=1, source_target_pairs={{0,2},{1,3},{2,4},{3,5},{4,6},{5,7},{6,0},{7,1},{8,10},{9,11},{10,... | collective-permute-start | bytes 688136 | tf_op jit(solution)/shard_map/ppermute | solution.py:85
  88.9 1.0 copy-start.6
  97.4 10.7 %collective-permute-start.22 = (bf16[4,256,512]{2,1,0:T(8,128)(2,1)S(1)}, bf16[4,256,512]{2,1,0:T(8,128)(2,1)}, u32[]{:S(2)}, u32[]{:S(2)}) collective-permute-start(bf16[4,256,512]{2,1,0:T(8,128)(2,1)S(1)} %get-tuple-element.66), channel_id=1, source_target_pairs={{0,1},{1,0},{2,3},{3,2},{4,5},{5,4},{6,7},{7,6},{8,9},{9,8},{10,11... | collective-permute-start | bytes 3145736 | tf_op jit(solution)/shard_map/ppermute | solution.py:63
  99.3 38.1 %all-to-all-start.2 = ((bf16[32,16,896]{2,1,0:T(8,128)(2,1)}), bf16[32,16,896]{2,1,0:T(8,128)(2,1)S(1)}, u32[]{:S(2)}, u32[]{:S(2)}) async-start(bf16[32,16,896]{2,1,0:T(8,128)(2,1)} %placed_grads.1), calls=%async_computation.2 | async-start | bytes 1835008 | tf_op jit(solution)/shard_map/all_to_all | solution.py:502
  108.1 1.2 copy-start.7
  110.8 9.3 %collective-permute-start.23 = (bf16[256,512]{1,0:T(8,128)(2,1)S(1)}, bf16[256,512]{1,0:T(8,128)(2,1)S(1)}, u32[]{:S(2)}, u32[]{:S(2)}) collective-permute-start(bf16[256,512]{1,0:T(8,128)(2,1)S(1)} %get-tuple-element.68), channel_id=1, source_target_pairs={{0,6},{1,7},{2,0},{3,1},{4,2},{5,3},{6,4},{7,5},{8,14},{9,15},{10,... | collective-permute-start | bytes 786440 | tf_op jit(solution)/shard_map/ppermute | solution.py:85
  111.8 10.8 %collective-permute-start.24 = (bf16[256,512]{1,0:T(8,128)(2,1)S(1)}, bf16[256,512]{1,0:T(8,128)(2,1)S(1)}, u32[]{:S(2)}, u32[]{:S(2)}) collective-permute-start(bf16[256,512]{1,0:T(8,128)(2,1)S(1)} %get-tuple-element.69), channel_id=1, source_target_pairs={{0,4},{1,5},{2,6},{3,7},{4,0},{5,1},{6,2},{7,3},{8,12},{9,13},{10,... | collective-permute-start | bytes 786440 | tf_op jit(solution)/shard_map/ppermute | solution.py:85
  112.1 14.7 %collective-permute-start.25 = (bf16[256,512]{1,0:T(8,128)(2,1)S(1)}, bf16[256,512]{1,0:T(8,128)(2,1)S(1)}, u32[]{:S(2)}, u32[]{:S(2)}) collective-permute-start(bf16[256,512]{1,0:T(8,128)(2,1)S(1)} %get-tuple-element.70), channel_id=1, source_target_pairs={{0,2},{1,3},{2,4},{3,5},{4,6},{5,7},{6,0},{7,1},{8,10},{9,11},{10,... | collective-permute-start | bytes 786440 | tf_op jit(solution)/shard_map/ppermute | solution.py:85
  126.8 10.6 %copy-start.2 = (bf16[8,16,896]{2,1,0:T(8,128)(2,1)S(1)}, bf16[8,16,896]{2,1,0:T(8,128)(2,1)}, u32[]{:S(2)}) copy-start(bf16[8,16,896]{2,1,0:T(8,128)(2,1)} %enc.3) | copy-start | bytes 688132
  127.7 11.6 %copy-start.10 = (bf16[256,512]{1,0:T(8,128)(2,1)S(1)}, bf16[256,512]{1,0:T(8,128)(2,1)}, u32[]{:S(2)}) copy-start(bf16[256,512]{1,0:T(8,128)(2,1)} %get-tuple-element.38) | copy-start | bytes 786436
  127.8 1.2 collective-permute-start.26
  129.0 3.6 %collective-permute-start.27 = (f32[256]{0:T(256)S(1)}, f32[256]{0:T(256)S(1)}, u32[]{:S(2)}, u32[]{:S(2)}) collective-permute-start(f32[256]{0:T(256)S(1)} %add.55), channel_id=1, source_target_pairs={{0,2},{1,3},{2,0},{3,1},{4,6},{5,7},{6,4},{7,5},{8,10},{9,11},{10,... | collective-permute-start | bytes 3080 | tf_op jit(solution)/shard_map/ppermute | solution.py:510
  132.6 4.8 %collective-permute-start.28 = (f32[256]{0:T(256)S(1)}, f32[256]{0:T(256)S(1)}, u32[]{:S(2)}, u32[]{:S(2)}) collective-permute-start(f32[256]{0:T(256)S(1)} %add.56), channel_id=1, source_target_pairs={{0,6},{1,7},{2,4},{3,5},{4,2},{5,3},{6,0},{7,1},{8,14},{9,15},{10,... | collective-permute-start | bytes 3080 | tf_op jit(solution)/shard_map/ppermute | solution.py:510
